TPU v7x, 256 devices: a whole 4x4x8 slice. The times are simulated.
256 devices in a mesh: lon: 16 (over y, x_lo, core), lat: 16 (over x_hi, z).
Axes of the slice: x: 4 (x_hi: 2, x_lo: 2; x = x_hi * 2 + x_lo), y: 4, z: 8, core: 2. Of those that a mesh axis runs over, the one named last changes fastest.
Arguments:
- eastbound_current: float32 [32, 512, 4096], P(None, 'lat', 'lon'), may hold values from -3 to 3
- poleward_current: float32 [32, 512, 4096], P(None, 'lat', 'lon'), may hold values from -3 to 3
- warmth_excess: float32 [32, 512, 4096], P(None, 'lat', 'lon'), may hold values from -5 to 5
- saltiness_excess: float32 [32, 512, 4096], P(None, 'lat', 'lon'), may hold values from -5 to 5
- water_indicator: int32 [32, 512, 4096], P(None, 'lat', 'lon'), may hold values 0 or 1
- column_layer_count: int32 [512, 4096], P('lat', 'lon'), may hold values from 1 to 32
Outputs:
- east_next: float32 [32, 512, 4096], P(None, 'lat', 'lon')
- north_next: float32 [32, 512, 4096], P(None, 'lat', 'lon')
- temp_next: float32 [32, 512, 4096], P(None, 'lat', 'lon')
- salt_next: float32 [32, 512, 4096], P(None, 'lat', 'lon')
All inputs are finite; a program needn't handle non-finite values. No bound on the sum of `water_indicator` on one device may be relied on, other than what follows from the above.
Results may differ from a plain program's by a relative error of at most 0.00002.
Values sent between devices are 32-bit elements; how exact they have to be, the bound alone decides.
A program may use at most 128 MiB of HBM per device.

v0:
```python
import jax
import jax.numpy as jnp
from jax import lax
from jax.sharding import PartitionSpec as P

time_step = 0.2
lateral_diff = 0.1
vertical_diff = 0.5
pressure_coef = 0.1
drag_coef = 2.0
coriolis_max = 1.0
level_depth = 100.0
thermal_expand = 0.1655
haline_contract = 0.76554
cabbel_temp = 0.05952
cabbel_salt = 0.00054914
cabbel_mixed = 0.0024341
thermo_temp = 0.0001497
thermo_salt = 1.109e-05


def view_at(field, lat_step, lon_step):
    rows = field.shape[1] - 2
    cols = field.shape[2] - 2
    return field[:, 1 + lat_step : 1 + lat_step + rows, 1 + lon_step : 1 + lon_step + cols]


def column_flux(centre, mixing):
    between = -vertical_diff * mixing * (centre[1:] - centre[:-1])
    surface = jnp.zeros_like(centre[:1])
    above = jnp.concatenate([surface, between], axis=0)
    below = jnp.concatenate([between, surface], axis=0)
    return above - below


def advance(extended, column_layer_count, row_start, total_rows):
    eastward = extended[0]
    northward = extended[1]
    temper = extended[2]
    saline = extended[3]
    wet = extended[4]
    levels = extended.shape[1]
    rows = extended.shape[2] - 2
    level_index = jnp.arange(levels, dtype=jnp.int32)[:, None, None]
    wet_here = view_at(wet, 0, 0)
    mask_east = wet_here * view_at(wet, 0, 1)
    mask_west = view_at(wet, 0, -1) * wet_here
    mask_north = wet_here * view_at(wet, 1, 0)
    mask_south = view_at(wet, -1, 0) * wet_here
    mixing = (
        wet_here[:-1]
        * wet_here[1:]
        * (level_index[1:] < column_layer_count[None]).astype(jnp.float32)
    )
    bottom = (level_index == column_layer_count[None] - 1).astype(jnp.float32)
    depth = (level_index.astype(jnp.float32) + 0.5) * level_depth
    density = (
        -thermal_expand * (1.0 + 0.5 * cabbel_temp * temper + thermo_temp * depth) * temper
        + haline_contract * (1.0 - 0.5 * cabbel_salt * saline - thermo_salt * depth) * saline
        - cabbel_mixed * temper * saline
    )
    pressure = jnp.cumsum(wet * density, axis=0)
    row_index = (row_start + jnp.arange(rows, dtype=jnp.int32)).astype(jnp.float32)[None, :, None]
    coriolis_t = coriolis_max * (2.0 * (row_index + 0.5) / total_rows - 1.0)
    coriolis_v = coriolis_max * (2.0 * (row_index + 1.0) / total_rows - 1.0)

    def tracer(field):
        centre = view_at(field, 0, 0)
        east_side = view_at(field, 0, 1)
        west_side = view_at(field, 0, -1)
        north_side = view_at(field, 1, 0)
        south_side = view_at(field, -1, 0)
        flux_east = mask_east * (
            view_at(eastward, 0, 0) * (centre + east_side) * 0.5
            - lateral_diff * (east_side - centre)
        )
        flux_west = mask_west * (
            view_at(eastward, 0, -1) * (west_side + centre) * 0.5
            - lateral_diff * (centre - west_side)
        )
        flux_north = mask_north * (
            view_at(northward, 0, 0) * (centre + north_side) * 0.5
            - lateral_diff * (north_side - centre)
        )
        flux_south = mask_south * (
            view_at(northward, -1, 0) * (south_side + centre) * 0.5
            - lateral_diff * (centre - south_side)
        )
        tendency = flux_west - flux_east + (flux_south - flux_north) + column_flux(centre, mixing)
        return wet_here * (centre + time_step * tendency)

    east_here = view_at(eastward, 0, 0)
    north_here = view_at(northward, 0, 0)
    corner_ne = wet_here * view_at(wet, 0, 1) * view_at(wet, 1, 0) * view_at(wet, 1, 1)
    corner_se = view_at(wet, -1, 0) * view_at(wet, -1, 1) * wet_here * view_at(wet, 0, 1)
    corner_nw = view_at(wet, 0, -1) * wet_here * view_at(wet, 1, -1) * view_at(wet, 1, 0)
    cell_east = view_at(wet, 0, 1) * (
        ((east_here + view_at(eastward, 0, 1)) * 0.5) ** 2
        - lateral_diff * (view_at(eastward, 0, 1) - east_here)
    )
    cell_west = wet_here * (
        ((view_at(eastward, 0, -1) + east_here) * 0.5) ** 2
        - lateral_diff * (east_here - view_at(eastward, 0, -1))
    )
    product_ne = (
        (north_here + view_at(northward, 0, 1)) * 0.5 * (east_here + view_at(eastward, 1, 0)) * 0.5
    )
    product_se = (
        (view_at(northward, -1, 0) + view_at(northward, -1, 1))
        * 0.5
        * (view_at(eastward, -1, 0) + east_here)
        * 0.5
    )
    product_nw = (
        (view_at(eastward, 0, -1) + view_at(eastward, 1, -1))
        * 0.5
        * (view_at(northward, 0, -1) + north_here)
        * 0.5
    )
    shear_north = corner_ne * (product_ne - lateral_diff * (view_at(eastward, 1, 0) - east_here))
    shear_south = corner_se * (product_se - lateral_diff * (east_here - view_at(eastward, -1, 0)))
    north_mean = (
        north_here
        + view_at(northward, 0, 1)
        + view_at(northward, -1, 0)
        + view_at(northward, -1, 1)
    ) * 0.25
    east_tend = (
        cell_west
        - cell_east
        + (shear_south - shear_north)
        + coriolis_t * north_mean
        - pressure_coef * (view_at(pressure, 0, 1) - view_at(pressure, 0, 0))
        + column_flux(east_here, mixing)
        - drag_coef * bottom * east_here
    )
    east_next = mask_east * (east_here + time_step * east_tend)
    cell_north = view_at(wet, 1, 0) * (
        ((north_here + view_at(northward, 1, 0)) * 0.5) ** 2
        - lateral_diff * (view_at(northward, 1, 0) - north_here)
    )
    cell_south = wet_here * (
        ((view_at(northward, -1, 0) + north_here) * 0.5) ** 2
        - lateral_diff * (north_here - view_at(northward, -1, 0))
    )
    stress_east = corner_ne * (product_ne - lateral_diff * (view_at(northward, 0, 1) - north_here))
    stress_west = corner_nw * (product_nw - lateral_diff * (north_here - view_at(northward, 0, -1)))
    east_mean = (
        east_here + view_at(eastward, 0, -1) + view_at(eastward, 1, 0) + view_at(eastward, 1, -1)
    ) * 0.25
    north_tend = (
        stress_west
        - stress_east
        + (cell_south - cell_north)
        - coriolis_v * east_mean
        - pressure_coef * (view_at(pressure, 1, 0) - view_at(pressure, 0, 0))
        + column_flux(north_here, mixing)
        - drag_coef * bottom * north_here
    )
    north_next = mask_north * (north_here + time_step * north_tend)
    return (east_next, north_next, tracer(temper), tracer(saline))


def shift(value, mapping):
    lat_size = lax.axis_size("lat")
    lon_size = lax.axis_size("lon")
    pairs = []
    for a in range(lat_size):
        for b in range(lon_size):
            target = mapping(a, b, lat_size, lon_size)
            if target is not None:
                pairs.append((b * lat_size + a, target[1] * lat_size + target[0]))
    return lax.ppermute(value, ("lon", "lat"), pairs)


def per_device(
    eastbound_current,
    poleward_current,
    warmth_excess,
    saltiness_excess,
    water_indicator,
    column_layer_count,
):
    fields = jnp.stack(
        (
            eastbound_current,
            poleward_current,
            warmth_excess,
            saltiness_excess,
            water_indicator.astype(jnp.float32),
        )
    )
    top = fields[:, :, -1, :]
    bottom = fields[:, :, 0, :]
    west_col = fields[:, :, :, 0]
    east_col = fields[:, :, :, -1]

    def east_of(a, b, na, nl):
        return (a, (b + 1) % nl)

    def west_of(a, b, na, nl):
        return (a, (b - 1) % nl)

    def north_of(a, b, na, nl):
        return (a + 1, b) if a + 1 < na else None

    def south_of(a, b, na, nl):
        return (a - 1, b) if a > 0 else None

    def north_east(a, b, na, nl):
        return (a + 1, (b + 1) % nl) if a + 1 < na else None

    def north_west(a, b, na, nl):
        return (a + 1, (b - 1) % nl) if a + 1 < na else None

    def south_east(a, b, na, nl):
        return (a - 1, (b + 1) % nl) if a > 0 else None

    def south_west(a, b, na, nl):
        return (a - 1, (b - 1) % nl) if a > 0 else None

    def mirror(a, b, na, nl):
        return (a, nl - 1 - b) if a == na - 1 else None

    def mirror_left(a, b, na, nl):
        return (a, (nl - b) % nl) if a == na - 1 else None

    def mirror_right(a, b, na, nl):
        return (a, (nl - 2 - b) % nl) if a == na - 1 else None

    halo_west = shift(east_col, east_of)
    halo_east = shift(west_col, west_of)
    halo_south = shift(top, north_of)
    halo_north = shift(bottom, south_of)
    corner_sw = shift(top[:, :, -1:], north_east)
    corner_se = shift(top[:, :, :1], north_west)
    corner_nw = shift(bottom[:, :, -1:], south_east)
    corner_ne = shift(bottom[:, :, :1], south_west)
    fold_row = shift(top, mirror)
    fold_left = shift(top[:, :, :1], mirror_left)
    fold_right = shift(top[:, :, -1:], mirror_right)

    sign = jnp.array([-1.0, -1.0, 1.0, 1.0, 1.0], dtype=jnp.float32)[:, None, None]
    ghost = sign * jnp.concatenate([fold_left, fold_row[:, :, ::-1], fold_right], axis=2)
    north_row = jnp.concatenate([corner_nw, halo_north, corner_ne], axis=2)
    is_top = lax.axis_index("lat") == lax.axis_size("lat") - 1
    north_row = jnp.where(is_top, ghost, north_row)
    south_row = jnp.concatenate([corner_sw, halo_south, corner_se], axis=2)
    middle = jnp.concatenate([halo_west[..., None], fields, halo_east[..., None]], axis=3)
    extended = jnp.concatenate([south_row[:, :, None, :], middle, north_row[:, :, None, :]], axis=2)
    rows = eastbound_current.shape[1]
    row_start = lax.axis_index("lat") * rows
    total_rows = rows * lax.axis_size("lat")
    return advance(extended, column_layer_count, row_start, total_rows)


def solution(mesh):
    placed = (
        P(None, "lat", "lon"),
        P(None, "lat", "lon"),
        P(None, "lat", "lon"),
        P(None, "lat", "lon"),
        P(None, "lat", "lon"),
        P("lat", "lon"),
    )
    return jax.shard_map(
        per_device,
        mesh=mesh,
        in_specs=placed,
        out_specs=(
            P(None, "lat", "lon"),
            P(None, "lat", "lon"),
            P(None, "lat", "lon"),
            P(None, "lat", "lon"),
        ),
        check_vma=False,
    )
```

profile of v0, /device:TPU:31, one launch (start us, length us, event | category | flops | bytes accessed | tf_op | source)
XLA Modules:
  0.0 106.6 jit_solution(14959910278308689803)
XLA Ops:
  0.6 0.0 copy-start.2
  0.6 0.0 copy-start.3
  0.7 2.0 %bitcast_dynamic-update-slice_fusion.4 = f32[5,32,32,256]{3,1,0,2:T(8,128)S(1)} fusion(f32[32,32,256]{2,1,0:T(8,128)} %param.7), kind=kLoop, calls=%fused_computation.60 | loop fusion | bytes 2097152
  2.6 0.0 copy-start.4
  2.7 0.6 bitcast_dynamic-update-slice_fusion.3
  3.3 0.0 copy-start.5
  3.3 0.6 bitcast_dynamic-update-slice_fusion.2
  3.9 0.0 copy-done.4
  3.9 0.6 bitcast_dynamic-update-slice_fusion.1
  4.5 0.0 copy-done.5
  4.6 0.6 bitcast_dynamic-update-slice_fusion
  5.2 0.9 fusion.65
  6.1 1.5 %collective-permute-start.5 = (f32[5,32,1]{2,1,0:T(8,128)}, f32[5,32,1]{2,1,0:T(8,128)}, u32[]{:S(2)}, u32[]{:S(2)}) collective-permute-start(f32[5,32,1]{2,1,0:T(8,128)} %get-tuple-element.20), channel_id=1, source_target_pairs={{15,15},{31,255},{47,239},{63,223},{79,207},{95,191},{111,175},{12... | collective-permute-start | bytes 1928 | tf_op jit(solution)/shard_map/ppermute | solution.py:173
  7.6 4.1 %collective-permute-start.2 = (f32[5,32,1]{2,1,0:T(8,128)}, f32[5,32,1]{2,1,0:T(8,128)S(1)}, u32[]{:S(2)}, u32[]{:S(2)}) collective-permute-start(f32[5,32,1]{2,1,0:T(8,128)} %get-tuple-element.20), channel_id=1, source_target_pairs={{0,241},{16,1},{32,17},{48,33},{64,49},{80,65},{96,81},{112,97},{1... | collective-permute-start | bytes 1928 | tf_op jit(solution)/shard_map/ppermute | solution.py:173
  11.7 1.3 %collective-permute-start.7 = (f32[5,32,1]{2,1,0:T(8,128)}, f32[5,32,1]{2,1,0:T(8,128)}, u32[]{:S(2)}, u32[]{:S(2)}) collective-permute-start(f32[5,32,1]{2,1,0:T(8,128)} %get-tuple-element.21), channel_id=1, source_target_pairs={{15,239},{31,223},{47,207},{63,191},{79,175},{95,159},{111,143},{1... | collective-permute-start | bytes 1928 | tf_op jit(solution)/shard_map/ppermute | solution.py:173
  13.1 2.4 %fusion.64 = (f32[5,32,32,1]{3,1,0,2:T(8,128)S(1)}, f32[5,32,32,1]{3,1,0,2:T(8,128)}) fusion(f32[5,32,32,256]{3,1,0,2:T(8,128)S(1)} %bitcast_dynamic-update-slice_fusion), kind=kLoop, calls=%fused_computation.108 | loop fusion | bytes 81920 | tf_op jit(solution)/shard_map/slice | solution.py:196
  15.5 0.0 copy-done.1
  15.5 3.0 %copy.61 = f32[5,32,32,1]{2,1,0,3:T(8,128)S(1)} copy(f32[5,32,32,1]{3,1,0,2:T(8,128)} %get-tuple-element.14) | data formatting | bytes 40960 | tf_op jit(solution)/shard_map/slice | solution.py:195
  18.5 0.2 collective-permute-start.4
  18.6 1.4 %copy.60 = f32[5,32,32,1]{2,1,0,3:T(8,128)S(1)} copy(f32[5,32,32,1]{3,1,0,2:T(8,128)S(1)} %get-tuple-element.13) | data formatting | bytes 40960 | tf_op jit(solution)/shard_map/slice | solution.py:196
  20.0 3.8 %collective-permute-start.3 = (f32[5,32,32]{2,1,0:T(8,128)S(1)}, f32[5,32,32]{2,1,0:T(8,128)S(1)}, u32[]{:S(2)}, u32[]{:S(2)}) collective-permute-start(f32[5,32,32]{2,1,0:T(8,128)S(1)} %bitcast.52), channel_id=1, source_target_pairs={{0,16},{16,32},{32,48},{48,64},{64,80},{80,96},{96,112},{112,128},... | collective-permute-start | bytes 61448 | tf_op jit(solution)/shard_map/ppermute | solution.py:173
  23.8 0.1 slice_bitcast_fusion.7
  23.9 0.7 fusion.66
  24.7 0.7 collective-permute-done.3
  25.3 7.7 %collective-permute-start = (f32[5,32,1]{2,1,0:T(8,128)}, f32[5,32,1]{2,1,0:T(8,128)}, u32[]{:S(2)}, u32[]{:S(2)}) collective-permute-start(f32[5,32,1]{2,1,0:T(8,128)} %get-tuple-element.21), channel_id=1, source_target_pairs={{0,17},{16,33},{32,49},{48,65},{64,81},{80,97},{96,113},{112,129},... | collective-permute-start | bytes 1928 | tf_op jit(solution)/shard_map/ppermute | solution.py:173
  33.1 2.2 %copy.62 = f32[5,32,32,1]{3,1,0,2:T(8,128)S(1)} copy(f32[5,32,32,1]{2,1,0,3:T(8,128)S(1)} %bitcast.51) | data formatting | bytes 40960 | tf_op jit(solution)/shard_map/broadcast_in_dim | solution.py:249
  35.3 0.0 collective-permute-done.4
  35.3 0.9 collective-permute-start.6
  36.2 3.5 %copy.63 = f32[5,32,32,1]{3,1,0,2:T(8,128)} copy(f32[5,32,32,1]{2,1,0,3:T(8,128)S(1)} %bitcast.49) | data formatting | bytes 40960 | tf_op jit(solution)/shard_map/broadcast_in_dim | solution.py:249
  39.7 5.7 %pad_maximum_fusion.1 = f32[5,32,32,258]{3,1,0,2:T(8,128)S(1)} fusion(f32[5,32,32,1]{3,1,0,2:T(8,128)} %copy.63, f32[5,32,32,256]{3,1,0,2:T(8,128)} %copy-done.1, f32[5,32,32,1]{3,1,0,2:T(8,128)S(1)} %copy.62), kind=kLoop, calls=%fused_computation.1 | loop fusion | flops 2641920 | bytes 10567680 | tf_op jit(solution)/shard_map/concatenate | solution.py:249
  45.3 0.0 copy-start.8
  45.4 0.0 copy-start.9
  45.4 0.0 copy-start.7
  45.4 7.5 %copy.70 = f32[5,32,32,258]{3,2,1,0:T(8,128)} copy(f32[5,32,32,258]{3,1,0,2:T(8,128)S(1)} %pad_maximum_fusion.1) | data formatting | bytes 10567680 | tf_op jit(solution)/shard_map/concatenate | solution.py:249
  52.9 0.0 collective-permute-done.6
  52.9 4.4 %collective-permute-start.9 = (f32[5,32,256]{2,1,0:T(8,128)S(1)}, f32[5,32,256]{2,1,0:T(8,128)S(1)}, u32[]{:S(2)}, u32[]{:S(2)}) collective-permute-start(f32[5,32,256]{2,1,0:T(8,128)S(1)} %get-tuple-element.16), channel_id=1, source_target_pairs={{1,0},{17,16},{33,32},{49,48},{65,64},{81,80},{97,96},{113,112},{1... | collective-permute-start | bytes 491528 | tf_op jit(solution)/shard_map/ppermute | solution.py:173
  57.3 0.2 rev.3
  57.6 0.0 collective-permute-done.5
  57.6 1.9 %collective-permute-start.1 = (f32[5,32,256]{2,1,0:T(8,128)S(1)}, f32[5,32,256]{2,1,0:T(8,128)S(1)}, u32[]{:S(2)}, u32[]{:S(2)}) collective-permute-start(f32[5,32,256]{2,1,0:T(8,128)S(1)} %get-tuple-element.15), channel_id=1, source_target_pairs={{0,1},{16,17},{32,33},{48,49},{64,65},{80,81},{96,97},{112,113},{1... | collective-permute-start | bytes 491528 | tf_op jit(solution)/shard_map/ppermute | solution.py:173
  59.5 0.0 collective-permute-done.7
  59.5 0.0 copy-done.8
  59.5 6.7 %collective-permute-start.8 = (f32[5,32,1]{2,1,0:T(8,128)S(1)}, f32[5,32,1]{2,1,0:T(8,128)S(1)}, u32[]{:S(2)}, u32[]{:S(2)}) collective-permute-start(f32[5,32,1]{2,1,0:T(8,128)S(1)} %copy-done.8), channel_id=1, source_target_pairs={{1,16},{17,32},{33,48},{49,64},{65,80},{81,96},{97,112},{113,128},... | collective-permute-start | bytes 1928 | tf_op jit(solution)/shard_map/ppermute | solution.py:173
  66.3 1.1 %maximum_multiply_fusion = f32[5,32,1,258]{3,1,0,2:T(8,128)S(1)} fusion(f32[5,32,1,1]{3,1,0,2:T(8,128)} %bitcast.13, f32[5,32,1,256]{3,1,0,2:T(8,128)S(1)} %bitcast.46, f32[5,32,1,1]{3,1,0,2:T(8,128)} %bitcast.11, f32[5]{0:T(128)S(1)} %copy-done.9), kind=kLoop, calls=%fused_computation.91 | loop fusion | flops 123840 | bytes 330260 | tf_op jit(solution)/shard_map/mul | solution.py:244
  67.3 0.0 collective-permute-done.2
  67.4 1.9 %collective-permute-start.10 = (f32[5,32,1]{2,1,0:T(8,128)S(1)}, f32[5,32,1]{2,1,0:T(8,128)S(1)}, u32[]{:S(2)}, u32[]{:S(2)}) collective-permute-start(f32[5,32,1]{2,1,0:T(8,128)S(1)} %copy-done.7), channel_id=1, source_target_pairs={{1,240},{17,0},{33,16},{49,32},{65,48},{81,64},{97,80},{113,96},{1... | collective-permute-start | bytes 1928 | tf_op jit(solution)/shard_map/ppermute | solution.py:173
  69.3 0.0 collective-permute-done
  69.3 0.0 collective-permute-done.1
  69.3 1.0 maximum_bitcast_fusion
  70.4 0.3 copy.69
  70.6 0.0 collective-permute-done.9
  70.6 0.1 concatenate.72
  70.7 0.0 collective-permute-done.8
  70.8 5.4 %collective-permute-done.10 = f32[5,32,1]{2,1,0:T(8,128)S(1)} collective-permute-done((f32[5,32,1]{2,1,0:T(8,128)S(1)}, f32[5,32,1]{2,1,0:T(8,128)S(1)}, u32[]{:S(2)}, u32[]{:S(2)}) %collective-permute-start.10) | collective-permute-done | bytes 672 | tf_op jit(solution)/shard_map/ppermute | solution.py:173
  76.1 0.8 broadcast_select_fusion
  76.9 4.7 %pad_maximum_fusion = f32[5,32,34,258]{3,2,1,0:T(8,128)S(1)} fusion(f32[5,32,1,258]{3,2,1,0:T(1,128)S(1)} %broadcast_select_fusion, f32[5,32,32,258]{3,2,1,0:T(8,128)} %copy.70, f32[5,32,1,258]{3,2,1,0:T(1,128)S(1)} %copy.69), kind=kLoop, calls=%fused_computation | loop fusion | flops 2807040 | bytes 11228160 | tf_op jit(solution)/shard_map/concatenate | solution.py:250
  81.6 1.9 %slice_bitcast_fusion.1 = (f32[32,34,258]{2,1,0:T(8,128)S(1)}, f32[32,34,258]{2,1,0:T(8,128)}, f32[32,34,258]{2,1,0:T(8,128)S(1)}, f32[32,34,258]{2,1,0:T(8,128)S(1)}, f32[32,34,258]{2,1,0:T(8,128)S(1)}) fusion(f32[5,32,34,258]{3,2,1,0:T(8,128)S(1)} %pad_maximum_fusion), kind=kLoop, calls=%fused_computation.3 | loop fusion | bytes 11228160 | tf_op jit(solution)/shard_map/squeeze | solution.py:39
  83.5 1.1 %fusion = f32[32,34,258]{2,1,0:T(8,128)S(1)} fusion(f32[32]{0:T(128)S(1)} %get-tuple-element.24, f32[32]{0:T(128)S(1)} %get-tuple-element.25, f32[5,32,34,258]{3,2,1,0:T(8,128)S(1)} %pad_maximum_fusion), kind=kOutput, calls=%fused_computation.7 | output fusion | flops 12912384 | bytes 7022080 | tf_op jit(solution)/shard_map/jit(cumsum)/reduce_window_sum | solution.py:62
  84.7 0.4 copy-done
  85.1 1.2 %fusion.41 = (f32[31,32,256]{2,1,0:T(8,128)S(1)}, f32[31,32,256]{2,1,0:T(8,128)S(1)}) fusion(f32[32,34,258]{2,1,0:T(8,128)S(1)} %copy-done, f32[32,34,258]{2,1,0:T(8,128)S(1)} %get-tuple-element.12, s32[32,256]{1,0:T(8,128)S(1)} %copy-done.6, s32[31]{0:T(128)S(1)} %slice_bitcast_fusion.7), kind=kLoop, calls=%fused_computation.67 | loop fusion | flops 1523712 | bytes 6127740 | tf_op jit(solution)/shard_map/mul | solution.py:29
  86.3 4.5 %add_multiply_fusion = (f32[32,32,256]{2,1,0:T(8,128)}, f32[32,32,256]{2,1,0:T(8,128)S(1)}) fusion(f32[31,32,256]{2,1,0:T(8,128)S(1)} %get-tuple-element.6, f32[32,34,258]{2,1,0:T(8,128)S(1)} %copy-done, f32[32,34,258]{2,1,0:T(8,128)S(1)} %get-tuple-element.12, f32[32,34,258]{2,1,0:T(8,128)S(1)} %get-tuple-element.10, f32[32,34,258]{2,1,0:T(8,128)S(1)} %get-tuple-element.11), kind=kLoop, calls=%fused_computation.62 | loop fusion | flops 10485760 | bytes 17793024 | tf_op jit(solution)/shard_map/mul | solution.py:90
  90.8 1.7 %fusion.42 = (f32[31,32,256]{2,1,0:T(8,128)S(1)}, f32[31,32,256]{2,1,0:T(8,128)S(1)}, f32[31,32,256]{2,1,0:T(8,128)S(1)}) fusion(f32[31,32,256]{2,1,0:T(8,128)S(1)} %get-tuple-element.7, f32[32,34,258]{2,1,0:T(8,128)S(1)} %get-tuple-element.8, f32[32,34,258]{2,1,0:T(8,128)S(1)} %get-tuple-element.10, f32[32,34,258]{2,1,0:T(8,128)S(1)} %get-tuple-element.11), kind=kLoop, calls=%fused_computation.69 | loop fusion | flops 1523712 | bytes 10158080 | tf_op jit(solution)/shard_map/mul | solution.py:29
  92.5 3.9 %add_multiply_fusion.1 = f32[32,32,256]{2,1,0:T(8,128)} fusion(f32[31,32,256]{2,1,0:T(8,128)S(1)} %get-tuple-element.17, f32[32,34,258]{2,1,0:T(8,128)S(1)} %get-tuple-element.8, f32[32,32,256]{2,1,0:T(8,128)S(1)} %get-tuple-element.5, f32[32,34,258]{2,1,0:T(8,128)S(1)} %get-tuple-element.12, f32[32,34,258]{2,1,0:T(8,128)S(1)} %get-tuple-element.10, ...), kind=kLoop, calls=%fused_computation.63 | loop fusion | flops 10223616 | bytes 16744448 | tf_op jit(solution)/shard_map/mul | solution.py:90
  96.4 4.8 %fusion.23 = f32[32,32,256]{2,1,0:T(8,128)} fusion(f32[32,34,258]{2,1,0:T(8,128)S(1)} %fusion, f32[32,34,258]{2,1,0:T(8,128)S(1)} %get-tuple-element.12, f32[31,32,256]{2,1,0:T(8,128)S(1)} %get-tuple-element.18, f32[32,34,258]{2,1,0:T(8,128)S(1)} %get-tuple-element.10, f32[32,34,258]{2,1,0:T(8,128)S(1)} %get-tuple-element.11, f32[32]{0:T(128)S(1)} %get-tuple-element.26, ...), kind=kLoop, calls=%fused_computation.32 | loop fusion | flops 15204352 | bytes 19923072 | tf_op jit(solution)/shard_map/mul | solution.py:160
  101.2 5.4 %fusion.19 = f32[32,32,256]{2,1,0:T(8,128)} fusion(f32[32,32,256]{2,1,0:T(8,128)S(1)} %get-tuple-element.5, f32[32,34,258]{2,1,0:T(8,128)S(1)} %fusion, f32[32,34,258]{2,1,0:T(8,128)S(1)} %get-tuple-element.12, f32[31,32,256]{2,1,0:T(8,128)S(1)} %get-tuple-element.19, f32[32,34,258]{2,1,0:T(8,128)S(1)} %get-tuple-element.11, ...), kind=kLoop, calls=%fused_computation.28 | loop fusion | flops 14680064 | bytes 20971648 | tf_op jit(solution)/shard_map/mul | solution.py:137
  (13 shorter events, 0.1 us)
Async XLA Ops:
  0.6 2.0 %copy-start.2 = (f32[32,32,256]{2,1,0:T(8,128)S(1)}, f32[32,32,256]{2,1,0:T(8,128)}, u32[]{:S(2)}) copy-start(f32[32,32,256]{2,1,0:T(8,128)} %param.8) | copy-start | bytes 3145732
  0.6 2.6 %copy-start.3 = (f32[32,32,256]{2,1,0:T(8,128)S(1)}, f32[32,32,256]{2,1,0:T(8,128)}, u32[]{:S(2)}) copy-start(f32[32,32,256]{2,1,0:T(8,128)} %param.9) | copy-start | bytes 3145732
  2.6 1.3 %copy-start.4 = (f32[32,32,256]{2,1,0:T(8,128)S(1)}, f32[32,32,256]{2,1,0:T(8,128)}, u32[]{:S(2)}) copy-start(f32[32,32,256]{2,1,0:T(8,128)} %param.10) | copy-start | bytes 3145732
  3.3 1.3 %copy-start.5 = (s32[32,32,256]{2,1,0:T(8,128)S(1)}, s32[32,32,256]{2,1,0:T(8,128)}, u32[]{:S(2)}) copy-start(s32[32,32,256]{2,1,0:T(8,128)} %param.11) | copy-start | bytes 3145732
  5.2 10.3 %copy-start.1 = (f32[5,32,32,256]{3,1,0,2:T(8,128)}, f32[5,32,32,256]{3,1,0,2:T(8,128)S(1)}, u32[]{:S(2)}) copy-start(f32[5,32,32,256]{3,1,0,2:T(8,128)S(1)} %bitcast_dynamic-update-slice_fusion) | copy-start | bytes 15728644
  6.1 51.5 %collective-permute-start.5 = (f32[5,32,1]{2,1,0:T(8,128)}, f32[5,32,1]{2,1,0:T(8,128)}, u32[]{:S(2)}, u32[]{:S(2)}) collective-permute-start(f32[5,32,1]{2,1,0:T(8,128)} %get-tuple-element.20), channel_id=1, source_target_pairs={{15,15},{31,255},{47,239},{63,223},{79,207},{95,191},{111,175},{12... | collective-permute-start | bytes 1928 | tf_op jit(solution)/shard_map/ppermute | solution.py:173
  7.6 59.7 %collective-permute-start.2 = (f32[5,32,1]{2,1,0:T(8,128)}, f32[5,32,1]{2,1,0:T(8,128)S(1)}, u32[]{:S(2)}, u32[]{:S(2)}) collective-permute-start(f32[5,32,1]{2,1,0:T(8,128)} %get-tuple-element.20), channel_id=1, source_target_pairs={{0,241},{16,1},{32,17},{48,33},{64,49},{80,65},{96,81},{112,97},{1... | collective-permute-start | bytes 1928 | tf_op jit(solution)/shard_map/ppermute | solution.py:173
  11.7 47.8 %collective-permute-start.7 = (f32[5,32,1]{2,1,0:T(8,128)}, f32[5,32,1]{2,1,0:T(8,128)}, u32[]{:S(2)}, u32[]{:S(2)}) collective-permute-start(f32[5,32,1]{2,1,0:T(8,128)} %get-tuple-element.21), channel_id=1, source_target_pairs={{15,239},{31,223},{47,207},{63,191},{79,175},{95,159},{111,143},{1... | collective-permute-start | bytes 1928 | tf_op jit(solution)/shard_map/ppermute | solution.py:173
  18.5 5.5 %copy-start.6 = (s32[32,256]{1,0:T(8,128)S(1)}, s32[32,256]{1,0:T(8,128)}, u32[]{:S(2)}) copy-start(s32[32,256]{1,0:T(8,128)} %param.12) | copy-start | bytes 98308
  18.5 16.9 %collective-permute-start.4 = (f32[5,32,32]{2,1,0:T(8,128)S(1)}, f32[5,32,32]{2,1,0:T(8,128)S(1)}, u32[]{:S(2)}, u32[]{:S(2)}) collective-permute-start(f32[5,32,32]{2,1,0:T(8,128)S(1)} %bitcast.50), channel_id=1, source_target_pairs={{0,240},{16,0},{32,16},{48,32},{64,48},{80,64},{96,80},{112,96},{1... | collective-permute-start | bytes 61448 | tf_op jit(solution)/shard_map/ppermute | solution.py:173
  20.0 5.3 %collective-permute-start.3 = (f32[5,32,32]{2,1,0:T(8,128)S(1)}, f32[5,32,32]{2,1,0:T(8,128)S(1)}, u32[]{:S(2)}, u32[]{:S(2)}) collective-permute-start(f32[5,32,32]{2,1,0:T(8,128)S(1)} %bitcast.52), channel_id=1, source_target_pairs={{0,16},{16,32},{32,48},{48,64},{64,80},{80,96},{96,112},{112,128},... | collective-permute-start | bytes 61448 | tf_op jit(solution)/shard_map/ppermute | solution.py:173
  25.3 44.0 %collective-permute-start = (f32[5,32,1]{2,1,0:T(8,128)}, f32[5,32,1]{2,1,0:T(8,128)}, u32[]{:S(2)}, u32[]{:S(2)}) collective-permute-start(f32[5,32,1]{2,1,0:T(8,128)} %get-tuple-element.21), channel_id=1, source_target_pairs={{0,17},{16,33},{32,49},{48,65},{64,81},{80,97},{96,113},{112,129},... | collective-permute-start | bytes 1928 | tf_op jit(solution)/shard_map/ppermute | solution.py:173
  35.3 17.6 %collective-permute-start.6 = (f32[5,32,256]{2,1,0:T(8,128)S(1)}, f32[5,32,256]{2,1,0:T(8,128)S(1)}, u32[]{:S(2)}, u32[]{:S(2)}) collective-permute-start(f32[5,32,256]{2,1,0:T(8,128)S(1)} %get-tuple-element.15), channel_id=1, source_target_pairs={{15,255},{31,239},{47,223},{63,207},{79,191},{95,175},{111,159},{1... | collective-permute-start | bytes 491528 | tf_op jit(solution)/shard_map/ppermute | solution.py:173
  45.3 14.2 %copy-start.8 = (f32[5,32,1]{2,1,0:T(8,128)S(1)}, f32[5,32,1]{2,1,0:T(8,128)}, u32[]{:S(2)}) copy-start(f32[5,32,1]{2,1,0:T(8,128)} %get-tuple-element.22) | copy-start | bytes 1924
  45.4 20.9 %copy-start.9 = (f32[5]{0:T(128)S(1)}, f32[5]{0:T(128)}, u32[]{:S(2)}) copy-start(f32[5]{0:T(128)} %constant.64.clone) | copy-start | bytes 64
  45.4 22.0 %copy-start.7 = (f32[5,32,1]{2,1,0:T(8,128)S(1)}, f32[5,32,1]{2,1,0:T(8,128)}, u32[]{:S(2)}) copy-start(f32[5,32,1]{2,1,0:T(8,128)} %get-tuple-element.23) | copy-start | bytes 1924
  52.9 17.7 %collective-permute-start.9 = (f32[5,32,256]{2,1,0:T(8,128)S(1)}, f32[5,32,256]{2,1,0:T(8,128)S(1)}, u32[]{:S(2)}, u32[]{:S(2)}) collective-permute-start(f32[5,32,256]{2,1,0:T(8,128)S(1)} %get-tuple-element.16), channel_id=1, source_target_pairs={{1,0},{17,16},{33,32},{49,48},{65,64},{81,80},{97,96},{113,112},{1... | collective-permute-start | bytes 491528 | tf_op jit(solution)/shard_map/ppermute | solution.py:173
  57.6 11.7 %collective-permute-start.1 = (f32[5,32,256]{2,1,0:T(8,128)S(1)}, f32[5,32,256]{2,1,0:T(8,128)S(1)}, u32[]{:S(2)}, u32[]{:S(2)}) collective-permute-start(f32[5,32,256]{2,1,0:T(8,128)S(1)} %get-tuple-element.15), channel_id=1, source_target_pairs={{0,1},{16,17},{32,33},{48,49},{64,65},{80,81},{96,97},{112,113},{1... | collective-permute-start | bytes 491528 | tf_op jit(solution)/shard_map/ppermute | solution.py:173
  59.5 11.2 %collective-permute-start.8 = (f32[5,32,1]{2,1,0:T(8,128)S(1)}, f32[5,32,1]{2,1,0:T(8,128)S(1)}, u32[]{:S(2)}, u32[]{:S(2)}) collective-permute-start(f32[5,32,1]{2,1,0:T(8,128)S(1)} %copy-done.8), channel_id=1, source_target_pairs={{1,16},{17,32},{33,48},{49,64},{65,80},{81,96},{97,112},{113,128},... | collective-permute-start | bytes 1928 | tf_op jit(solution)/shard_map/ppermute | solution.py:173
  67.4 8.8 %collective-permute-start.10 = (f32[5,32,1]{2,1,0:T(8,128)S(1)}, f32[5,32,1]{2,1,0:T(8,128)S(1)}, u32[]{:S(2)}, u32[]{:S(2)}) collective-permute-start(f32[5,32,1]{2,1,0:T(8,128)S(1)} %copy-done.7), channel_id=1, source_target_pairs={{1,240},{17,0},{33,16},{49,32},{65,48},{81,64},{97,80},{113,96},{1... | collective-permute-start | bytes 1928 | tf_op jit(solution)/shard_map/ppermute | solution.py:173
  83.5 1.5 %copy-start = (f32[32,34,258]{2,1,0:T(8,128)S(1)}, f32[32,34,258]{2,1,0:T(8,128)}, u32[]{:S(2)}) copy-start(f32[32,34,258]{2,1,0:T(8,128)} %get-tuple-element.9) | copy-start | bytes 3368452
where the time goes:
time: 107 us
  other arithmetic  36.5 us (34%)
  starting transfers between devices  34.5 us (32%)
  local copies, waits for them, and re-layouts  28.6 us (27%)
  waiting for transfers between devices  6.05 us (6%)
    ppermute x11, starting transfers between devices, shift(): return lax.ppermute(value, ('lon', 'lat'), pairs)  34.5 us
    mul x2, other arithmetic, tracer(): return wet_here * (centre + time_step * tendency)  8.4 us
    concatenate x1, local copies, waits for them, and re-layouts, per_device(): jnp.concatenate([halo_west[..., None], fields, halo_east[..., None]], axi...  7.52 us
    ppermute x11, waiting for transfers between devices, shift(): return lax.ppermute(value, ('lon', 'lat'), pairs)  6.05 us
    concatenate x1, other arithmetic, per_device(): jnp.concatenate([halo_west[..., None], fields, halo_east[..., None]], axi...  5.68 us
    mul x1, other arithmetic, advance(): east_next = mask_east * (east_here + time_step * east_tend)  5.38 us
    mul x1, other arithmetic, advance(): north_next = mask_north * (north_here + time_step * north_tend)  4.8 us
    concatenate x1, other arithmetic, per_device(): jnp.concatenate([south_row[:, :, None, :], middle, north_row[:, :, None,...  4.68 us
  transfers between devices with their start and end apart: 11, of which 2 were waited for; matrix products, arithmetic and copies ran while one was open for 27% of the time, Pallas kernels for 0%

commit v1 on v0

--- a/solution.py
+++ b/solution.py
@@ -1,6 +1,8 @@
 import jax
 import jax.numpy as jnp
 from jax import lax
+from jax.experimental import pallas as pl
+from jax.experimental.pallas import tpu as pltpu
 from jax.sharding import PartitionSpec as P
 
 time_step = 0.2
@@ -173,6 +175,183 @@
     return lax.ppermute(value, ("lon", "lat"), pairs)
 
 
+def stencil_kernel(
+    cor_ref, u_ref, v_ref, t_ref, s_ref, wet_ref, clc_ref, rows_ref, cols_ref,
+    east_ref, north_ref, temp_ref, salt_ref,
+):
+    levels, rows, cols = u_ref.shape
+    fields = 5
+    lane = lax.broadcasted_iota(jnp.int32, (rows, cols), 1)
+    sub = lax.broadcasted_iota(jnp.int32, (rows, cols), 0)
+    at_east = lane == cols - 1
+    at_west = lane == 0
+    at_north = sub == rows - 1
+    at_south = sub == 0
+    cor_t = cor_ref[0]
+    cor_v = cor_ref[1]
+    count = clc_ref[...]
+
+    def east(x, col):
+        return jnp.where(at_east, col, pltpu.roll(x, cols - 1, 1))
+
+    def west(x, col):
+        return jnp.where(at_west, col, pltpu.roll(x, 1, 1))
+
+    def north(x, row):
+        return jnp.where(at_north, row, pltpu.roll(x, rows - 1, 0))
+
+    def south(x, row):
+        return jnp.where(at_south, row, pltpu.roll(x, 1, 0))
+
+    def body(k, carry):
+        pres, pres_e, pres_n = carry
+        km = jnp.maximum(k - 1, 0)
+        kp = jnp.minimum(k + 1, levels - 1)
+
+        def row(variant, field):
+            return rows_ref[variant * fields + field, pl.ds(k, 1), :]
+
+        def col(field):
+            pair = cols_ref[field, k]
+            return pair[:, 0:1], pair[:, 1:2]
+
+        w = wet_ref[k].astype(jnp.float32)
+        w_above = wet_ref[km].astype(jnp.float32)
+        w_below = wet_ref[kp].astype(jnp.float32)
+        w_wc, w_ec = col(4)
+        w_e = east(w, w_ec)
+        w_w = west(w, w_wc)
+        w_n = north(w, row(0, 4))
+        w_s = south(w, row(3, 4))
+        w_ne = north(w_e, row(1, 4))
+        w_se = south(w_e, row(4, 4))
+        w_nw = north(w_w, row(2, 4))
+        mask_east = w * w_e
+        mask_west = w_w * w
+        mask_north = w * w_n
+        mask_south = w_s * w
+        mix_below = jnp.where(
+            k < levels - 1, w * w_below * (k + 1 < count).astype(jnp.float32), 0.0
+        )
+        mix_above = jnp.where(k > 0, w_above * w * (k < count).astype(jnp.float32), 0.0)
+        bottom = (k == count - 1).astype(jnp.float32)
+
+        def column(ref, centre):
+            upper = ref[km]
+            lower = ref[kp]
+            above = -vertical_diff * mix_above * (centre - upper)
+            below = -vertical_diff * mix_below * (lower - centre)
+            return above - below
+
+        depth = (k.astype(jnp.float32) + 0.5) * level_depth
+
+        def density(temper, saline):
+            return (
+                -thermal_expand * (1.0 + 0.5 * cabbel_temp * temper + thermo_temp * depth) * temper
+                + haline_contract * (1.0 - 0.5 * cabbel_salt * saline - thermo_salt * depth) * saline
+                - cabbel_mixed * temper * saline
+            )
+
+        tc = t_ref[k]
+        sc = s_ref[k]
+        t_wc, t_ec = col(2)
+        s_wc, s_ec = col(3)
+        pres = pres + w * density(tc, sc)
+        pres_e = pres_e + w_ec * density(t_ec, s_ec)
+        pres_n = pres_n + row(0, 4) * density(row(0, 2), row(0, 3))
+        p_e = east(pres, pres_e)
+        p_n = north(pres, pres_n)
+
+        uc = u_ref[k]
+        u_wc, u_ec = col(0)
+        u_e = east(uc, u_ec)
+        u_w = west(uc, u_wc)
+        u_n = north(uc, row(0, 0))
+        u_s = south(uc, row(3, 0))
+        u_nw = north(u_w, row(2, 0))
+        vc = v_ref[k]
+        v_wc, v_ec = col(1)
+        v_e = east(vc, v_ec)
+        v_w = west(vc, v_wc)
+        v_n = north(vc, row(0, 1))
+        v_s = south(vc, row(3, 1))
+        v_se = south(v_e, row(4, 1))
+
+        def tracer(ref, centre, field, wcol, ecol):
+            east_side = east(centre, ecol)
+            west_side = west(centre, wcol)
+            north_side = north(centre, row(0, field))
+            south_side = south(centre, row(3, field))
+            flux_east = mask_east * (
+                uc * (centre + east_side) * 0.5 - lateral_diff * (east_side - centre)
+            )
+            flux_west = mask_west * (
+                u_w * (west_side + centre) * 0.5 - lateral_diff * (centre - west_side)
+            )
+            flux_north = mask_north * (
+                vc * (centre + north_side) * 0.5 - lateral_diff * (north_side - centre)
+            )
+            flux_south = mask_south * (
+                v_s * (south_side + centre) * 0.5 - lateral_diff * (centre - south_side)
+            )
+            tendency = (
+                flux_west - flux_east + (flux_south - flux_north) + column(ref, centre)
+            )
+            return w * (centre + time_step * tendency)
+
+        temp_ref[k] = tracer(t_ref, tc, 2, t_wc, t_ec)
+        salt_ref[k] = tracer(s_ref, sc, 3, s_wc, s_ec)
+
+        corner_ne = w * w_e * w_n * w_ne
+        corner_se = w_s * w_se * w * w_e
+        corner_nw = w_w * w * w_nw * w_n
+        half_e = (uc + u_e) * 0.5
+        cell_east = w_e * (half_e * half_e - lateral_diff * (u_e - uc))
+        half_w = (u_w + uc) * 0.5
+        cell_west = w * (half_w * half_w - lateral_diff * (uc - u_w))
+        product_ne = (vc + v_e) * 0.5 * (uc + u_n) * 0.5
+        product_se = (v_s + v_se) * 0.5 * (u_s + uc) * 0.5
+        product_nw = (u_w + u_nw) * 0.5 * (v_w + vc) * 0.5
+        shear_north = corner_ne * (product_ne - lateral_diff * (u_n - uc))
+        shear_south = corner_se * (product_se - lateral_diff * (uc - u_s))
+        north_mean = (vc + v_e + v_s + v_se) * 0.25
+        east_tend = (
+            cell_west
+            - cell_east
+            + (shear_south - shear_north)
+            + cor_t * north_mean
+            - pressure_coef * (p_e - pres)
+            + column(u_ref, uc)
+            - drag_coef * bottom * uc
+        )
+        east_ref[k] = mask_east * (uc + time_step * east_tend)
+        half_n = (vc + v_n) * 0.5
+        cell_north = w_n * (half_n * half_n - lateral_diff * (v_n - vc))
+        half_s = (v_s + vc) * 0.5
+        cell_south = w * (half_s * half_s - lateral_diff * (vc - v_s))
+        stress_east = corner_ne * (product_ne - lateral_diff * (v_e - vc))
+        stress_west = corner_nw * (product_nw - lateral_diff * (vc - v_w))
+        east_mean = (uc + u_w + u_n + u_nw) * 0.25
+        north_tend = (
+            stress_west
+            - stress_east
+            + (cell_south - cell_north)
+            - cor_v * east_mean
+            - pressure_coef * (p_n - pres)
+            + column(v_ref, vc)
+            - drag_coef * bottom * vc
+        )
+        north_ref[k] = mask_north * (vc + time_step * north_tend)
+        return pres, pres_e, pres_n
+
+    init = (
+        jnp.zeros((rows, cols), jnp.float32),
+        jnp.zeros((rows, 1), jnp.float32),
+        jnp.zeros((1, cols), jnp.float32),
+    )
+    lax.fori_loop(0, levels, body, init)
+
+
 def per_device(
     eastbound_current,
     poleward_current,
@@ -181,19 +360,21 @@
     water_indicator,
     column_layer_count,
 ):
-    fields = jnp.stack(
-        (
-            eastbound_current,
-            poleward_current,
-            warmth_excess,
-            saltiness_excess,
-            water_indicator.astype(jnp.float32),
-        )
-    )
-    top = fields[:, :, -1, :]
-    bottom = fields[:, :, 0, :]
-    west_col = fields[:, :, :, 0]
-    east_col = fields[:, :, :, -1]
+    inputs = (
+        eastbound_current,
+        poleward_current,
+        warmth_excess,
+        saltiness_excess,
+        water_indicator,
+    )
+
+    def edge(pick):
+        return jnp.stack([pick(field).astype(jnp.float32) for field in inputs])
+
+    top = edge(lambda f: f[:, -1, :])
+    bottom = edge(lambda f: f[:, 0, :])
+    west_col = edge(lambda f: f[:, :, 0])
+    east_col = edge(lambda f: f[:, :, -1])
 
     def east_of(a, b, na, nl):
         return (a, (b + 1) % nl)
@@ -246,12 +427,43 @@
     is_top = lax.axis_index("lat") == lax.axis_size("lat") - 1
     north_row = jnp.where(is_top, ghost, north_row)
     south_row = jnp.concatenate([corner_sw, halo_south, corner_se], axis=2)
-    middle = jnp.concatenate([halo_west[..., None], fields, halo_east[..., None]], axis=3)
-    extended = jnp.concatenate([south_row[:, :, None, :], middle, north_row[:, :, None, :]], axis=2)
-    rows = eastbound_current.shape[1]
+    width = top.shape[2]
+    halo_rows = jnp.stack(
+        [
+            north_row[:, :, 1 : width + 1],
+            north_row[:, :, 2 : width + 2],
+            north_row[:, :, 0:width],
+            south_row[:, :, 1 : width + 1],
+            south_row[:, :, 2 : width + 2],
+            south_row[:, :, 0:width],
+        ]
+    )
+    halo_rows = halo_rows.reshape((-1,) + halo_rows.shape[2:])
+    halo_cols = jnp.stack([halo_west, halo_east], axis=-1)
+
+    levels, rows, cols = eastbound_current.shape
     row_start = lax.axis_index("lat") * rows
     total_rows = rows * lax.axis_size("lat")
-    return advance(extended, column_layer_count, row_start, total_rows)
+    row_index = (row_start + jnp.arange(rows, dtype=jnp.int32)).astype(jnp.float32)[:, None]
+    coriolis_t = coriolis_max * (2.0 * (row_index + 0.5) / total_rows - 1.0)
+    coriolis_v = coriolis_max * (2.0 * (row_index + 1.0) / total_rows - 1.0)
+    coriolis = jnp.broadcast_to(jnp.stack([coriolis_t, coriolis_v]), (2, rows, cols))
+
+    block = jax.ShapeDtypeStruct((levels, rows, cols), jnp.float32)
+    return pl.pallas_call(
+        stencil_kernel,
+        out_shape=(block, block, block, block),
+    )(
+        coriolis,
+        eastbound_current,
+        poleward_current,
+        warmth_excess,
+        saltiness_excess,
+        water_indicator,
+        column_layer_count,
+        halo_rows,
+        halo_cols,
+    )
 
 
 def solution(mesh):

time: 107 us -> 93.2 us (0.87)
  the two profiles are of different devices: /device:TPU:31 before, /device:TPU:4 now
where the time goes in v1:
time: 93.2 us; the launch traced here: 92.6 us
  starting transfers between devices  30.8 us (33%)
  local copies, waits for them, and re-layouts  27.3 us (29%)
  Pallas kernels  17.7 us (19%)
  waiting for transfers between devices  8.51 us (9%)
  other arithmetic  7.39 us (8%)
  between operations  0.94 us (1%)
    ppermute x11, starting transfers between devices, shift(): return lax.ppermute(value, ('lon', 'lat'), pairs)  30.8 us
    pallas_call x1, Pallas kernels, per_device(): pl.pallas_call(stencil_kernel, out_shape=(block, block, block, block))  17.7 us
    unnamed x38, local copies, waits for them, and re-layouts  10.2 us
    ppermute x11, waiting for transfers between devices, shift(): return lax.ppermute(value, ('lon', 'lat'), pairs)  8.51 us
    slice x5, local copies, waits for them, and re-layouts, per_device(): east_col = edge(lambda f: f[:, :, -1])  4.25 us
    another operation x1, other arithmetic, per_device(): halo_cols = jnp.stack([halo_west, halo_east], axis=-1)  4.01 us
    another operation x4, local copies, waits for them, and re-layouts, edge(): return jnp.stack([pick(field).astype(jnp.float32) for field in inputs])  3.77 us
    another operation x2, local copies, waits for them, and re-layouts, per_device(): halo_cols = jnp.stack([halo_west, halo_east], axis=-1)  3.57 us
  transfers between devices with their start and end apart: 11, of which 3 were waited for; matrix products, arithmetic and copies ran while one was open for 31% of the time, Pallas kernels for 0%

profile of v1, /device:TPU:4, one launch (start us, length us, event | category | flops | bytes accessed | tf_op | source)
XLA Modules:
  0.0 92.6 jit_solution(6174296502266594146)
XLA Ops:
  0.6 0.0 copy-start
  0.6 1.2 %convert_bitcast_fusion = (f32[1,32,256]{2,0,1:T(1,128)S(1)}, f32[1,32,256]{2,0,1:T(1,128)S(1)}) fusion(s32[32,32,256]{2,1,0:T(8,128)} %wet_ref.1), kind=kLoop, calls=%fused_computation.26 | loop fusion | flops 16384 | bytes 131072 | tf_op jit(solution)/shard_map/convert_element_type | solution.py:372
  1.8 1.3 %slice_bitcast_fusion.3 = (f32[1,32,256]{2,0,1:T(1,128)S(1)}, f32[1,32,256]{2,0,1:T(1,128)S(1)}, f32[1,32,256]{2,0,1:T(1,128)S(1)}, f32[1,32,256]{2,0,1:T(1,128)S(1)}) fusion(f32[32,32,256]{2,1,0:T(8,128)} %s_ref.1, f32[32,32,256]{2,1,0:T(8,128)} %t_ref.1), kind=kLoop, calls=%fused_computation.27 | loop fusion | bytes 262144 | tf_op jit(solution)/shard_map/stack;squeeze | solution.py:372
  3.1 1.3 %slice_bitcast_fusion.5 = (f32[1,32,256]{2,0,1:T(1,128)S(1)}, f32[1,32,256]{2,0,1:T(1,128)S(1)}, f32[1,32,256]{2,0,1:T(1,128)S(1)}, f32[1,32,256]{2,0,1:T(1,128)S(1)}) fusion(f32[32,32,256]{2,1,0:T(8,128)} %v_ref.1, f32[32,32,256]{2,1,0:T(8,128)} %u_ref.1), kind=kLoop, calls=%fused_computation.29 | loop fusion | bytes 262144 | tf_op jit(solution)/shard_map/stack;squeeze | solution.py:372
  4.4 0.2 stack.52
  4.7 0.0 copy-start.1
  4.7 1.5 %collective-permute-start.1 = (f32[5,32,256]{2,0,1:T(8,128)S(1)}, f32[5,32,256]{2,0,1:T(8,128)}, u32[]{:S(2)}, u32[]{:S(2)}) collective-permute-start(f32[5,32,256]{2,0,1:T(8,128)S(1)} %stack.52), channel_id=1, source_target_pairs={{15,255},{31,239},{47,223},{63,207},{79,191},{95,175},{111,159},{1... | collective-permute-start | bytes 491528 | tf_op jit(solution)/shard_map/ppermute | solution.py:175
  6.2 0.7 fusion.14
  6.9 0.7 collective-permute-start
  7.6 0.9 %stack.53 = f32[5,32,256]{2,0,1:T(8,128)} concatenate(f32[1,32,256]{2,0,1:T(1,128)S(1)} %get-tuple-element.33, f32[1,32,256]{2,0,1:T(1,128)S(1)} %get-tuple-element.20, f32[1,32,256]{2,0,1:T(1,128)S(1)} %get-tuple-element.31, f32[1,32,256]{2,0,1:T(1,128)S(1)} %get-tuple-element.16, f32[1,32,256]{2,0,1:T(1,128)S(1)} %get-tuple-element.14), dimensions={0} | concatenate | bytes 327680 | tf_op jit(solution)/shard_map/stack | solution.py:372
  8.5 7.8 %collective-permute-start.4 = (f32[5,32,256]{2,0,1:T(8,128)}, f32[5,32,256]{2,0,1:T(8,128)}, u32[]{:S(2)}, u32[]{:S(2)}) collective-permute-start(f32[5,32,256]{2,0,1:T(8,128)} %stack.53), channel_id=1, source_target_pairs={{1,0},{17,16},{33,32},{49,48},{65,64},{81,80},{97,96},{113,112},{1... | collective-permute-start | bytes 491528 | tf_op jit(solution)/shard_map/ppermute | solution.py:175
  16.4 1.0 %fusion.12 = (f32[32,32,1]{2,1,0:T(8,128)}, f32[32,32,1]{2,1,0:T(8,128)S(1)}) fusion(f32[32,32,256]{2,1,0:T(8,128)S(1)} %copy-done), kind=kLoop, calls=%fused_computation.44 | loop fusion | bytes 16384 | tf_op jit(solution)/shard_map/slice | solution.py:377
  17.4 0.2 fusion.11
  17.6 0.0 copy-start.4
  17.6 1.0 %fusion.10 = (f32[32,32,1]{2,1,0:T(8,128)}, f32[32,32,1]{2,1,0:T(8,128)S(1)}) fusion(f32[32,32,256]{2,1,0:T(8,128)S(1)} %copy-done.2), kind=kLoop, calls=%fused_computation.42 | loop fusion | bytes 16384 | tf_op jit(solution)/shard_map/slice | solution.py:377
  18.7 1.0 %fusion.9 = (f32[32,32,1]{2,1,0:T(8,128)}, f32[32,32,1]{2,1,0:T(8,128)S(1)}) fusion(f32[32,32,256]{2,1,0:T(8,128)S(1)} %copy-done.3), kind=kLoop, calls=%fused_computation.41 | loop fusion | bytes 16384 | tf_op jit(solution)/shard_map/slice | solution.py:377
  19.7 1.0 %fusion.8 = (s32[32,32,1]{2,1,0:T(8,128)}, s32[32,32,1]{2,1,0:T(8,128)S(1)}) fusion(s32[32,32,256]{2,1,0:T(8,128)S(1)} %copy-done.4), kind=kLoop, calls=%fused_computation.40 | loop fusion | bytes 16384 | tf_op jit(solution)/shard_map/slice | solution.py:377
  20.7 1.3 %copy.62 = f32[32,32,1]{1,0,2:T(8,128)S(1)} copy(f32[32,32,1]{2,1,0:T(8,128)} %get-tuple-element.12) | data formatting | bytes 8192
  22.0 0.6 constant_dynamic-update-slice_fusion.4
  22.6 0.2 copy.63
  22.8 1.3 %copy.64 = f32[32,32,1]{1,0,2:T(8,128)S(1)} copy(f32[32,32,1]{2,1,0:T(8,128)} %get-tuple-element.8) | data formatting | bytes 8192
  24.2 1.3 %copy.65 = f32[32,32,1]{1,0,2:T(8,128)S(1)} copy(f32[32,32,1]{2,1,0:T(8,128)} %get-tuple-element.6) | data formatting | bytes 8192
  25.5 1.3 %copy.66 = s32[32,32,1]{1,0,2:T(8,128)S(1)} copy(s32[32,32,1]{2,1,0:T(8,128)} %get-tuple-element.4) | data formatting | bytes 8192
  26.8 0.1 collective-permute-start.9
  26.9 0.2 copy.67
  27.2 0.6 constant_dynamic-update-slice_fusion.9
  27.8 0.2 copy.68
  28.0 0.3 copy.69
  28.3 0.3 copy.70
  28.6 0.3 copy.71
  28.8 0.6 constant_dynamic-update-slice_fusion.8
  29.5 0.6 constant_dynamic-update-slice_fusion.7
  30.1 0.6 constant_dynamic-update-slice_fusion.6
  30.7 0.6 constant_dynamic-update-slice_fusion.5
  31.3 3.8 %collective-permute-start.10 = (f32[5,32,32]{2,1,0:T(8,128)}, f32[5,32,32]{2,1,0:T(8,128)S(1)}, u32[]{:S(2)}, u32[]{:S(2)}) collective-permute-start(f32[5,32,32]{2,1,0:T(8,128)} %constant_dynamic-update-slice_fusion.5), channel_id=1, source_target_pairs={{0,240},{16,0},{32,16},{48,32},{64,48},{80,64},{96,80},{112,96},{1... | collective-permute-start | bytes 61448 | tf_op jit(solution)/shard_map/ppermute | solution.py:175
  35.1 1.7 %fusion.13 = (f32[5,32,1]{2,0,1:T(8,128)}, f32[5,32,1]{2,0,1:T(8,128)}) fusion(f32[5,32,256]{2,0,1:T(8,128)} %stack.53), kind=kLoop, calls=%fused_computation.45 | loop fusion | bytes 2560 | tf_op jit(solution)/shard_map/slice | solution.py:418
  36.9 0.0 collective-permute-done.9
  36.9 0.7 collective-permute-start.2
  37.6 1.0 %copy.60 = f32[5,32,32,1]{3,2,1,0:T(8,128)S(1)} copy(f32[5,32,32,1]{2,1,0,3:T(8,128)S(1)} %bitcast.68) | data formatting | bytes 40960 | tf_op jit(solution)/shard_map/stack | solution.py:442
  38.6 0.0 collective-permute-done.10
  38.6 1.9 %collective-permute-start.3 = (f32[5,32,1]{2,0,1:T(8,128)}, f32[5,32,1]{2,0,1:T(8,128)S(1)}, u32[]{:S(2)}, u32[]{:S(2)}) collective-permute-start(f32[5,32,1]{2,0,1:T(8,128)} %get-tuple-element.24), channel_id=1, source_target_pairs={{1,16},{17,32},{33,48},{49,64},{65,80},{81,96},{97,112},{113,128},... | collective-permute-start | bytes 1928 | tf_op jit(solution)/shard_map/ppermute | solution.py:175
  40.5 2.6 %copy.61 = f32[5,32,32,1]{3,2,1,0:T(8,128)} copy(f32[5,32,32,1]{2,1,0,3:T(8,128)S(1)} %bitcast.69) | data formatting | bytes 40960 | tf_op jit(solution)/shard_map/stack | solution.py:442
  43.1 0.0 collective-permute-done.1
  43.1 5.9 %collective-permute-start.5 = (f32[5,32,1]{2,0,1:T(8,128)}, f32[5,32,1]{2,0,1:T(8,128)S(1)}, u32[]{:S(2)}, u32[]{:S(2)}) collective-permute-start(f32[5,32,1]{2,0,1:T(8,128)} %get-tuple-element.25), channel_id=1, source_target_pairs={{1,240},{17,0},{33,16},{49,32},{65,48},{81,64},{97,80},{113,96},{1... | collective-permute-start | bytes 1928 | tf_op jit(solution)/shard_map/ppermute | solution.py:175
  48.9 4.0 %pad_maximum_fusion.cols_ref = f32[5,32,32,2]{3,2,1,0:T(8,128)} fusion(f32[5,32,32,1]{3,2,1,0:T(8,128)} %copy.61, f32[5,32,32,1]{3,2,1,0:T(8,128)S(1)} %copy.60), kind=kLoop, calls=%fused_computation | loop fusion | flops 10240 | bytes 81920 | tf_op jit(solution)/shard_map/stack | solution.py:442
  52.9 1.1 %rev.3 = f32[5,32,256]{2,0,1:T(8,128)S(1)} reverse(f32[5,32,256]{2,0,1:T(8,128)} %collective-permute-done.1), dimensions={2} | reverse | bytes 327680 | tf_op jit(solution)/shard_map/rev | solution.py:425
  54.1 0.0 collective-permute-done
  54.1 3.5 %collective-permute-start.6 = (f32[5,32,256]{2,0,1:T(8,128)S(1)}, f32[5,32,256]{2,0,1:T(8,128)S(1)}, u32[]{:S(2)}, u32[]{:S(2)}) collective-permute-start(f32[5,32,256]{2,0,1:T(8,128)S(1)} %stack.52), channel_id=1, source_target_pairs={{0,1},{16,17},{32,33},{48,49},{64,65},{80,81},{96,97},{112,113},{1... | collective-permute-start | bytes 491528 | tf_op jit(solution)/shard_map/ppermute | solution.py:175
  57.6 0.0 collective-permute-done.2
  57.6 2.1 %collective-permute-start.7 = (f32[5,32,1]{2,0,1:T(8,128)}, f32[5,32,1]{2,0,1:T(8,128)S(1)}, u32[]{:S(2)}, u32[]{:S(2)}) collective-permute-start(f32[5,32,1]{2,0,1:T(8,128)} %get-tuple-element.26), channel_id=1, source_target_pairs={{0,241},{16,1},{32,17},{48,33},{64,49},{80,65},{96,81},{112,97},{1... | collective-permute-start | bytes 1928 | tf_op jit(solution)/shard_map/ppermute | solution.py:175
  59.7 0.0 collective-permute-done.3
  59.7 2.8 %collective-permute-start.8 = (f32[5,32,1]{2,0,1:T(8,128)}, f32[5,32,1]{2,0,1:T(8,128)S(1)}, u32[]{:S(2)}, u32[]{:S(2)}) collective-permute-start(f32[5,32,1]{2,0,1:T(8,128)} %get-tuple-element.27), channel_id=1, source_target_pairs={{0,17},{16,33},{32,49},{48,65},{64,81},{80,97},{96,113},{112,129},... | collective-permute-start | bytes 1928 | tf_op jit(solution)/shard_map/ppermute | solution.py:175
  62.5 0.0 collective-permute-done.5
  62.6 1.3 %fusion = f32[5,32,258]{2,0,1:T(8,128)S(1)} fusion(f32[5,32,1]{2,0,1:T(8,128)S(1)} %collective-permute-done.2, f32[5,32,256]{2,0,1:T(8,128)S(1)} %rev.3, f32[5,32,1]{2,0,1:T(8,128)S(1)} %collective-permute-done, f32[5,32,1]{2,0,1:T(8,128)S(1)} %collective-permute-done.5, f32[5,32,256]{2,0,1:T(8,128)} %collective-permute-done.4, ...), kind=kLoop, calls=%fused_computation.2 | loop fusion | flops 247680 | bytes 495381 | tf_op jit(solution)/shard_map/jit(_where)/select_n | solution.py:428
  63.9 0.1 fusion.7
  64.0 0.1 fusion.6
  64.1 2.4 %collective-permute-done.6 = f32[5,32,256]{2,0,1:T(8,128)S(1)} collective-permute-done((f32[5,32,256]{2,0,1:T(8,128)S(1)}, f32[5,32,256]{2,0,1:T(8,128)S(1)}, u32[]{:S(2)}, u32[]{:S(2)}) %collective-permute-start.6) | collective-permute-done | bytes 163872 | tf_op jit(solution)/shard_map/ppermute | solution.py:175
  66.6 2.6 %collective-permute-done.7 = f32[5,32,1]{2,0,1:T(8,128)S(1)} collective-permute-done((f32[5,32,1]{2,0,1:T(8,128)}, f32[5,32,1]{2,0,1:T(8,128)S(1)}, u32[]{:S(2)}, u32[]{:S(2)}) %collective-permute-start.7) | collective-permute-done | bytes 672 | tf_op jit(solution)/shard_map/ppermute | solution.py:175
  69.2 0.2 fusion.4
  69.4 3.4 %collective-permute-done.8 = f32[5,32,1]{2,0,1:T(8,128)S(1)} collective-permute-done((f32[5,32,1]{2,0,1:T(8,128)}, f32[5,32,1]{2,0,1:T(8,128)S(1)}, u32[]{:S(2)}, u32[]{:S(2)}) %collective-permute-start.8) | collective-permute-done | bytes 672 | tf_op jit(solution)/shard_map/ppermute | solution.py:175
  72.8 0.1 fusion.2
  73.0 1.3 %copy.49 = f32[6,5,32,256]{3,2,1,0:T(8,128)} copy(f32[6,5,32,256]{3,1,2,0:T(8,128)S(1)} %fusion.2) | data formatting | bytes 1966080 | tf_op jit(solution)/shard_map/stack | solution.py:431
  74.2 0.7 broadcast_in_dim.10.cor_ref
  74.9 17.7 %shard_map.102 = (f32[32,32,256]{2,1,0:T(8,128)}, f32[32,32,256]{2,1,0:T(8,128)}, f32[32,32,256]{2,1,0:T(8,128)}, f32[32,32,256]{2,1,0:T(8,128)}) custom-call(f32[2,32,256]{2,1,0:T(8,128)} %broadcast_in_dim.10.cor_ref, f32[32,32,256]{2,1,0:T(8,128)} %u_ref.1, f32[32,32,256]{2,1,0:T(8,128)} %v_ref.1, f32[32,32,256]{2,1,0:T(8,128)} %t_ref.1, ...), custom_call_target="tpu_custom_call" | custom-call | tf_op jit(solution)/shard_map/pallas_call | solution.py:453
  (22 shorter events, 0.1 us)
Async XLA Ops:
  0.6 15.8 %copy-start = (f32[32,32,256]{2,1,0:T(8,128)S(1)}, f32[32,32,256]{2,1,0:T(8,128)}, u32[]{:S(2)}) copy-start(f32[32,32,256]{2,1,0:T(8,128)} %u_ref.1) | copy-start | bytes 3145732
  4.7 12.7 %copy-start.1 = (f32[32,32,256]{2,1,0:T(8,128)S(1)}, f32[32,32,256]{2,1,0:T(8,128)}, u32[]{:S(2)}) copy-start(f32[32,32,256]{2,1,0:T(8,128)} %v_ref.1) | copy-start | bytes 3145732
  4.7 38.4 %collective-permute-start.1 = (f32[5,32,256]{2,0,1:T(8,128)S(1)}, f32[5,32,256]{2,0,1:T(8,128)}, u32[]{:S(2)}, u32[]{:S(2)}) collective-permute-start(f32[5,32,256]{2,0,1:T(8,128)S(1)} %stack.52), channel_id=1, source_target_pairs={{15,255},{31,239},{47,223},{63,207},{79,191},{95,175},{111,159},{1... | collective-permute-start | bytes 491528 | tf_op jit(solution)/shard_map/ppermute | solution.py:175
  6.9 47.1 %collective-permute-start = (f32[5,32,1]{2,0,1:T(8,128)}, f32[5,32,1]{2,0,1:T(8,128)S(1)}, u32[]{:S(2)}, u32[]{:S(2)}) collective-permute-start(f32[5,32,1]{2,0,1:T(8,128)} %get-tuple-element.26), channel_id=1, source_target_pairs={{15,15},{31,255},{47,239},{63,223},{79,207},{95,191},{111,175},{12... | collective-permute-start | bytes 1928 | tf_op jit(solution)/shard_map/ppermute | solution.py:175
  8.5 9.1 %copy-start.2 = (f32[32,32,256]{2,1,0:T(8,128)S(1)}, f32[32,32,256]{2,1,0:T(8,128)}, u32[]{:S(2)}) copy-start(f32[32,32,256]{2,1,0:T(8,128)} %t_ref.1) | copy-start | bytes 3145732
  8.5 54.0 %collective-permute-start.4 = (f32[5,32,256]{2,0,1:T(8,128)}, f32[5,32,256]{2,0,1:T(8,128)}, u32[]{:S(2)}, u32[]{:S(2)}) collective-permute-start(f32[5,32,256]{2,0,1:T(8,128)} %stack.53), channel_id=1, source_target_pairs={{1,0},{17,16},{33,32},{49,48},{65,64},{81,80},{97,96},{113,112},{1... | collective-permute-start | bytes 491528 | tf_op jit(solution)/shard_map/ppermute | solution.py:175
  17.4 1.3 %copy-start.3 = (f32[32,32,256]{2,1,0:T(8,128)S(1)}, f32[32,32,256]{2,1,0:T(8,128)}, u32[]{:S(2)}) copy-start(f32[32,32,256]{2,1,0:T(8,128)} %s_ref.1) | copy-start | bytes 3145732
  17.6 2.0 %copy-start.4 = (s32[32,32,256]{2,1,0:T(8,128)S(1)}, s32[32,32,256]{2,1,0:T(8,128)}, u32[]{:S(2)}) copy-start(s32[32,32,256]{2,1,0:T(8,128)} %wet_ref.1) | copy-start | bytes 3145732
  22.8 3.9 %copy-start.6 = (f32[5,32,32]{2,1,0:T(8,128)S(1)}, f32[5,32,32]{2,1,0:T(8,128)}, u32[]{:S(2)}) copy-start(f32[5,32,32]{2,1,0:T(8,128)} %constant_dynamic-update-slice_fusion.4) | copy-start | bytes 61444
  26.8 10.0 %collective-permute-start.9 = (f32[5,32,32]{2,1,0:T(8,128)S(1)}, f32[5,32,32]{2,1,0:T(8,128)S(1)}, u32[]{:S(2)}, u32[]{:S(2)}) collective-permute-start(f32[5,32,32]{2,1,0:T(8,128)S(1)} %constant_dynamic-update-slice_fusion), channel_id=1, source_target_pairs={{0,16},{16,32},{32,48},{48,64},{64,80},{80,96},{96,112},{112,128},... | collective-permute-start | bytes 61448 | tf_op jit(solution)/shard_map/ppermute | solution.py:175
  27.2 9.7 %copy-start.5 = (f32[5,32,1]{2,0,1:T(8,128)S(1)}, f32[5,32,1]{2,0,1:T(8,128)}, u32[]{:S(2)}) copy-start(f32[5,32,1]{2,0,1:T(8,128)} %get-tuple-element.27) | copy-start | bytes 1924
  31.3 7.3 %collective-permute-start.10 = (f32[5,32,32]{2,1,0:T(8,128)}, f32[5,32,32]{2,1,0:T(8,128)S(1)}, u32[]{:S(2)}, u32[]{:S(2)}) collective-permute-start(f32[5,32,32]{2,1,0:T(8,128)} %constant_dynamic-update-slice_fusion.5), channel_id=1, source_target_pairs={{0,240},{16,0},{32,16},{48,32},{64,48},{80,64},{96,80},{112,96},{1... | collective-permute-start | bytes 61448 | tf_op jit(solution)/shard_map/ppermute | solution.py:175
  36.9 20.7 %collective-permute-start.2 = (f32[5,32,1]{2,0,1:T(8,128)S(1)}, f32[5,32,1]{2,0,1:T(8,128)S(1)}, u32[]{:S(2)}, u32[]{:S(2)}) collective-permute-start(f32[5,32,1]{2,0,1:T(8,128)S(1)} %copy-done.5), channel_id=1, source_target_pairs={{15,239},{31,223},{47,207},{63,191},{79,175},{95,159},{111,143},{1... | collective-permute-start | bytes 1928 | tf_op jit(solution)/shard_map/ppermute | solution.py:175
  38.6 21.1 %collective-permute-start.3 = (f32[5,32,1]{2,0,1:T(8,128)}, f32[5,32,1]{2,0,1:T(8,128)S(1)}, u32[]{:S(2)}, u32[]{:S(2)}) collective-permute-start(f32[5,32,1]{2,0,1:T(8,128)} %get-tuple-element.24), channel_id=1, source_target_pairs={{1,16},{17,32},{33,48},{49,64},{65,80},{81,96},{97,112},{113,128},... | collective-permute-start | bytes 1928 | tf_op jit(solution)/shard_map/ppermute | solution.py:175
  43.1 19.5 %copy-start.7 = (f32[5]{0:T(128)S(1)}, f32[5]{0:T(128)}, u32[]{:S(2)}) copy-start(f32[5]{0:T(128)} %constant.24.clone) | copy-start | bytes 64
  43.1 19.4 %collective-permute-start.5 = (f32[5,32,1]{2,0,1:T(8,128)}, f32[5,32,1]{2,0,1:T(8,128)S(1)}, u32[]{:S(2)}, u32[]{:S(2)}) collective-permute-start(f32[5,32,1]{2,0,1:T(8,128)} %get-tuple-element.25), channel_id=1, source_target_pairs={{1,240},{17,0},{33,16},{49,32},{65,48},{81,64},{97,80},{113,96},{1... | collective-permute-start | bytes 1928 | tf_op jit(solution)/shard_map/ppermute | solution.py:175
  54.1 12.5 %collective-permute-start.6 = (f32[5,32,256]{2,0,1:T(8,128)S(1)}, f32[5,32,256]{2,0,1:T(8,128)S(1)}, u32[]{:S(2)}, u32[]{:S(2)}) collective-permute-start(f32[5,32,256]{2,0,1:T(8,128)S(1)} %stack.52), channel_id=1, source_target_pairs={{0,1},{16,17},{32,33},{48,49},{64,65},{80,81},{96,97},{112,113},{1... | collective-permute-start | bytes 491528 | tf_op jit(solution)/shard_map/ppermute | solution.py:175
  57.6 11.6 %collective-permute-start.7 = (f32[5,32,1]{2,0,1:T(8,128)}, f32[5,32,1]{2,0,1:T(8,128)S(1)}, u32[]{:S(2)}, u32[]{:S(2)}) collective-permute-start(f32[5,32,1]{2,0,1:T(8,128)} %get-tuple-element.26), channel_id=1, source_target_pairs={{0,241},{16,1},{32,17},{48,33},{64,49},{80,65},{96,81},{112,97},{1... | collective-permute-start | bytes 1928 | tf_op jit(solution)/shard_map/ppermute | solution.py:175
  59.7 13.1 %collective-permute-start.8 = (f32[5,32,1]{2,0,1:T(8,128)}, f32[5,32,1]{2,0,1:T(8,128)S(1)}, u32[]{:S(2)}, u32[]{:S(2)}) collective-permute-start(f32[5,32,1]{2,0,1:T(8,128)} %get-tuple-element.27), channel_id=1, source_target_pairs={{0,17},{16,33},{32,49},{48,65},{64,81},{80,97},{96,113},{112,129},... | collective-permute-start | bytes 1928 | tf_op jit(solution)/shard_map/ppermute | solution.py:175

commit v2 on v1

--- a/solution.py
+++ b/solution.py
@@ -388,45 +388,27 @@
     def south_of(a, b, na, nl):
         return (a - 1, b) if a > 0 else None
 
-    def north_east(a, b, na, nl):
-        return (a + 1, (b + 1) % nl) if a + 1 < na else None
-
-    def north_west(a, b, na, nl):
-        return (a + 1, (b - 1) % nl) if a + 1 < na else None
-
-    def south_east(a, b, na, nl):
-        return (a - 1, (b + 1) % nl) if a > 0 else None
-
-    def south_west(a, b, na, nl):
-        return (a - 1, (b - 1) % nl) if a > 0 else None
-
     def mirror(a, b, na, nl):
         return (a, nl - 1 - b) if a == na - 1 else None
 
-    def mirror_left(a, b, na, nl):
-        return (a, (nl - b) % nl) if a == na - 1 else None
-
-    def mirror_right(a, b, na, nl):
-        return (a, (nl - 2 - b) % nl) if a == na - 1 else None
-
-    halo_west = shift(east_col, east_of)
-    halo_east = shift(west_col, west_of)
     halo_south = shift(top, north_of)
     halo_north = shift(bottom, south_of)
-    corner_sw = shift(top[:, :, -1:], north_east)
-    corner_se = shift(top[:, :, :1], north_west)
-    corner_nw = shift(bottom[:, :, -1:], south_east)
-    corner_ne = shift(bottom[:, :, :1], south_west)
     fold_row = shift(top, mirror)
-    fold_left = shift(top[:, :, :1], mirror_left)
-    fold_right = shift(top[:, :, -1:], mirror_right)
-
     sign = jnp.array([-1.0, -1.0, 1.0, 1.0, 1.0], dtype=jnp.float32)[:, None, None]
-    ghost = sign * jnp.concatenate([fold_left, fold_row[:, :, ::-1], fold_right], axis=2)
-    north_row = jnp.concatenate([corner_nw, halo_north, corner_ne], axis=2)
     is_top = lax.axis_index("lat") == lax.axis_size("lat") - 1
-    north_row = jnp.where(is_top, ghost, north_row)
-    south_row = jnp.concatenate([corner_sw, halo_south, corner_se], axis=2)
+    halo_north = jnp.where(is_top, sign * fold_row[:, :, ::-1], halo_north)
+    west_tall = jnp.concatenate(
+        [halo_south[:, :, None, 0], west_col, halo_north[:, :, None, 0]], axis=2
+    )
+    east_tall = jnp.concatenate(
+        [halo_south[:, :, None, -1], east_col, halo_north[:, :, None, -1]], axis=2
+    )
+    halo_west = shift(east_tall, east_of)
+    halo_east = shift(west_tall, west_of)
+    north_row = jnp.concatenate(
+        [halo_west[:, :, -1:], halo_north, halo_east[:, :, -1:]], axis=2
+    )
+    south_row = jnp.concatenate([halo_west[:, :, :1], halo_south, halo_east[:, :, :1]], axis=2)
     width = top.shape[2]
     halo_rows = jnp.stack(
         [
@@ -439,7 +421,7 @@
         ]
     )
     halo_rows = halo_rows.reshape((-1,) + halo_rows.shape[2:])
-    halo_cols = jnp.stack([halo_west, halo_east], axis=-1)
+    halo_cols = jnp.stack([halo_west[:, :, 1:-1], halo_east[:, :, 1:-1]], axis=-1)
 
     levels, rows, cols = eastbound_current.shape
     row_start = lax.axis_index("lat") * rows

time: 93.2 us -> 75.8 us (0.81)
  starting transfers between devices: 30.8 us -> 14.9 us
  waiting for transfers between devices: 8.51 us -> 1.94 us
  local copies, waits for them, and re-layouts: 27.3 us -> 30.4 us
  other arithmetic: 7.39 us -> 9.39 us
    ppermute x11 -> x5, starting transfers between devices: 30.8 us -> 14.9 us  [shift(): return lax.ppermute(value, ('lon', 'lat'), pairs)]
    ppermute x11 -> x5, waiting for transfers between devices: 8.51 us -> 1.94 us  [shift(): return lax.ppermute(value, ('lon', 'lat'), pairs)]
    another operation x7 -> x4, local copies, waits for them, and re-layouts: 8.61 us -> 3.74 us  [per_device(): jnp.stack([halo_west[:, :, 1:-1], halo_east[:, :, 1:-1]], axis=-1)]
    unnamed x38, local copies, waits for them, and re-layouts: 10.2 us -> 13.7 us
    slice x2 -> x9, local copies, waits for them, and re-layouts: 2.48 us -> 5.91 us  [the longest x5 5.58 us: per_device(): top = edge(lambda f: f[:, -1, :])]
    unnamed x1 -> x4, other arithmetic: 0.16 us -> 3.16 us
    select_n x1 -> x0, other arithmetic: 1.29 us -> none  [per_device(): north_row = jnp.where(is_top, ghost, north_row)]
    convert_element_type x1 -> x0, other arithmetic: 1.17 us -> none  [edge(): return jnp.stack([pick(field).astype(jnp.float32) for field in inputs])]
  transfers between devices with their start and end apart: 11 -> 5, of which waited for: 3 -> 1; matrix products, arithmetic and copies ran while one was open for 31% -> 26% of each run, Pallas kernels for 0% -> 0%
where the time goes in v2:
time: 75.8 us; the launch traced here: 75.2 us
  local copies, waits for them, and re-layouts  30.4 us (40%)
  Pallas kernels  17.7 us (23%)
  starting transfers between devices  14.9 us (20%)
  other arithmetic  9.39 us (12%)
  waiting for transfers between devices  1.94 us (3%)
  between operations  0.9 us (1%)
    pallas_call x1, Pallas kernels, per_device(): pl.pallas_call(stencil_kernel, out_shape=(block, block, block, block))  17.7 us
    ppermute x5, starting transfers between devices, shift(): return lax.ppermute(value, ('lon', 'lat'), pairs)  14.9 us
    unnamed x38, local copies, waits for them, and re-layouts  13.7 us
    slice x5, local copies, waits for them, and re-layouts, per_device(): top = edge(lambda f: f[:, -1, :])  5.58 us
    slice x5, local copies, waits for them, and re-layouts, per_device(): east_col = edge(lambda f: f[:, :, -1])  5.33 us
    another operation x1, other arithmetic, per_device(): jnp.stack([halo_west[:, :, 1:-1], halo_east[:, :, 1:-1]], axis=-1)  3.99 us
    another operation x4, local copies, waits for them, and re-layouts, per_device(): jnp.stack([halo_west[:, :, 1:-1], halo_east[:, :, 1:-1]], axis=-1)  3.74 us
    unnamed x4, other arithmetic  3.16 us
  transfers between devices with their start and end apart: 5, of which 1 were waited for; matrix products, arithmetic and copies ran while one was open for 26% of the time, Pallas kernels for 0%

profile of v2, /device:TPU:4, one launch (start us, length us, event | category | flops | bytes accessed | tf_op | source)
XLA Modules:
  0.0 75.2 jit_solution(17509625446163500099)
XLA Ops:
  0.6 0.0 copy-start
  0.6 1.2 %fusion.19 = (f32[32,1,256]{2,1,0:T(1,128)S(1)}, f32[32,1,256]{2,1,0:T(1,128)S(1)}) fusion(f32[32,32,256]{2,1,0:T(8,128)} %u_ref.1), kind=kLoop, calls=%fused_computation.65 | loop fusion | bytes 131072 | tf_op jit(solution)/shard_map/slice | solution.py:374
  1.8 1.1 %fusion.18 = (f32[32,1,256]{2,1,0:T(1,128)S(1)}, f32[32,1,256]{2,1,0:T(1,128)S(1)}) fusion(f32[32,32,256]{2,1,0:T(8,128)} %v_ref.1), kind=kLoop, calls=%fused_computation.64 | loop fusion | bytes 131072 | tf_op jit(solution)/shard_map/slice | solution.py:374
  2.9 0.0 copy-start.1
  2.9 1.2 %fusion.17 = (f32[32,1,256]{2,1,0:T(1,128)S(1)}, f32[32,1,256]{2,1,0:T(1,128)S(1)}) fusion(f32[32,32,256]{2,1,0:T(8,128)} %t_ref.1), kind=kLoop, calls=%fused_computation.63 | loop fusion | bytes 131072 | tf_op jit(solution)/shard_map/slice | solution.py:374
  4.1 1.1 %fusion.16 = (f32[32,1,256]{2,1,0:T(1,128)S(1)}, f32[32,1,256]{2,1,0:T(1,128)S(1)}) fusion(f32[32,32,256]{2,1,0:T(8,128)} %s_ref.1), kind=kLoop, calls=%fused_computation.62 | loop fusion | bytes 131072 | tf_op jit(solution)/shard_map/slice | solution.py:374
  5.2 1.1 %fusion.15 = (s32[32,1,256]{2,1,0:T(1,128)S(1)}, s32[32,1,256]{2,1,0:T(1,128)S(1)}) fusion(s32[32,32,256]{2,1,0:T(8,128)} %wet_ref.1), kind=kLoop, calls=%fused_computation.61 | loop fusion | bytes 131072 | tf_op jit(solution)/shard_map/slice | solution.py:374
  6.3 0.6 constant_dynamic-update-slice_fusion.4
  6.9 0.6 constant_dynamic-update-slice_fusion.3
  7.5 0.6 constant_dynamic-update-slice_fusion.2
  8.1 0.6 constant_dynamic-update-slice_fusion.1
  8.7 0.6 constant_dynamic-update-slice_fusion
  9.3 1.3 %collective-permute-start = (f32[5,32,256]{2,1,0:T(8,128)}, f32[5,32,256]{2,1,0:T(8,128)}, u32[]{:S(2)}, u32[]{:S(2)}) collective-permute-start(f32[5,32,256]{2,1,0:T(8,128)} %constant_dynamic-update-slice_fusion), channel_id=1, source_target_pairs={{15,255},{31,239},{47,223},{63,207},{79,191},{95,175},{111,159},{1... | collective-permute-start | bytes 491528 | tf_op jit(solution)/shard_map/ppermute | solution.py:175
  10.6 3.8 %collective-permute-start.2 = (f32[5,32,256]{2,1,0:T(8,128)}, f32[5,32,256]{2,1,0:T(8,128)S(1)}, u32[]{:S(2)}, u32[]{:S(2)}) collective-permute-start(f32[5,32,256]{2,1,0:T(8,128)} %constant_dynamic-update-slice_fusion), channel_id=1, source_target_pairs={{0,1},{16,17},{32,33},{48,49},{64,65},{80,81},{96,97},{112,113},{1... | collective-permute-start | bytes 491528 | tf_op jit(solution)/shard_map/ppermute | solution.py:175
  14.4 0.6 constant_dynamic-update-slice_fusion.8
  15.0 0.6 constant_dynamic-update-slice_fusion.7
  15.6 0.6 constant_dynamic-update-slice_fusion.6
  16.2 0.6 constant_dynamic-update-slice_fusion.5
  16.8 5.8 %collective-permute-start.1 = (f32[5,32,256]{2,1,0:T(8,128)}, f32[5,32,256]{2,1,0:T(8,128)S(1)}, u32[]{:S(2)}, u32[]{:S(2)}) collective-permute-start(f32[5,32,256]{2,1,0:T(8,128)} %constant_dynamic-update-slice_fusion.5), channel_id=1, source_target_pairs={{1,0},{17,16},{33,32},{49,48},{65,64},{81,80},{97,96},{113,112},{1... | collective-permute-start | bytes 491528 | tf_op jit(solution)/shard_map/ppermute | solution.py:175
  22.6 0.0 copy-start.2
  22.7 2.2 %fusion.14 = (f32[32,32,1]{2,1,0:T(8,128)S(1)}, f32[32,32,1]{2,1,0:T(8,128)}) fusion(f32[32,32,256]{2,1,0:T(8,128)} %u_ref.1), kind=kLoop, calls=%fused_computation.60 | loop fusion | bytes 16384 | tf_op jit(solution)/shard_map/slice | solution.py:377
  24.9 0.2 fusion.13
  25.1 0.0 copy-done.1
  25.1 1.0 %fusion.12 = (f32[32,32,1]{2,1,0:T(8,128)S(1)}, f32[32,32,1]{2,1,0:T(8,128)}) fusion(f32[32,32,256]{2,1,0:T(8,128)S(1)} %copy-done.1), kind=kLoop, calls=%fused_computation.58 | loop fusion | bytes 16384 | tf_op jit(solution)/shard_map/slice | solution.py:377
  26.1 1.0 %fusion.11 = (f32[32,32,1]{2,1,0:T(8,128)S(1)}, f32[32,32,1]{2,1,0:T(8,128)}) fusion(f32[32,32,256]{2,1,0:T(8,128)S(1)} %copy-done.2), kind=kLoop, calls=%fused_computation.57 | loop fusion | bytes 16384 | tf_op jit(solution)/shard_map/slice | solution.py:377
  27.1 1.0 %fusion.10 = (s32[32,32,1]{2,1,0:T(8,128)S(1)}, s32[32,32,1]{2,1,0:T(8,128)}) fusion(s32[32,32,256]{2,1,0:T(8,128)S(1)} %copy-done.3), kind=kLoop, calls=%fused_computation.56 | loop fusion | bytes 16384 | tf_op jit(solution)/shard_map/slice | solution.py:377
  28.0 1.9 %copy.130 = f32[32,32,1]{1,0,2:T(8,128)} copy(f32[32,32,1]{2,1,0:T(8,128)} %get-tuple-element.15) | data formatting | bytes 8192
  29.9 0.7 constant_dynamic-update-slice_fusion.14
  30.6 0.9 %copy.131 = f32[32,32,1]{1,0,2:T(8,128)} copy(f32[32,32,1]{2,1,0:T(8,128)S(1)} %get-tuple-element.13) | data formatting | bytes 8192
  31.5 1.3 %copy.132 = f32[32,32,1]{1,0,2:T(8,128)S(1)} copy(f32[32,32,1]{2,1,0:T(8,128)} %get-tuple-element.11) | data formatting | bytes 8192
  32.8 1.3 %copy.133 = f32[32,32,1]{1,0,2:T(8,128)S(1)} copy(f32[32,32,1]{2,1,0:T(8,128)} %get-tuple-element.9) | data formatting | bytes 8192
  34.1 1.3 %copy.134 = s32[32,32,1]{1,0,2:T(8,128)S(1)} copy(s32[32,32,1]{2,1,0:T(8,128)} %get-tuple-element.7) | data formatting | bytes 8192
  35.4 0.3 copy.135
  35.7 0.3 copy.136
  35.9 0.3 copy.137
  36.2 0.3 copy.138
  36.5 0.3 copy.139
  36.9 0.0 collective-permute-done
  36.9 1.1 %rev.3 = f32[5,32,256]{2,1,0:T(8,128)S(1)} reverse(f32[5,32,256]{2,1,0:T(8,128)} %collective-permute-done), dimensions={2} | reverse | bytes 327680 | tf_op jit(solution)/shard_map/rev | solution.py:399
  38.0 0.0 collective-permute-done.1
  38.0 0.8 %bitcast_dynamic-update-slice_fusion.1 = (f32[6,5,32,256]{3,2,1,0:T(8,128)}, f32[5,32,256]{2,1,0:T(8,128)S(1)}) fusion(f32[5,32,256]{2,1,0:T(8,128)S(1)} %collective-permute-done.1, f32[5,32,256]{2,1,0:T(8,128)S(1)} %rev.3, f32[5]{0:T(128)S(1)} %copy-done.5, pred[]{:T(512)S(6)} %eq.3), kind=kLoop, calls=%fused_computation.14 | loop fusion | flops 81919 | bytes 655381
  38.7 0.1 fusion.21
  38.8 0.0 collective-permute-done.2
  38.8 0.1 fusion.20
  38.9 0.1 pad_maximum_fusion.6
  39.0 0.1 collective-permute-start.4
  39.1 0.1 pad_maximum_fusion.5
  39.2 3.9 %collective-permute-start.3 = (f32[5,32,34]{2,1,0:T(8,128)S(1)}, f32[5,32,34]{2,1,0:T(8,128)S(1)}, u32[]{:S(2)}, u32[]{:S(2)}) collective-permute-start(f32[5,32,34]{2,1,0:T(8,128)S(1)} %pad_maximum_fusion.5), channel_id=1, source_target_pairs={{0,240},{16,0},{32,16},{48,32},{64,48},{80,64},{96,80},{112,96},{1... | collective-permute-start | bytes 65288 | tf_op jit(solution)/shard_map/ppermute | solution.py:175
  43.2 1.9 %collective-permute-done.4 = f32[5,32,34]{2,1,0:T(8,128)S(1)} collective-permute-done((f32[5,32,34]{2,1,0:T(8,128)S(1)}, f32[5,32,34]{2,1,0:T(8,128)S(1)}, u32[]{:S(2)}, u32[]{:S(2)}) %collective-permute-start.4) | collective-permute-done | bytes 21792 | tf_op jit(solution)/shard_map/ppermute | solution.py:175
  45.1 0.1 slice_bitcast_fusion.1
  45.2 1.0 %copy.118 = f32[5,32,32,1]{3,2,1,0:T(8,128)S(1)} copy(f32[5,32,32,1]{2,1,0,3:T(8,128)S(1)} %slice_bitcast_fusion.1) | data formatting | bytes 40960 | tf_op jit(solution)/shard_map/stack | solution.py:424
  46.2 0.0 collective-permute-done.3
  46.2 0.1 slice_bitcast_fusion
  46.3 2.6 %copy.119 = f32[5,32,32,1]{3,2,1,0:T(8,128)} copy(f32[5,32,32,1]{2,1,0,3:T(8,128)S(1)} %slice_bitcast_fusion) | data formatting | bytes 40960 | tf_op jit(solution)/shard_map/stack | solution.py:424
  48.9 0.1 fusion.23
  48.9 0.8 %fusion.7 = f32[6,5,32,256]{3,2,1,0:T(8,128)} fusion(f32[6,5,32,256]{3,2,1,0:T(8,128)} %get-tuple-element.4, f32[5,32,1]{2,1,0:T(8,128)S(1)} %get-tuple-element.33, f32[5,32,256]{2,1,0:T(8,128)S(1)} %get-tuple-element.5), kind=kLoop, calls=%fused_computation.12 | loop fusion | flops 40960 | bytes 328320
  49.8 0.1 fusion.22
  49.8 0.8 %fusion.5 = f32[6,5,32,256]{3,2,1,0:T(8,128)} fusion(f32[6,5,32,256]{3,2,1,0:T(8,128)} %fusion.7, f32[5,32,256]{2,1,0:T(8,128)S(1)} %get-tuple-element.5, f32[5,32,1]{2,1,0:T(8,128)S(1)} %get-tuple-element.31), kind=kLoop, calls=%fused_computation.9 | loop fusion | flops 40960 | bytes 328320
  50.6 4.0 %pad_maximum_fusion.cols_ref = f32[5,32,32,2]{3,2,1,0:T(8,128)} fusion(f32[5,32,32,1]{3,2,1,0:T(8,128)} %copy.119, f32[5,32,32,1]{3,2,1,0:T(8,128)S(1)} %copy.118), kind=kLoop, calls=%fused_computation | loop fusion | flops 10240 | bytes 81920 | tf_op jit(solution)/shard_map/stack | solution.py:424
  54.6 0.7 bitcast_dynamic-update-slice_fusion
  55.3 0.8 %fusion.3 = f32[6,5,32,256]{3,2,1,0:T(8,128)} fusion(f32[6,5,32,256]{3,2,1,0:T(8,128)} %bitcast_dynamic-update-slice_fusion, f32[5,32,1]{2,1,0:T(8,128)S(1)} %get-tuple-element.32, f32[5,32,256]{2,1,0:T(8,128)S(1)} %collective-permute-done.2), kind=kLoop, calls=%fused_computation.6 | loop fusion | flops 40960 | bytes 328320
  56.1 0.8 %fusion.1 = f32[6,5,32,256]{3,2,1,0:T(8,128)} fusion(f32[6,5,32,256]{3,2,1,0:T(8,128)} %fusion.3, f32[5,32,256]{2,1,0:T(8,128)S(1)} %collective-permute-done.2, f32[5,32,1]{2,1,0:T(8,128)S(1)} %get-tuple-element.30), kind=kLoop, calls=%fused_computation.3 | loop fusion | flops 40960 | bytes 328320 | tf_op jit(solution)/shard_map/stack | solution.py:413
  56.9 0.7 broadcast_in_dim.10.cor_ref
  57.6 17.7 %shard_map.102 = (f32[32,32,256]{2,1,0:T(8,128)}, f32[32,32,256]{2,1,0:T(8,128)}, f32[32,32,256]{2,1,0:T(8,128)}, f32[32,32,256]{2,1,0:T(8,128)}) custom-call(f32[2,32,256]{2,1,0:T(8,128)} %broadcast_in_dim.10.cor_ref, f32[32,32,256]{2,1,0:T(8,128)} %u_ref.1, f32[32,32,256]{2,1,0:T(8,128)} %v_ref.1, f32[32,32,256]{2,1,0:T(8,128)} %t_ref.1, ...), custom_call_target="tpu_custom_call" | custom-call | tf_op jit(solution)/shard_map/pallas_call | solution.py:435
  (19 shorter events, 0.1 us)
Async XLA Ops:
  0.6 24.3 %copy-start = (f32[32,32,256]{2,1,0:T(8,128)S(1)}, f32[32,32,256]{2,1,0:T(8,128)}, u32[]{:S(2)}) copy-start(f32[32,32,256]{2,1,0:T(8,128)} %v_ref.1) | copy-start | bytes 3145732
  2.9 22.2 %copy-start.1 = (f32[32,32,256]{2,1,0:T(8,128)S(1)}, f32[32,32,256]{2,1,0:T(8,128)}, u32[]{:S(2)}) copy-start(f32[32,32,256]{2,1,0:T(8,128)} %t_ref.1) | copy-start | bytes 3145732
  9.3 27.6 %collective-permute-start = (f32[5,32,256]{2,1,0:T(8,128)}, f32[5,32,256]{2,1,0:T(8,128)}, u32[]{:S(2)}, u32[]{:S(2)}) collective-permute-start(f32[5,32,256]{2,1,0:T(8,128)} %constant_dynamic-update-slice_fusion), channel_id=1, source_target_pairs={{15,255},{31,239},{47,223},{63,207},{79,191},{95,175},{111,159},{1... | collective-permute-start | bytes 491528 | tf_op jit(solution)/shard_map/ppermute | solution.py:175
  10.6 28.2 %collective-permute-start.2 = (f32[5,32,256]{2,1,0:T(8,128)}, f32[5,32,256]{2,1,0:T(8,128)S(1)}, u32[]{:S(2)}, u32[]{:S(2)}) collective-permute-start(f32[5,32,256]{2,1,0:T(8,128)} %constant_dynamic-update-slice_fusion), channel_id=1, source_target_pairs={{0,1},{16,17},{32,33},{48,49},{64,65},{80,81},{96,97},{112,113},{1... | collective-permute-start | bytes 491528 | tf_op jit(solution)/shard_map/ppermute | solution.py:175
  16.8 21.1 %collective-permute-start.1 = (f32[5,32,256]{2,1,0:T(8,128)}, f32[5,32,256]{2,1,0:T(8,128)S(1)}, u32[]{:S(2)}, u32[]{:S(2)}) collective-permute-start(f32[5,32,256]{2,1,0:T(8,128)} %constant_dynamic-update-slice_fusion.5), channel_id=1, source_target_pairs={{1,0},{17,16},{33,32},{49,48},{65,64},{81,80},{97,96},{113,112},{1... | collective-permute-start | bytes 491528 | tf_op jit(solution)/shard_map/ppermute | solution.py:175
  22.6 3.4 %copy-start.2 = (f32[32,32,256]{2,1,0:T(8,128)S(1)}, f32[32,32,256]{2,1,0:T(8,128)}, u32[]{:S(2)}) copy-start(f32[32,32,256]{2,1,0:T(8,128)} %s_ref.1) | copy-start | bytes 3145732
  24.9 2.2 %copy-start.3 = (s32[32,32,256]{2,1,0:T(8,128)S(1)}, s32[32,32,256]{2,1,0:T(8,128)}, u32[]{:S(2)}) copy-start(s32[32,32,256]{2,1,0:T(8,128)} %wet_ref.1) | copy-start | bytes 3145732
  31.5 5.2 %copy-start.4 = (f32[32,32,1]{1,0,2:T(8,128)S(1)}, f32[32,32,1]{1,0,2:T(8,128)}, u32[]{:S(2)}) copy-start(f32[32,32,1]{1,0,2:T(8,128)} %copy.131) | copy-start | bytes 12292
  31.5 6.5 %copy-start.5 = (f32[5]{0:T(128)S(1)}, f32[5]{0:T(128)}, u32[]{:S(2)}) copy-start(f32[5]{0:T(128)} %constant.24.clone) | copy-start | bytes 64
  39.0 6.1 %collective-permute-start.4 = (f32[5,32,34]{2,1,0:T(8,128)S(1)}, f32[5,32,34]{2,1,0:T(8,128)S(1)}, u32[]{:S(2)}, u32[]{:S(2)}) collective-permute-start(f32[5,32,34]{2,1,0:T(8,128)S(1)} %pad_maximum_fusion.6), channel_id=1, source_target_pairs={{0,16},{16,32},{32,48},{48,64},{64,80},{80,96},{96,112},{112,128},... | collective-permute-start | bytes 65288 | tf_op jit(solution)/shard_map/ppermute | solution.py:175
  39.2 6.9 %collective-permute-start.3 = (f32[5,32,34]{2,1,0:T(8,128)S(1)}, f32[5,32,34]{2,1,0:T(8,128)S(1)}, u32[]{:S(2)}, u32[]{:S(2)}) collective-permute-start(f32[5,32,34]{2,1,0:T(8,128)S(1)} %pad_maximum_fusion.5), channel_id=1, source_target_pairs={{0,240},{16,0},{32,16},{48,32},{64,48},{80,64},{96,80},{112,96},{1... | collective-permute-start | bytes 65288 | tf_op jit(solution)/shard_map/ppermute | solution.py:175

commit v3 on v2

--- a/solution.py
+++ b/solution.py
@@ -175,8 +175,31 @@
     return lax.ppermute(value, ("lon", "lat"), pairs)
 
 
+def edge_kernel(*refs):
+    fields = len(refs) - 4
+    sources = refs[:fields]
+    top_ref, bottom_ref, west_ref, east_ref = refs[fields:]
+    levels, rows, cols = sources[0].shape
+    lane = lax.broadcasted_iota(jnp.int32, (rows, levels), 1)
+    for field, source in enumerate(sources):
+
+        def body(k, carry):
+            west, east = carry
+            x = source[k].astype(jnp.float32)
+            top_ref[field, pl.ds(k, 1), :] = x[rows - 1 : rows, :]
+            bottom_ref[field, pl.ds(k, 1), :] = x[0:1, :]
+            west = jnp.where(lane == k, x[:, 0:1], west)
+            east = jnp.where(lane == k, x[:, cols - 1 : cols], east)
+            return west, east
+
+        zero = jnp.zeros((rows, levels), jnp.float32)
+        west, east = lax.fori_loop(0, levels, body, (zero, zero))
+        west_ref[field] = west
+        east_ref[field] = east
+
+
 def stencil_kernel(
-    cor_ref, u_ref, v_ref, t_ref, s_ref, wet_ref, clc_ref, rows_ref, cols_ref,
+    cor_ref, u_ref, v_ref, t_ref, s_ref, wet_ref, clc_ref, rn_ref, rs_ref, tw_ref, te_ref,
     east_ref, north_ref, temp_ref, salt_ref,
 ):
     levels, rows, cols = u_ref.shape
@@ -187,6 +210,10 @@
     at_west = lane == 0
     at_north = sub == rows - 1
     at_south = sub == 0
+    row_lane = lax.broadcasted_iota(jnp.int32, (1, cols), 1)
+    row_east = row_lane == cols - 1
+    row_west = row_lane == 0
+    pick = lax.broadcasted_iota(jnp.int32, (levels, cols), 0)
     cor_t = cor_ref[0]
     cor_v = cor_ref[1]
     count = clc_ref[...]
@@ -208,12 +235,37 @@
         km = jnp.maximum(k - 1, 0)
         kp = jnp.minimum(k + 1, levels - 1)
 
+        onehot = (pick == k).astype(jnp.float32)
+        spread = {}
+
+        def tall(field):
+            if field not in spread:
+                spread[field] = tuple(
+                    jnp.dot(
+                        ref[field],
+                        onehot,
+                        precision=lax.Precision.HIGHEST,
+                        preferred_element_type=jnp.float32,
+                    )
+                    for ref in (tw_ref, te_ref)
+                )
+            return spread[field]
+
         def row(variant, field):
-            return rows_ref[variant * fields + field, pl.ds(k, 1), :]
+            west_t, east_t = tall(field)
+            if variant == 0:
+                return rn_ref[field, pl.ds(k, 1), :]
+            if variant == 3:
+                return rs_ref[field, pl.ds(k, 1), :]
+            if variant == 1:
+                return jnp.where(row_east, east_t[rows + 1 : rows + 2], pltpu.roll(row(0, field), cols - 1, 1))
+            if variant == 2:
+                return jnp.where(row_west, west_t[rows + 1 : rows + 2], pltpu.roll(row(0, field), 1, 1))
+            return jnp.where(row_east, east_t[rows : rows + 1], pltpu.roll(row(3, field), cols - 1, 1))
 
         def col(field):
-            pair = cols_ref[field, k]
-            return pair[:, 0:1], pair[:, 1:2]
+            west_t, east_t = tall(field)
+            return west_t[0:rows], east_t[0:rows]
 
         w = wet_ref[k].astype(jnp.float32)
         w_above = wet_ref[km].astype(jnp.float32)
@@ -346,7 +398,7 @@
 
     init = (
         jnp.zeros((rows, cols), jnp.float32),
-        jnp.zeros((rows, 1), jnp.float32),
+        jnp.zeros((rows, cols), jnp.float32),
         jnp.zeros((1, cols), jnp.float32),
     )
     lax.fori_loop(0, levels, body, init)
@@ -368,13 +420,17 @@
         water_indicator,
     )
 
-    def edge(pick):
-        return jnp.stack([pick(field).astype(jnp.float32) for field in inputs])
-
-    top = edge(lambda f: f[:, -1, :])
-    bottom = edge(lambda f: f[:, 0, :])
-    west_col = edge(lambda f: f[:, :, 0])
-    east_col = edge(lambda f: f[:, :, -1])
+    levels, rows, cols = eastbound_current.shape
+    fields = len(inputs)
+    top, bottom, west_col, east_col = pl.pallas_call(
+        edge_kernel,
+        out_shape=(
+            jax.ShapeDtypeStruct((fields, levels, cols), jnp.float32),
+            jax.ShapeDtypeStruct((fields, levels, cols), jnp.float32),
+            jax.ShapeDtypeStruct((fields, rows, levels), jnp.float32),
+            jax.ShapeDtypeStruct((fields, rows, levels), jnp.float32),
+        ),
+    )(*inputs)
 
     def east_of(a, b, na, nl):
         return (a, (b + 1) % nl)
@@ -397,33 +453,16 @@
     sign = jnp.array([-1.0, -1.0, 1.0, 1.0, 1.0], dtype=jnp.float32)[:, None, None]
     is_top = lax.axis_index("lat") == lax.axis_size("lat") - 1
     halo_north = jnp.where(is_top, sign * fold_row[:, :, ::-1], halo_north)
+    pad = jnp.zeros((fields, 6, levels), jnp.float32)
     west_tall = jnp.concatenate(
-        [halo_south[:, :, None, 0], west_col, halo_north[:, :, None, 0]], axis=2
+        [west_col, halo_south[:, None, :, 0], halo_north[:, None, :, 0], pad], axis=1
     )
     east_tall = jnp.concatenate(
-        [halo_south[:, :, None, -1], east_col, halo_north[:, :, None, -1]], axis=2
+        [east_col, halo_south[:, None, :, -1], halo_north[:, None, :, -1], pad], axis=1
     )
     halo_west = shift(east_tall, east_of)
     halo_east = shift(west_tall, west_of)
-    north_row = jnp.concatenate(
-        [halo_west[:, :, -1:], halo_north, halo_east[:, :, -1:]], axis=2
-    )
-    south_row = jnp.concatenate([halo_west[:, :, :1], halo_south, halo_east[:, :, :1]], axis=2)
-    width = top.shape[2]
-    halo_rows = jnp.stack(
-        [
-            north_row[:, :, 1 : width + 1],
-            north_row[:, :, 2 : width + 2],
-            north_row[:, :, 0:width],
-            south_row[:, :, 1 : width + 1],
-            south_row[:, :, 2 : width + 2],
-            south_row[:, :, 0:width],
-        ]
-    )
-    halo_rows = halo_rows.reshape((-1,) + halo_rows.shape[2:])
-    halo_cols = jnp.stack([halo_west[:, :, 1:-1], halo_east[:, :, 1:-1]], axis=-1)
-
-    levels, rows, cols = eastbound_current.shape
+
     row_start = lax.axis_index("lat") * rows
     total_rows = rows * lax.axis_size("lat")
     row_index = (row_start + jnp.arange(rows, dtype=jnp.int32)).astype(jnp.float32)[:, None]
@@ -443,8 +482,10 @@
         saltiness_excess,
         water_indicator,
         column_layer_count,
-        halo_rows,
-        halo_cols,
+        halo_north,
+        halo_south,
+        halo_west,
+        halo_east,
     )
 
 

time: 75.8 us -> 65.5 us (0.86)
  the two profiles are of different devices: /device:TPU:4 before, /device:TPU:228 now
where the time goes in v3:
time: 65.5 us; the launch traced here: 65.4 us
  Pallas kernels  36.9 us (56%)
  starting transfers between devices  11.9 us (18%)
  waiting for transfers between devices  11.1 us (17%)
  local copies, waits for them, and re-layouts  4.44 us (7%)
  between operations  0.74 us (1%)
    pallas_call x1, Pallas kernels, per_device(): pl.pallas_call(stencil_kernel, out_shape=(block, block, block, block))  21.3 us
    pallas_call x1, Pallas kernels, per_device(): pl.pallas_call(edge_kernel, out_shape=(jax.ShapeDtypeStruct((fields, leve...  15.6 us
    ppermute x5, starting transfers between devices, shift(): return lax.ppermute(value, ('lon', 'lat'), pairs)  11.9 us
    ppermute x5, waiting for transfers between devices, shift(): return lax.ppermute(value, ('lon', 'lat'), pairs)  11.1 us
    unnamed x14, local copies, waits for them, and re-layouts  1.95 us
  transfers between devices with their start and end apart: 5, of which 4 were waited for; matrix products, arithmetic and copies ran while one was open for 3% of the time, Pallas kernels for 0%

profile of v3, /device:TPU:228, one launch (start us, length us, event | category | flops | bytes accessed | tf_op | source)
XLA Modules:
  0.0 65.4 jit_solution(11883613340889352645)
XLA Ops:
  0.6 15.6 %shard_map.102 = (f32[5,32,256]{2,1,0:T(8,128)}, f32[5,32,256]{2,1,0:T(8,128)}, f32[5,32,32]{2,1,0:T(8,128)}, f32[5,32,32]{2,1,0:T(8,128)}) custom-call(f32[32,32,256]{2,1,0:T(8,128)} %u_ref.1, f32[32,32,256]{2,1,0:T(8,128)} %v_ref.1, f32[32,32,256]{2,1,0:T(8,128)} %t_ref.1, f32[32,32,256]{2,1,0:T(8,128)} %s_ref.1, s32[32,32,256]{2,1,0:T(8,128)} %wet_ref.1), custom_call_target="tpu_custom_call" | custom-call | tf_op jit(solution)/shard_map/pallas_call | solution.py:425
  16.2 1.3 %collective-permute-start.2 = (f32[5,32,256]{2,1,0:T(8,128)}, f32[5,32,256]{2,1,0:T(8,128)S(1)}, u32[]{:S(2)}, u32[]{:S(2)}) collective-permute-start(f32[5,32,256]{2,1,0:T(8,128)} %get-tuple-element.8), channel_id=1, source_target_pairs={{0,1},{16,17},{32,33},{48,49},{64,65},{80,81},{96,97},{112,113},{1... | collective-permute-start | bytes 491528 | tf_op jit(solution)/shard_map/ppermute | solution.py:175
  17.5 5.0 %collective-permute-start = (f32[5,32,256]{2,1,0:T(8,128)}, f32[5,32,256]{2,1,0:T(8,128)S(1)}, u32[]{:S(2)}, u32[]{:S(2)}) collective-permute-start(f32[5,32,256]{2,1,0:T(8,128)} %get-tuple-element.8), channel_id=1, source_target_pairs={{15,255},{31,239},{47,223},{63,207},{79,191},{95,175},{111,159},{1... | collective-permute-start | bytes 491528 | tf_op jit(solution)/shard_map/ppermute | solution.py:175
  22.5 1.3 %collective-permute-start.1 = (f32[5,32,256]{2,1,0:T(8,128)}, f32[5,32,256]{2,1,0:T(8,128)S(1)}, u32[]{:S(2)}, u32[]{:S(2)}) collective-permute-start(f32[5,32,256]{2,1,0:T(8,128)} %get-tuple-element.9), channel_id=1, source_target_pairs={{1,0},{17,16},{33,32},{49,48},{65,64},{81,80},{97,96},{113,112},{1... | collective-permute-start | bytes 491528 | tf_op jit(solution)/shard_map/ppermute | solution.py:175
  23.9 0.1 pad.7.clone
  23.9 0.3 collective-permute-done.2.rs_ref
  24.3 0.0 copy-start
  24.3 0.1 fusion
  24.4 0.6 copy-done
  24.9 0.1 copy.22
  25.0 0.1 copy.21
  25.1 5.5 %collective-permute-done = f32[5,32,256]{2,1,0:T(8,128)S(1)} collective-permute-done((f32[5,32,256]{2,1,0:T(8,128)}, f32[5,32,256]{2,1,0:T(8,128)S(1)}, u32[]{:S(2)}, u32[]{:S(2)}) %collective-permute-start) | collective-permute-done | bytes 163872 | tf_op jit(solution)/shard_map/ppermute | solution.py:175
  30.6 0.2 copy.16
  30.9 0.3 rev.3
  31.2 0.0 copy-start.5
  31.2 0.0 collective-permute-done.1
  31.2 0.2 copy.17
  31.4 0.4 copy-done.5
  31.8 0.0 copy-start.3
  31.8 0.0 copy-start.4
  31.8 0.1 multiply_select_fusion
  32.0 0.7 %copy-done.3 = f32[5,32,32]{2,1,0:T(8,128)S(1)} copy-done((f32[5,32,32]{2,1,0:T(8,128)S(1)}, f32[5,32,32]{2,1,0:T(8,128)}, u32[]{:S(2)}) %copy-start.3) | copy-done | bytes 20504
  32.7 0.0 copy-done.4
  32.8 0.1 maximum_maximum_fusion.1
  32.8 4.3 %collective-permute-start.4 = (f32[5,40,32]{2,1,0:T(8,128)S(1)}, f32[5,40,32]{2,1,0:T(8,128)S(1)}, u32[]{:S(2)}, u32[]{:S(2)}) collective-permute-start(f32[5,40,32]{2,1,0:T(8,128)S(1)} %get-tuple-element.16), channel_id=1, source_target_pairs={{0,240},{16,0},{32,16},{48,32},{64,48},{80,64},{96,80},{112,96},{1... | collective-permute-start | bytes 76808 | tf_op jit(solution)/shard_map/ppermute | solution.py:175
  37.1 0.0 collective-permute-start.3
  37.1 0.9 %copy.20.rn_ref = f32[5,32,256]{2,1,0:T(8,128)} copy(f32[5,32,256]{1,2,0:T(8,128)S(1)} %multiply_select_fusion) | data formatting | bytes 327680 | tf_op jit(solution)/shard_map/jit(_where)/select_n | solution.py:455
  38.0 1.4 %collective-permute-done.4.te_ref = f32[5,40,32]{2,1,0:T(8,128)S(1)} collective-permute-done((f32[5,40,32]{2,1,0:T(8,128)S(1)}, f32[5,40,32]{2,1,0:T(8,128)S(1)}, u32[]{:S(2)}, u32[]{:S(2)}) %collective-permute-start.4) | collective-permute-done | bytes 25632 | tf_op jit(solution)/shard_map/ppermute | solution.py:175
  39.4 0.0 copy-start.1
  39.4 3.9 %collective-permute-done.3.tw_ref = f32[5,40,32]{2,1,0:T(8,128)S(1)} collective-permute-done((f32[5,40,32]{2,1,0:T(8,128)S(1)}, f32[5,40,32]{2,1,0:T(8,128)S(1)}, u32[]{:S(2)}, u32[]{:S(2)}) %collective-permute-start.3) | collective-permute-done | bytes 25632 | tf_op jit(solution)/shard_map/ppermute | solution.py:175
  43.3 0.0 copy-start.2
  43.3 0.7 %broadcast_in_dim.13.cor_ref = f32[2,32,256]{2,1,0:T(8,128)} broadcast(f32[2,32]{1,0:T(2,128)S(1)} %maximum_bitcast_fusion), dimensions={0,1} | broadcast | bytes 65792 | tf_op jit(solution)/shard_map/broadcast_in_dim | solution.py:471
  44.0 0.0 copy-done.1
  44.0 0.0 copy-done.2
  44.0 21.3 %shard_map.103 = (f32[32,32,256]{2,1,0:T(8,128)}, f32[32,32,256]{2,1,0:T(8,128)}, f32[32,32,256]{2,1,0:T(8,128)}, f32[32,32,256]{2,1,0:T(8,128)}) custom-call(f32[2,32,256]{2,1,0:T(8,128)} %broadcast_in_dim.13.cor_ref, f32[32,32,256]{2,1,0:T(8,128)} %u_ref.1, f32[32,32,256]{2,1,0:T(8,128)} %v_ref.1, f32[32,32,256]{2,1,0:T(8,128)} %t_ref.1, ...), custom_call_target="tpu_custom_call" | custom-call | tf_op jit(solution)/shard_map/pallas_call | solution.py:474
  (4 shorter events, 0.0 us)
Async XLA Ops:
  16.2 8.0 %collective-permute-start.2 = (f32[5,32,256]{2,1,0:T(8,128)}, f32[5,32,256]{2,1,0:T(8,128)S(1)}, u32[]{:S(2)}, u32[]{:S(2)}) collective-permute-start(f32[5,32,256]{2,1,0:T(8,128)} %get-tuple-element.8), channel_id=1, source_target_pairs={{0,1},{16,17},{32,33},{48,49},{64,65},{80,81},{96,97},{112,113},{1... | collective-permute-start | bytes 491528 | tf_op jit(solution)/shard_map/ppermute | solution.py:175
  17.5 13.1 %collective-permute-start = (f32[5,32,256]{2,1,0:T(8,128)}, f32[5,32,256]{2,1,0:T(8,128)S(1)}, u32[]{:S(2)}, u32[]{:S(2)}) collective-permute-start(f32[5,32,256]{2,1,0:T(8,128)} %get-tuple-element.8), channel_id=1, source_target_pairs={{15,255},{31,239},{47,223},{63,207},{79,191},{95,175},{111,159},{1... | collective-permute-start | bytes 491528 | tf_op jit(solution)/shard_map/ppermute | solution.py:175
  22.5 8.7 %collective-permute-start.1 = (f32[5,32,256]{2,1,0:T(8,128)}, f32[5,32,256]{2,1,0:T(8,128)S(1)}, u32[]{:S(2)}, u32[]{:S(2)}) collective-permute-start(f32[5,32,256]{2,1,0:T(8,128)} %get-tuple-element.9), channel_id=1, source_target_pairs={{1,0},{17,16},{33,32},{49,48},{65,64},{81,80},{97,96},{113,112},{1... | collective-permute-start | bytes 491528 | tf_op jit(solution)/shard_map/ppermute | solution.py:175
  24.3 0.7 %copy-start = (f32[5,32,256]{2,1,0:T(8,128)}, f32[5,32,256]{2,1,0:T(8,128)S(1)}, u32[]{:S(2)}) copy-start(f32[5,32,256]{2,1,0:T(8,128)S(1)} %collective-permute-done.2.rs_ref) | copy-start | bytes 491524
  31.2 0.7 %copy-start.5 = (f32[5]{0:T(128)S(1)}, f32[5]{0:T(128)}, u32[]{:S(2)}) copy-start(f32[5]{0:T(128)} %constant.26.clone) | copy-start | bytes 64
  31.8 0.9 %copy-start.3 = (f32[5,32,32]{2,1,0:T(8,128)S(1)}, f32[5,32,32]{2,1,0:T(8,128)}, u32[]{:S(2)}) copy-start(f32[5,32,32]{2,1,0:T(8,128)} %get-tuple-element.11) | copy-start | bytes 61444
  31.8 0.9 %copy-start.4 = (f32[5,32,32]{2,1,0:T(8,128)S(1)}, f32[5,32,32]{2,1,0:T(8,128)}, u32[]{:S(2)}) copy-start(f32[5,32,32]{2,1,0:T(8,128)} %get-tuple-element.10) | copy-start | bytes 61444
  32.8 6.5 %collective-permute-start.4 = (f32[5,40,32]{2,1,0:T(8,128)S(1)}, f32[5,40,32]{2,1,0:T(8,128)S(1)}, u32[]{:S(2)}, u32[]{:S(2)}) collective-permute-start(f32[5,40,32]{2,1,0:T(8,128)S(1)} %get-tuple-element.16), channel_id=1, source_target_pairs={{0,240},{16,0},{32,16},{48,32},{64,48},{80,64},{96,80},{112,96},{1... | collective-permute-start | bytes 76808 | tf_op jit(solution)/shard_map/ppermute | solution.py:175
  37.1 6.2 %collective-permute-start.3 = (f32[5,40,32]{2,1,0:T(8,128)S(1)}, f32[5,40,32]{2,1,0:T(8,128)S(1)}, u32[]{:S(2)}, u32[]{:S(2)}) collective-permute-start(f32[5,40,32]{2,1,0:T(8,128)S(1)} %get-tuple-element.17), channel_id=1, source_target_pairs={{0,16},{16,32},{32,48},{48,64},{64,80},{80,96},{96,112},{112,128},... | collective-permute-start | bytes 76808 | tf_op jit(solution)/shard_map/ppermute | solution.py:175
  39.4 4.6 %copy-start.1 = (f32[5,40,32]{2,1,0:T(8,128)}, f32[5,40,32]{2,1,0:T(8,128)S(1)}, u32[]{:S(2)}) copy-start(f32[5,40,32]{2,1,0:T(8,128)S(1)} %collective-permute-done.4.te_ref) | copy-start | bytes 76804
  43.3 0.7 %copy-start.2 = (f32[5,40,32]{2,1,0:T(8,128)}, f32[5,40,32]{2,1,0:T(8,128)S(1)}, u32[]{:S(2)}) copy-start(f32[5,40,32]{2,1,0:T(8,128)S(1)} %collective-permute-done.3.tw_ref) | copy-start | bytes 76804

commit v4 on v3

--- a/solution.py
+++ b/solution.py
@@ -179,21 +179,26 @@
     fields = len(refs) - 4
     sources = refs[:fields]
     top_ref, bottom_ref, west_ref, east_ref = refs[fields:]
-    levels, rows, cols = sources[0].shape
+    chunk, rows, cols = sources[0].shape
+    levels = west_ref.shape[2]
+    step = pl.program_id(0)
     lane = lax.broadcasted_iota(jnp.int32, (rows, levels), 1)
+
+    @pl.when(step == 0)
+    def _():
+        west_ref[...] = jnp.zeros(west_ref.shape, jnp.float32)
+        east_ref[...] = jnp.zeros(east_ref.shape, jnp.float32)
+
     for field, source in enumerate(sources):
-
-        def body(k, carry):
-            west, east = carry
-            x = source[k].astype(jnp.float32)
-            top_ref[field, pl.ds(k, 1), :] = x[rows - 1 : rows, :]
-            bottom_ref[field, pl.ds(k, 1), :] = x[0:1, :]
-            west = jnp.where(lane == k, x[:, 0:1], west)
-            east = jnp.where(lane == k, x[:, cols - 1 : cols], east)
-            return west, east
-
-        zero = jnp.zeros((rows, levels), jnp.float32)
-        west, east = lax.fori_loop(0, levels, body, (zero, zero))
+        west = west_ref[field]
+        east = east_ref[field]
+        for r in range(chunk):
+            x = source[r].astype(jnp.float32)
+            top_ref[field, r : r + 1, :] = x[rows - 1 : rows, :]
+            bottom_ref[field, r : r + 1, :] = x[0:1, :]
+            here = lane == step * chunk + r
+            west = jnp.where(here, x[:, 0:1], west)
+            east = jnp.where(here, x[:, cols - 1 : cols], east)
         west_ref[field] = west
         east_ref[field] = east
 
@@ -422,8 +427,14 @@
 
     levels, rows, cols = eastbound_current.shape
     fields = len(inputs)
+    chunk = 8 if levels % 8 == 0 else levels
+    row_block = pl.BlockSpec((fields, chunk, cols), lambda c: (0, c, 0))
+    col_block = pl.BlockSpec((fields, rows, levels), lambda c: (0, 0, 0))
     top, bottom, west_col, east_col = pl.pallas_call(
         edge_kernel,
+        grid=(levels // chunk,),
+        in_specs=[pl.BlockSpec((chunk, rows, cols), lambda c: (c, 0, 0))] * fields,
+        out_specs=(row_block, row_block, col_block, col_block),
         out_shape=(
             jax.ShapeDtypeStruct((fields, levels, cols), jnp.float32),
             jax.ShapeDtypeStruct((fields, levels, cols), jnp.float32),

time: 65.5 us -> 55 us (0.84)
  Pallas kernels: 36.9 us -> 26.3 us
    pallas_call x1, Pallas kernels: 15.6 us -> 4.97 us  [per_device(): pl.pallas_call(edge_kernel, grid=(levels // chunk,), in_specs=[pl.BlockSp...]
where the time goes in v4:
time: 55 us; the launch traced here: 54.7 us
  Pallas kernels  26.3 us (48%)
  starting transfers between devices  11.9 us (22%)
  waiting for transfers between devices  11.1 us (20%)
  local copies, waits for them, and re-layouts  4.44 us (8%)
  between operations  0.74 us (1%)
    pallas_call x1, Pallas kernels, per_device(): pl.pallas_call(stencil_kernel, out_shape=(block, block, block, block))  21.3 us
    ppermute x5, starting transfers between devices, shift(): return lax.ppermute(value, ('lon', 'lat'), pairs)  11.9 us
    ppermute x5, waiting for transfers between devices, shift(): return lax.ppermute(value, ('lon', 'lat'), pairs)  11.1 us
    pallas_call x1, Pallas kernels, per_device(): pl.pallas_call(edge_kernel, grid=(levels // chunk,), in_specs=[pl.BlockSp...  4.97 us
    unnamed x14, local copies, waits for them, and re-layouts  1.95 us
  transfers between devices with their start and end apart: 5, of which 4 were waited for; matrix products, arithmetic and copies ran while one was open for 3% of the time, Pallas kernels for 0%

profile of v4, /device:TPU:228, one launch (start us, length us, event | category | flops | bytes accessed | tf_op | source)
XLA Modules:
  0.0 54.7 jit_solution(386016212294373126)
XLA Ops:
  0.6 5.0 %shard_map.102 = (f32[5,32,256]{2,1,0:T(8,128)}, f32[5,32,256]{2,1,0:T(8,128)}, f32[5,32,32]{2,1,0:T(8,128)}, f32[5,32,32]{2,1,0:T(8,128)}) custom-call(f32[32,32,256]{2,1,0:T(8,128)} %u_ref.1, f32[32,32,256]{2,1,0:T(8,128)} %v_ref.1, f32[32,32,256]{2,1,0:T(8,128)} %t_ref.1, f32[32,32,256]{2,1,0:T(8,128)} %s_ref.1, s32[32,32,256]{2,1,0:T(8,128)} %wet_ref.1), custom_call_target="tpu_custom_call" | custom-call | tf_op jit(solution)/shard_map/pallas_call | solution.py:433
  5.6 1.3 %collective-permute-start.2 = (f32[5,32,256]{2,1,0:T(8,128)}, f32[5,32,256]{2,1,0:T(8,128)S(1)}, u32[]{:S(2)}, u32[]{:S(2)}) collective-permute-start(f32[5,32,256]{2,1,0:T(8,128)} %get-tuple-element.8), channel_id=1, source_target_pairs={{0,1},{16,17},{32,33},{48,49},{64,65},{80,81},{96,97},{112,113},{1... | collective-permute-start | bytes 491528 | tf_op jit(solution)/shard_map/ppermute | solution.py:175
  6.9 5.0 %collective-permute-start = (f32[5,32,256]{2,1,0:T(8,128)}, f32[5,32,256]{2,1,0:T(8,128)S(1)}, u32[]{:S(2)}, u32[]{:S(2)}) collective-permute-start(f32[5,32,256]{2,1,0:T(8,128)} %get-tuple-element.8), channel_id=1, source_target_pairs={{15,255},{31,239},{47,223},{63,207},{79,191},{95,175},{111,159},{1... | collective-permute-start | bytes 491528 | tf_op jit(solution)/shard_map/ppermute | solution.py:175
  11.9 1.3 %collective-permute-start.1 = (f32[5,32,256]{2,1,0:T(8,128)}, f32[5,32,256]{2,1,0:T(8,128)S(1)}, u32[]{:S(2)}, u32[]{:S(2)}) collective-permute-start(f32[5,32,256]{2,1,0:T(8,128)} %get-tuple-element.9), channel_id=1, source_target_pairs={{1,0},{17,16},{33,32},{49,48},{65,64},{81,80},{97,96},{113,112},{1... | collective-permute-start | bytes 491528 | tf_op jit(solution)/shard_map/ppermute | solution.py:175
  13.2 0.1 pad.7.clone
  13.3 0.3 collective-permute-done.2.rs_ref
  13.6 0.0 copy-start
  13.6 0.1 fusion
  13.7 0.6 %copy-done = f32[5,32,256]{2,1,0:T(8,128)} copy-done((f32[5,32,256]{2,1,0:T(8,128)}, f32[5,32,256]{2,1,0:T(8,128)S(1)}, u32[]{:S(2)}) %copy-start) | copy-done | bytes 163864
  14.3 0.1 copy.22
  14.4 0.1 copy.21
  14.5 5.5 %collective-permute-done = f32[5,32,256]{2,1,0:T(8,128)S(1)} collective-permute-done((f32[5,32,256]{2,1,0:T(8,128)}, f32[5,32,256]{2,1,0:T(8,128)S(1)}, u32[]{:S(2)}, u32[]{:S(2)}) %collective-permute-start) | collective-permute-done | bytes 163872 | tf_op jit(solution)/shard_map/ppermute | solution.py:175
  20.0 0.2 copy.16
  20.2 0.3 rev.3
  20.5 0.0 copy-start.5
  20.6 0.0 collective-permute-done.1
  20.6 0.2 copy.17
  20.8 0.4 copy-done.5
  21.2 0.0 copy-start.3
  21.2 0.0 copy-start.4
  21.2 0.1 multiply_select_fusion
  21.4 0.7 %copy-done.3 = f32[5,32,32]{2,1,0:T(8,128)S(1)} copy-done((f32[5,32,32]{2,1,0:T(8,128)S(1)}, f32[5,32,32]{2,1,0:T(8,128)}, u32[]{:S(2)}) %copy-start.3) | copy-done | bytes 20504
  22.1 0.0 copy-done.4
  22.1 0.1 maximum_maximum_fusion.1
  22.2 4.3 %collective-permute-start.4 = (f32[5,40,32]{2,1,0:T(8,128)S(1)}, f32[5,40,32]{2,1,0:T(8,128)S(1)}, u32[]{:S(2)}, u32[]{:S(2)}) collective-permute-start(f32[5,40,32]{2,1,0:T(8,128)S(1)} %get-tuple-element.16), channel_id=1, source_target_pairs={{0,240},{16,0},{32,16},{48,32},{64,48},{80,64},{96,80},{112,96},{1... | collective-permute-start | bytes 76808 | tf_op jit(solution)/shard_map/ppermute | solution.py:175
  26.5 0.0 collective-permute-start.3
  26.5 0.9 %copy.20.rn_ref = f32[5,32,256]{2,1,0:T(8,128)} copy(f32[5,32,256]{1,2,0:T(8,128)S(1)} %multiply_select_fusion) | data formatting | bytes 327680 | tf_op jit(solution)/shard_map/jit(_where)/select_n | solution.py:466
  27.4 1.4 %collective-permute-done.4.te_ref = f32[5,40,32]{2,1,0:T(8,128)S(1)} collective-permute-done((f32[5,40,32]{2,1,0:T(8,128)S(1)}, f32[5,40,32]{2,1,0:T(8,128)S(1)}, u32[]{:S(2)}, u32[]{:S(2)}) %collective-permute-start.4) | collective-permute-done | bytes 25632 | tf_op jit(solution)/shard_map/ppermute | solution.py:175
  28.8 0.0 copy-start.1
  28.8 3.9 %collective-permute-done.3.tw_ref = f32[5,40,32]{2,1,0:T(8,128)S(1)} collective-permute-done((f32[5,40,32]{2,1,0:T(8,128)S(1)}, f32[5,40,32]{2,1,0:T(8,128)S(1)}, u32[]{:S(2)}, u32[]{:S(2)}) %collective-permute-start.3) | collective-permute-done | bytes 25632 | tf_op jit(solution)/shard_map/ppermute | solution.py:175
  32.7 0.0 copy-start.2
  32.7 0.7 %broadcast_in_dim.13.cor_ref = f32[2,32,256]{2,1,0:T(8,128)} broadcast(f32[2,32]{1,0:T(2,128)S(1)} %maximum_bitcast_fusion), dimensions={0,1} | broadcast | bytes 65792 | tf_op jit(solution)/shard_map/broadcast_in_dim | solution.py:482
  33.4 0.0 copy-done.1
  33.4 0.0 copy-done.2
  33.4 21.3 %shard_map.103 = (f32[32,32,256]{2,1,0:T(8,128)}, f32[32,32,256]{2,1,0:T(8,128)}, f32[32,32,256]{2,1,0:T(8,128)}, f32[32,32,256]{2,1,0:T(8,128)}) custom-call(f32[2,32,256]{2,1,0:T(8,128)} %broadcast_in_dim.13.cor_ref, f32[32,32,256]{2,1,0:T(8,128)} %u_ref.1, f32[32,32,256]{2,1,0:T(8,128)} %v_ref.1, f32[32,32,256]{2,1,0:T(8,128)} %t_ref.1, ...), custom_call_target="tpu_custom_call" | custom-call | tf_op jit(solution)/shard_map/pallas_call | solution.py:485
  (4 shorter events, 0.0 us)
Async XLA Ops:
  5.6 8.0 %collective-permute-start.2 = (f32[5,32,256]{2,1,0:T(8,128)}, f32[5,32,256]{2,1,0:T(8,128)S(1)}, u32[]{:S(2)}, u32[]{:S(2)}) collective-permute-start(f32[5,32,256]{2,1,0:T(8,128)} %get-tuple-element.8), channel_id=1, source_target_pairs={{0,1},{16,17},{32,33},{48,49},{64,65},{80,81},{96,97},{112,113},{1... | collective-permute-start | bytes 491528 | tf_op jit(solution)/shard_map/ppermute | solution.py:175
  6.9 13.1 %collective-permute-start = (f32[5,32,256]{2,1,0:T(8,128)}, f32[5,32,256]{2,1,0:T(8,128)S(1)}, u32[]{:S(2)}, u32[]{:S(2)}) collective-permute-start(f32[5,32,256]{2,1,0:T(8,128)} %get-tuple-element.8), channel_id=1, source_target_pairs={{15,255},{31,239},{47,223},{63,207},{79,191},{95,175},{111,159},{1... | collective-permute-start | bytes 491528 | tf_op jit(solution)/shard_map/ppermute | solution.py:175
  11.9 8.7 %collective-permute-start.1 = (f32[5,32,256]{2,1,0:T(8,128)}, f32[5,32,256]{2,1,0:T(8,128)S(1)}, u32[]{:S(2)}, u32[]{:S(2)}) collective-permute-start(f32[5,32,256]{2,1,0:T(8,128)} %get-tuple-element.9), channel_id=1, source_target_pairs={{1,0},{17,16},{33,32},{49,48},{65,64},{81,80},{97,96},{113,112},{1... | collective-permute-start | bytes 491528 | tf_op jit(solution)/shard_map/ppermute | solution.py:175
  13.6 0.7 %copy-start = (f32[5,32,256]{2,1,0:T(8,128)}, f32[5,32,256]{2,1,0:T(8,128)S(1)}, u32[]{:S(2)}) copy-start(f32[5,32,256]{2,1,0:T(8,128)S(1)} %collective-permute-done.2.rs_ref) | copy-start | bytes 491524
  20.5 0.7 %copy-start.5 = (f32[5]{0:T(128)S(1)}, f32[5]{0:T(128)}, u32[]{:S(2)}) copy-start(f32[5]{0:T(128)} %constant.26.clone) | copy-start | bytes 64
  21.2 0.9 %copy-start.3 = (f32[5,32,32]{2,1,0:T(8,128)S(1)}, f32[5,32,32]{2,1,0:T(8,128)}, u32[]{:S(2)}) copy-start(f32[5,32,32]{2,1,0:T(8,128)} %get-tuple-element.11) | copy-start | bytes 61444
  21.2 0.9 %copy-start.4 = (f32[5,32,32]{2,1,0:T(8,128)S(1)}, f32[5,32,32]{2,1,0:T(8,128)}, u32[]{:S(2)}) copy-start(f32[5,32,32]{2,1,0:T(8,128)} %get-tuple-element.10) | copy-start | bytes 61444
  22.2 6.5 %collective-permute-start.4 = (f32[5,40,32]{2,1,0:T(8,128)S(1)}, f32[5,40,32]{2,1,0:T(8,128)S(1)}, u32[]{:S(2)}, u32[]{:S(2)}) collective-permute-start(f32[5,40,32]{2,1,0:T(8,128)S(1)} %get-tuple-element.16), channel_id=1, source_target_pairs={{0,240},{16,0},{32,16},{48,32},{64,48},{80,64},{96,80},{112,96},{1... | collective-permute-start | bytes 76808 | tf_op jit(solution)/shard_map/ppermute | solution.py:175
  26.5 6.2 %collective-permute-start.3 = (f32[5,40,32]{2,1,0:T(8,128)S(1)}, f32[5,40,32]{2,1,0:T(8,128)S(1)}, u32[]{:S(2)}, u32[]{:S(2)}) collective-permute-start(f32[5,40,32]{2,1,0:T(8,128)S(1)} %get-tuple-element.17), channel_id=1, source_target_pairs={{0,16},{16,32},{32,48},{48,64},{64,80},{80,96},{96,112},{112,128},... | collective-permute-start | bytes 76808 | tf_op jit(solution)/shard_map/ppermute | solution.py:175
  28.8 4.6 %copy-start.1 = (f32[5,40,32]{2,1,0:T(8,128)}, f32[5,40,32]{2,1,0:T(8,128)S(1)}, u32[]{:S(2)}) copy-start(f32[5,40,32]{2,1,0:T(8,128)S(1)} %collective-permute-done.4.te_ref) | copy-start | bytes 76804
  32.7 0.7 %copy-start.2 = (f32[5,40,32]{2,1,0:T(8,128)}, f32[5,40,32]{2,1,0:T(8,128)S(1)}, u32[]{:S(2)}) copy-start(f32[5,40,32]{2,1,0:T(8,128)S(1)} %collective-permute-done.3.tw_ref) | copy-start | bytes 76804

commit v5 on v4

--- a/solution.py
+++ b/solution.py
@@ -204,10 +204,33 @@
 
 
 def stencil_kernel(
-    cor_ref, u_ref, v_ref, t_ref, s_ref, wet_ref, clc_ref, rn_ref, rs_ref, tw_ref, te_ref,
-    east_ref, north_ref, temp_ref, salt_ref,
+    cor_ref, u_ref, v_ref, t_ref, s_ref, wet_ref, ua_ref, va_ref, ta_ref, sa_ref, wa_ref,
+    ub_ref, vb_ref, tb_ref, sb_ref, wb_ref, clc_ref, rn_ref, rs_ref, tw_ref, te_ref,
+    east_ref, north_ref, temp_ref, salt_ref, p_ref, pe_ref, pn_ref,
 ):
-    levels, rows, cols = u_ref.shape
+    chunk, rows, cols = u_ref.shape
+    levels = tw_ref.shape[2]
+    step = pl.program_id(0)
+    near = {
+        id(u_ref): (ua_ref, ub_ref),
+        id(v_ref): (va_ref, vb_ref),
+        id(t_ref): (ta_ref, tb_ref),
+        id(s_ref): (sa_ref, sb_ref),
+        id(wet_ref): (wa_ref, wb_ref),
+    }
+
+    def level(ref, r, offset):
+        above, below = near[id(ref)]
+        if offset < 0:
+            return jnp.where(r == 0, above[0], ref[jnp.maximum(r - 1, 0)])
+        return jnp.where(r == chunk - 1, below[0], ref[jnp.minimum(r + 1, chunk - 1)])
+
+    @pl.when(step == 0)
+    def _():
+        p_ref[...] = jnp.zeros(p_ref.shape, jnp.float32)
+        pe_ref[...] = jnp.zeros(pe_ref.shape, jnp.float32)
+        pn_ref[...] = jnp.zeros(pn_ref.shape, jnp.float32)
+
     fields = 5
     lane = lax.broadcasted_iota(jnp.int32, (rows, cols), 1)
     sub = lax.broadcasted_iota(jnp.int32, (rows, cols), 0)
@@ -235,10 +258,9 @@
     def south(x, row):
         return jnp.where(at_south, row, pltpu.roll(x, 1, 0))
 
-    def body(k, carry):
+    def body(r, carry):
         pres, pres_e, pres_n = carry
-        km = jnp.maximum(k - 1, 0)
-        kp = jnp.minimum(k + 1, levels - 1)
+        k = step * chunk + r
 
         onehot = (pick == k).astype(jnp.float32)
         spread = {}
@@ -259,9 +281,9 @@
         def row(variant, field):
             west_t, east_t = tall(field)
             if variant == 0:
-                return rn_ref[field, pl.ds(k, 1), :]
+                return rn_ref[field, pl.ds(r, 1), :]
             if variant == 3:
-                return rs_ref[field, pl.ds(k, 1), :]
+                return rs_ref[field, pl.ds(r, 1), :]
             if variant == 1:
                 return jnp.where(row_east, east_t[rows + 1 : rows + 2], pltpu.roll(row(0, field), cols - 1, 1))
             if variant == 2:
@@ -272,9 +294,9 @@
             west_t, east_t = tall(field)
             return west_t[0:rows], east_t[0:rows]
 
-        w = wet_ref[k].astype(jnp.float32)
-        w_above = wet_ref[km].astype(jnp.float32)
-        w_below = wet_ref[kp].astype(jnp.float32)
+        w = wet_ref[r].astype(jnp.float32)
+        w_above = level(wet_ref, r, -1).astype(jnp.float32)
+        w_below = level(wet_ref, r, 1).astype(jnp.float32)
         w_wc, w_ec = col(4)
         w_e = east(w, w_ec)
         w_w = west(w, w_wc)
@@ -294,8 +316,8 @@
         bottom = (k == count - 1).astype(jnp.float32)
 
         def column(ref, centre):
-            upper = ref[km]
-            lower = ref[kp]
+            upper = level(ref, r, -1)
+            lower = level(ref, r, 1)
             above = -vertical_diff * mix_above * (centre - upper)
             below = -vertical_diff * mix_below * (lower - centre)
             return above - below
@@ -309,8 +331,8 @@
                 - cabbel_mixed * temper * saline
             )
 
-        tc = t_ref[k]
-        sc = s_ref[k]
+        tc = t_ref[r]
+        sc = s_ref[r]
         t_wc, t_ec = col(2)
         s_wc, s_ec = col(3)
         pres = pres + w * density(tc, sc)
@@ -319,14 +341,14 @@
         p_e = east(pres, pres_e)
         p_n = north(pres, pres_n)
 
-        uc = u_ref[k]
+        uc = u_ref[r]
         u_wc, u_ec = col(0)
         u_e = east(uc, u_ec)
         u_w = west(uc, u_wc)
         u_n = north(uc, row(0, 0))
         u_s = south(uc, row(3, 0))
         u_nw = north(u_w, row(2, 0))
-        vc = v_ref[k]
+        vc = v_ref[r]
         v_wc, v_ec = col(1)
         v_e = east(vc, v_ec)
         v_w = west(vc, v_wc)
@@ -356,8 +378,8 @@
             )
             return w * (centre + time_step * tendency)
 
-        temp_ref[k] = tracer(t_ref, tc, 2, t_wc, t_ec)
-        salt_ref[k] = tracer(s_ref, sc, 3, s_wc, s_ec)
+        temp_ref[r] = tracer(t_ref, tc, 2, t_wc, t_ec)
+        salt_ref[r] = tracer(s_ref, sc, 3, s_wc, s_ec)
 
         corner_ne = w * w_e * w_n * w_ne
         corner_se = w_s * w_se * w * w_e
@@ -381,7 +403,7 @@
             + column(u_ref, uc)
             - drag_coef * bottom * uc
         )
-        east_ref[k] = mask_east * (uc + time_step * east_tend)
+        east_ref[r] = mask_east * (uc + time_step * east_tend)
         half_n = (vc + v_n) * 0.5
         cell_north = w_n * (half_n * half_n - lateral_diff * (v_n - vc))
         half_s = (v_s + vc) * 0.5
@@ -398,15 +420,14 @@
             + column(v_ref, vc)
             - drag_coef * bottom * vc
         )
-        north_ref[k] = mask_north * (vc + time_step * north_tend)
+        north_ref[r] = mask_north * (vc + time_step * north_tend)
         return pres, pres_e, pres_n
 
-    init = (
-        jnp.zeros((rows, cols), jnp.float32),
-        jnp.zeros((rows, cols), jnp.float32),
-        jnp.zeros((1, cols), jnp.float32),
-    )
-    lax.fori_loop(0, levels, body, init)
+    init = (p_ref[...], pe_ref[...], pn_ref[...])
+    pres, pres_e, pres_n = lax.fori_loop(0, chunk, body, init)
+    p_ref[...] = pres
+    pe_ref[...] = pres_e
+    pn_ref[...] = pres_n
 
 
 def per_device(
@@ -482,16 +503,36 @@
     coriolis = jnp.broadcast_to(jnp.stack([coriolis_t, coriolis_v]), (2, rows, cols))
 
     block = jax.ShapeDtypeStruct((levels, rows, cols), jnp.float32)
+    main = pl.BlockSpec((chunk, rows, cols), lambda c: (c, 0, 0))
+    above = pl.BlockSpec((1, rows, cols), lambda c: (jnp.maximum(c * chunk - 1, 0), 0, 0))
+    below = pl.BlockSpec(
+        (1, rows, cols), lambda c: (jnp.minimum(c * chunk + chunk, levels - 1), 0, 0)
+    )
+
+    def whole(shape):
+        return pl.BlockSpec(shape, lambda c: (0,) * len(shape))
+
+    halo_row = pl.BlockSpec((fields, chunk, cols), lambda c: (0, c, 0))
     return pl.pallas_call(
         stencil_kernel,
+        grid=(levels // chunk,),
+        in_specs=[whole((2, rows, cols))]
+        + [main] * fields
+        + [above] * fields
+        + [below] * fields
+        + [whole((rows, cols)), halo_row, halo_row, whole(halo_west.shape), whole(halo_east.shape)],
+        out_specs=(main, main, main, main),
         out_shape=(block, block, block, block),
+        scratch_shapes=[
+            pltpu.VMEM((rows, cols), jnp.float32),
+            pltpu.VMEM((rows, cols), jnp.float32),
+            pltpu.VMEM((1, cols), jnp.float32),
+        ],
     )(
         coriolis,
-        eastbound_current,
-        poleward_current,
-        warmth_excess,
-        saltiness_excess,
-        water_indicator,
+        *inputs,
+        *inputs,
+        *inputs,
         column_layer_count,
         halo_north,
         halo_south,

time: 55 us -> 54.4 us (0.989)
  Pallas kernels: 26.3 us -> 25.7 us
    pallas_call x1, Pallas kernels: 21.3 us -> 20.7 us  [per_device(): pl.pallas_call(stencil_kernel, grid=(levels // chunk,), in_specs=[whole((...]
where the time goes in v5:
time: 54.4 us; the launch traced here: 54.1 us
  Pallas kernels  25.7 us (47%)
  starting transfers between devices  11.9 us (22%)
  waiting for transfers between devices  11.1 us (20%)
  local copies, waits for them, and re-layouts  4.44 us (8%)
  between operations  0.74 us (1%)
    pallas_call x1, Pallas kernels, per_device(): pl.pallas_call(stencil_kernel, grid=(levels // chunk,), in_specs=[whole((...  20.7 us
    ppermute x5, starting transfers between devices, shift(): return lax.ppermute(value, ('lon', 'lat'), pairs)  11.9 us
    ppermute x5, waiting for transfers between devices, shift(): return lax.ppermute(value, ('lon', 'lat'), pairs)  11.1 us
    pallas_call x1, Pallas kernels, per_device(): pl.pallas_call(edge_kernel, grid=(levels // chunk,), in_specs=[pl.BlockSp...  4.97 us
    unnamed x14, local copies, waits for them, and re-layouts  1.95 us
  transfers between devices with their start and end apart: 5, of which 4 were waited for; matrix products, arithmetic and copies ran while one was open for 3% of the time, Pallas kernels for 0%

profile of v5, /device:TPU:228, one launch (start us, length us, event | category | flops | bytes accessed | tf_op | source)
XLA Modules:
  0.0 54.1 jit_solution(589309530981999271)
XLA Ops:
  0.6 5.0 %shard_map.102 = (f32[5,32,256]{2,1,0:T(8,128)}, f32[5,32,256]{2,1,0:T(8,128)}, f32[5,32,32]{2,1,0:T(8,128)}, f32[5,32,32]{2,1,0:T(8,128)}) custom-call(f32[32,32,256]{2,1,0:T(8,128)} %ub_ref.1, f32[32,32,256]{2,1,0:T(8,128)} %vb_ref.1, f32[32,32,256]{2,1,0:T(8,128)} %tb_ref.1, f32[32,32,256]{2,1,0:T(8,128)} %sb_ref.1, s32[32,32,256]{2,1,0:T(8,128)} %wb_ref.1), custom_call_target="tpu_custom_call" | custom-call | tf_op jit(solution)/shard_map/pallas_call | solution.py:454
  5.6 1.3 %collective-permute-start.2 = (f32[5,32,256]{2,1,0:T(8,128)}, f32[5,32,256]{2,1,0:T(8,128)S(1)}, u32[]{:S(2)}, u32[]{:S(2)}) collective-permute-start(f32[5,32,256]{2,1,0:T(8,128)} %get-tuple-element.8), channel_id=1, source_target_pairs={{0,1},{16,17},{32,33},{48,49},{64,65},{80,81},{96,97},{112,113},{1... | collective-permute-start | bytes 491528 | tf_op jit(solution)/shard_map/ppermute | solution.py:175
  6.9 5.0 %collective-permute-start = (f32[5,32,256]{2,1,0:T(8,128)}, f32[5,32,256]{2,1,0:T(8,128)S(1)}, u32[]{:S(2)}, u32[]{:S(2)}) collective-permute-start(f32[5,32,256]{2,1,0:T(8,128)} %get-tuple-element.8), channel_id=1, source_target_pairs={{15,255},{31,239},{47,223},{63,207},{79,191},{95,175},{111,159},{1... | collective-permute-start | bytes 491528 | tf_op jit(solution)/shard_map/ppermute | solution.py:175
  11.9 1.3 %collective-permute-start.1 = (f32[5,32,256]{2,1,0:T(8,128)}, f32[5,32,256]{2,1,0:T(8,128)S(1)}, u32[]{:S(2)}, u32[]{:S(2)}) collective-permute-start(f32[5,32,256]{2,1,0:T(8,128)} %get-tuple-element.9), channel_id=1, source_target_pairs={{1,0},{17,16},{33,32},{49,48},{65,64},{81,80},{97,96},{113,112},{1... | collective-permute-start | bytes 491528 | tf_op jit(solution)/shard_map/ppermute | solution.py:175
  13.2 0.1 pad.7.clone
  13.3 0.3 collective-permute-done.2.rs_ref
  13.6 0.0 copy-start
  13.6 0.1 fusion
  13.7 0.6 %copy-done = f32[5,32,256]{2,1,0:T(8,128)} copy-done((f32[5,32,256]{2,1,0:T(8,128)}, f32[5,32,256]{2,1,0:T(8,128)S(1)}, u32[]{:S(2)}) %copy-start) | copy-done | bytes 163864
  14.3 0.1 copy.22
  14.4 0.1 copy.21
  14.5 5.5 %collective-permute-done = f32[5,32,256]{2,1,0:T(8,128)S(1)} collective-permute-done((f32[5,32,256]{2,1,0:T(8,128)}, f32[5,32,256]{2,1,0:T(8,128)S(1)}, u32[]{:S(2)}, u32[]{:S(2)}) %collective-permute-start) | collective-permute-done | bytes 163872 | tf_op jit(solution)/shard_map/ppermute | solution.py:175
  20.0 0.2 copy.16
  20.2 0.3 rev.3
  20.5 0.0 copy-start.5
  20.6 0.0 collective-permute-done.1
  20.6 0.2 copy.17
  20.8 0.4 copy-done.5
  21.2 0.0 copy-start.3
  21.2 0.0 copy-start.4
  21.2 0.1 multiply_select_fusion
  21.4 0.7 %copy-done.3 = f32[5,32,32]{2,1,0:T(8,128)S(1)} copy-done((f32[5,32,32]{2,1,0:T(8,128)S(1)}, f32[5,32,32]{2,1,0:T(8,128)}, u32[]{:S(2)}) %copy-start.3) | copy-done | bytes 20504
  22.1 0.0 copy-done.4
  22.1 0.1 maximum_maximum_fusion.1
  22.2 4.3 %collective-permute-start.4 = (f32[5,40,32]{2,1,0:T(8,128)S(1)}, f32[5,40,32]{2,1,0:T(8,128)S(1)}, u32[]{:S(2)}, u32[]{:S(2)}) collective-permute-start(f32[5,40,32]{2,1,0:T(8,128)S(1)} %get-tuple-element.16), channel_id=1, source_target_pairs={{0,240},{16,0},{32,16},{48,32},{64,48},{80,64},{96,80},{112,96},{1... | collective-permute-start | bytes 76808 | tf_op jit(solution)/shard_map/ppermute | solution.py:175
  26.5 0.0 collective-permute-start.3
  26.5 0.9 %copy.20.rn_ref = f32[5,32,256]{2,1,0:T(8,128)} copy(f32[5,32,256]{1,2,0:T(8,128)S(1)} %multiply_select_fusion) | data formatting | bytes 327680 | tf_op jit(solution)/shard_map/jit(_where)/select_n | solution.py:487
  27.4 1.4 %collective-permute-done.4.te_ref = f32[5,40,32]{2,1,0:T(8,128)S(1)} collective-permute-done((f32[5,40,32]{2,1,0:T(8,128)S(1)}, f32[5,40,32]{2,1,0:T(8,128)S(1)}, u32[]{:S(2)}, u32[]{:S(2)}) %collective-permute-start.4) | collective-permute-done | bytes 25632 | tf_op jit(solution)/shard_map/ppermute | solution.py:175
  28.8 0.0 copy-start.1
  28.8 3.9 %collective-permute-done.3.tw_ref = f32[5,40,32]{2,1,0:T(8,128)S(1)} collective-permute-done((f32[5,40,32]{2,1,0:T(8,128)S(1)}, f32[5,40,32]{2,1,0:T(8,128)S(1)}, u32[]{:S(2)}, u32[]{:S(2)}) %collective-permute-start.3) | collective-permute-done | bytes 25632 | tf_op jit(solution)/shard_map/ppermute | solution.py:175
  32.7 0.0 copy-start.2
  32.7 0.7 %broadcast_in_dim.13.cor_ref = f32[2,32,256]{2,1,0:T(8,128)} broadcast(f32[2,32]{1,0:T(2,128)S(1)} %maximum_bitcast_fusion), dimensions={0,1} | broadcast | bytes 65792 | tf_op jit(solution)/shard_map/broadcast_in_dim | solution.py:503
  33.4 0.0 copy-done.1
  33.4 0.0 copy-done.2
  33.4 20.7 %shard_map.103 = (f32[32,32,256]{2,1,0:T(8,128)}, f32[32,32,256]{2,1,0:T(8,128)}, f32[32,32,256]{2,1,0:T(8,128)}, f32[32,32,256]{2,1,0:T(8,128)}) custom-call(f32[2,32,256]{2,1,0:T(8,128)} %broadcast_in_dim.13.cor_ref, f32[32,32,256]{2,1,0:T(8,128)} %ub_ref.1, f32[32,32,256]{2,1,0:T(8,128)} %vb_ref.1, f32[32,32,256]{2,1,0:T(8,128)} %tb_ref.1, ...), custom_call_target="tpu_custom_call" | custom-call | tf_op jit(solution)/shard_map/pallas_call | solution.py:516
  (4 shorter events, 0.0 us)
Async XLA Ops:
  5.6 8.0 %collective-permute-start.2 = (f32[5,32,256]{2,1,0:T(8,128)}, f32[5,32,256]{2,1,0:T(8,128)S(1)}, u32[]{:S(2)}, u32[]{:S(2)}) collective-permute-start(f32[5,32,256]{2,1,0:T(8,128)} %get-tuple-element.8), channel_id=1, source_target_pairs={{0,1},{16,17},{32,33},{48,49},{64,65},{80,81},{96,97},{112,113},{1... | collective-permute-start | bytes 491528 | tf_op jit(solution)/shard_map/ppermute | solution.py:175
  6.9 13.1 %collective-permute-start = (f32[5,32,256]{2,1,0:T(8,128)}, f32[5,32,256]{2,1,0:T(8,128)S(1)}, u32[]{:S(2)}, u32[]{:S(2)}) collective-permute-start(f32[5,32,256]{2,1,0:T(8,128)} %get-tuple-element.8), channel_id=1, source_target_pairs={{15,255},{31,239},{47,223},{63,207},{79,191},{95,175},{111,159},{1... | collective-permute-start | bytes 491528 | tf_op jit(solution)/shard_map/ppermute | solution.py:175
  11.9 8.7 %collective-permute-start.1 = (f32[5,32,256]{2,1,0:T(8,128)}, f32[5,32,256]{2,1,0:T(8,128)S(1)}, u32[]{:S(2)}, u32[]{:S(2)}) collective-permute-start(f32[5,32,256]{2,1,0:T(8,128)} %get-tuple-element.9), channel_id=1, source_target_pairs={{1,0},{17,16},{33,32},{49,48},{65,64},{81,80},{97,96},{113,112},{1... | collective-permute-start | bytes 491528 | tf_op jit(solution)/shard_map/ppermute | solution.py:175
  13.6 0.7 %copy-start = (f32[5,32,256]{2,1,0:T(8,128)}, f32[5,32,256]{2,1,0:T(8,128)S(1)}, u32[]{:S(2)}) copy-start(f32[5,32,256]{2,1,0:T(8,128)S(1)} %collective-permute-done.2.rs_ref) | copy-start | bytes 491524
  20.5 0.7 %copy-start.5 = (f32[5]{0:T(128)S(1)}, f32[5]{0:T(128)}, u32[]{:S(2)}) copy-start(f32[5]{0:T(128)} %constant.26.clone) | copy-start | bytes 64
  21.2 0.9 %copy-start.3 = (f32[5,32,32]{2,1,0:T(8,128)S(1)}, f32[5,32,32]{2,1,0:T(8,128)}, u32[]{:S(2)}) copy-start(f32[5,32,32]{2,1,0:T(8,128)} %get-tuple-element.11) | copy-start | bytes 61444
  21.2 0.9 %copy-start.4 = (f32[5,32,32]{2,1,0:T(8,128)S(1)}, f32[5,32,32]{2,1,0:T(8,128)}, u32[]{:S(2)}) copy-start(f32[5,32,32]{2,1,0:T(8,128)} %get-tuple-element.10) | copy-start | bytes 61444
  22.2 6.5 %collective-permute-start.4 = (f32[5,40,32]{2,1,0:T(8,128)S(1)}, f32[5,40,32]{2,1,0:T(8,128)S(1)}, u32[]{:S(2)}, u32[]{:S(2)}) collective-permute-start(f32[5,40,32]{2,1,0:T(8,128)S(1)} %get-tuple-element.16), channel_id=1, source_target_pairs={{0,240},{16,0},{32,16},{48,32},{64,48},{80,64},{96,80},{112,96},{1... | collective-permute-start | bytes 76808 | tf_op jit(solution)/shard_map/ppermute | solution.py:175
  26.5 6.2 %collective-permute-start.3 = (f32[5,40,32]{2,1,0:T(8,128)S(1)}, f32[5,40,32]{2,1,0:T(8,128)S(1)}, u32[]{:S(2)}, u32[]{:S(2)}) collective-permute-start(f32[5,40,32]{2,1,0:T(8,128)S(1)} %get-tuple-element.17), channel_id=1, source_target_pairs={{0,16},{16,32},{32,48},{48,64},{64,80},{80,96},{96,112},{112,128},... | collective-permute-start | bytes 76808 | tf_op jit(solution)/shard_map/ppermute | solution.py:175
  28.8 4.6 %copy-start.1 = (f32[5,40,32]{2,1,0:T(8,128)}, f32[5,40,32]{2,1,0:T(8,128)S(1)}, u32[]{:S(2)}) copy-start(f32[5,40,32]{2,1,0:T(8,128)S(1)} %collective-permute-done.4.te_ref) | copy-start | bytes 76804
  32.7 0.7 %copy-start.2 = (f32[5,40,32]{2,1,0:T(8,128)}, f32[5,40,32]{2,1,0:T(8,128)S(1)}, u32[]{:S(2)}) copy-start(f32[5,40,32]{2,1,0:T(8,128)S(1)} %collective-permute-done.3.tw_ref) | copy-start | bytes 76804

commit v6 on v5

--- a/solution.py
+++ b/solution.py
@@ -209,7 +209,7 @@
     east_ref, north_ref, temp_ref, salt_ref, p_ref, pe_ref, pn_ref,
 ):
     chunk, rows, cols = u_ref.shape
-    levels = tw_ref.shape[2]
+    levels = tw_ref.shape[1]
     step = pl.program_id(0)
     near = {
         id(u_ref): (ua_ref, ub_ref),
@@ -266,17 +266,18 @@
         spread = {}
 
         def tall(field):
-            if field not in spread:
-                spread[field] = tuple(
-                    jnp.dot(
-                        ref[field],
+            if not spread:
+                for ref in (tw_ref, te_ref):
+                    spread[id(ref)] = jnp.dot(
+                        ref[...],
                         onehot,
                         precision=lax.Precision.HIGHEST,
                         preferred_element_type=jnp.float32,
                     )
-                    for ref in (tw_ref, te_ref)
-                )
-            return spread[field]
+            span = tw_ref.shape[0] // fields
+            return tuple(
+                spread[id(ref)][field * span : (field + 1) * span] for ref in (tw_ref, te_ref)
+            )
 
         def row(variant, field):
             west_t, east_t = tall(field)
@@ -492,8 +493,8 @@
     east_tall = jnp.concatenate(
         [east_col, halo_south[:, None, :, -1], halo_north[:, None, :, -1], pad], axis=1
     )
-    halo_west = shift(east_tall, east_of)
-    halo_east = shift(west_tall, west_of)
+    halo_west = shift(east_tall, east_of).reshape(-1, levels)
+    halo_east = shift(west_tall, west_of).reshape(-1, levels)
 
     row_start = lax.axis_index("lat") * rows
     total_rows = rows * lax.axis_size("lat")

time: 54.4 us -> 56.5 us (1.039)
  Pallas kernels: 25.7 us -> 28.6 us
  local copies, waits for them, and re-layouts: 4.44 us -> 2.12 us
  waiting for transfers between devices: 11.1 us -> 12.6 us
    pallas_call x1, Pallas kernels: 20.7 us -> 23.6 us  [per_device(): pl.pallas_call(stencil_kernel, grid=(levels // chunk,), in_specs=[whole((...]
    ppermute x5, waiting for transfers between devices: 11.1 us -> 12.6 us  [shift(): return lax.ppermute(value, ('lon', 'lat'), pairs)]
    unnamed x14, local copies, waits for them, and re-layouts: 1.95 us -> 0.8 us
    select_n x1 -> x0, local copies, waits for them, and re-layouts: 0.87 us -> none  [per_device(): halo_north = jnp.where(is_top, sign * fold_row[:, :, ::-1], halo_north)]
  transfers between devices with their start and end apart: 5 -> 5, of which waited for: 4 -> 4; matrix products, arithmetic and copies ran while one was open for 3% -> 1% of each run, Pallas kernels for 0% -> 0%
where the time goes in v6:
time: 56.5 us; the launch traced here: 56.3 us
  Pallas kernels  28.6 us (51%)
  waiting for transfers between devices  12.6 us (22%)
  starting transfers between devices  11.9 us (21%)
  local copies, waits for them, and re-layouts  2.12 us (4%)
  between operations  0.81 us (1%)
    pallas_call x1, Pallas kernels, per_device(): pl.pallas_call(stencil_kernel, grid=(levels // chunk,), in_specs=[whole((...  23.6 us
    ppermute x5, waiting for transfers between devices, shift(): return lax.ppermute(value, ('lon', 'lat'), pairs)  12.6 us
    ppermute x5, starting transfers between devices, shift(): return lax.ppermute(value, ('lon', 'lat'), pairs)  11.9 us
    pallas_call x1, Pallas kernels, per_device(): pl.pallas_call(edge_kernel, grid=(levels // chunk,), in_specs=[pl.BlockSp...  4.97 us
  transfers between devices with their start and end apart: 5, of which 4 were waited for; matrix products, arithmetic and copies ran while one was open for 1% of the time, Pallas kernels for 0%

profile of v6, /device:TPU:228, one launch (start us, length us, event | category | flops | bytes accessed | tf_op | source)
XLA Modules:
  0.0 56.3 jit_solution(8722627266267561477)
XLA Ops:
  0.6 5.0 %shard_map.102 = (f32[5,32,256]{2,1,0:T(8,128)}, f32[5,32,256]{2,1,0:T(8,128)}, f32[5,32,32]{2,1,0:T(8,128)}, f32[5,32,32]{2,1,0:T(8,128)}) custom-call(f32[32,32,256]{2,1,0:T(8,128)} %ub_ref.1, f32[32,32,256]{2,1,0:T(8,128)} %vb_ref.1, f32[32,32,256]{2,1,0:T(8,128)} %tb_ref.1, f32[32,32,256]{2,1,0:T(8,128)} %sb_ref.1, s32[32,32,256]{2,1,0:T(8,128)} %wb_ref.1), custom_call_target="tpu_custom_call" | custom-call | tf_op jit(solution)/shard_map/pallas_call | solution.py:455
  5.6 1.3 %collective-permute-start.2 = (f32[5,32,256]{2,1,0:T(8,128)}, f32[5,32,256]{2,1,0:T(8,128)S(1)}, u32[]{:S(2)}, u32[]{:S(2)}) collective-permute-start(f32[5,32,256]{2,1,0:T(8,128)} %get-tuple-element.8), channel_id=1, source_target_pairs={{0,1},{16,17},{32,33},{48,49},{64,65},{80,81},{96,97},{112,113},{1... | collective-permute-start | bytes 491528 | tf_op jit(solution)/shard_map/ppermute | solution.py:175
  6.9 5.0 %collective-permute-start = (f32[5,32,256]{2,1,0:T(8,128)}, f32[5,32,256]{2,1,0:T(8,128)S(1)}, u32[]{:S(2)}, u32[]{:S(2)}) collective-permute-start(f32[5,32,256]{2,1,0:T(8,128)} %get-tuple-element.8), channel_id=1, source_target_pairs={{15,255},{31,239},{47,223},{63,207},{79,191},{95,175},{111,159},{1... | collective-permute-start | bytes 491528 | tf_op jit(solution)/shard_map/ppermute | solution.py:175
  11.9 1.3 %collective-permute-start.1 = (f32[5,32,256]{2,1,0:T(8,128)}, f32[5,32,256]{2,1,0:T(8,128)S(1)}, u32[]{:S(2)}, u32[]{:S(2)}) collective-permute-start(f32[5,32,256]{2,1,0:T(8,128)} %get-tuple-element.9), channel_id=1, source_target_pairs={{1,0},{17,16},{33,32},{49,48},{65,64},{81,80},{97,96},{113,112},{1... | collective-permute-start | bytes 491528 | tf_op jit(solution)/shard_map/ppermute | solution.py:175
  13.2 0.1 pad.7.clone
  13.3 0.3 collective-permute-done.2.rs_ref
  13.6 0.0 copy-start.1
  13.6 0.2 slice_reduce_fusion.1
  13.8 0.0 copy-start.6
  13.9 6.1 %collective-permute-done = f32[5,32,256]{2,1,0:T(8,128)S(1)} collective-permute-done((f32[5,32,256]{2,1,0:T(8,128)}, f32[5,32,256]{2,1,0:T(8,128)S(1)}, u32[]{:S(2)}, u32[]{:S(2)}) %collective-permute-start) | collective-permute-done | bytes 163872 | tf_op jit(solution)/shard_map/ppermute | solution.py:175
  20.0 0.2 rev.3
  20.2 0.0 copy-done.1
  20.2 0.0 collective-permute-done.1
  20.2 0.0 copy-done.6
  20.2 0.1 multiply_select_fusion.rn_ref
  20.3 0.0 copy-start
  20.3 0.0 copy-start.4
  20.3 0.0 copy-start.5
  20.4 0.2 slice_reduce_fusion
  20.6 0.7 %copy-done.4 = f32[5,32,32]{2,1,0:T(8,128)S(1)} copy-done((f32[5,32,32]{2,1,0:T(8,128)S(1)}, f32[5,32,32]{2,1,0:T(8,128)}, u32[]{:S(2)}) %copy-start.4) | copy-done | bytes 20504
  21.3 0.0 copy-done.5
  21.3 0.1 maximum_maximum_fusion.1
  21.4 0.0 copy-done
  21.4 4.3 %collective-permute-start.4 = (f32[5,40,32]{2,1,0:T(8,128)S(1)}, f32[5,40,32]{2,1,0:T(8,128)S(1)}, u32[]{:S(2)}, u32[]{:S(2)}) collective-permute-start(f32[5,40,32]{2,1,0:T(8,128)S(1)} %get-tuple-element.16), channel_id=1, source_target_pairs={{0,240},{16,0},{32,16},{48,32},{64,48},{80,64},{96,80},{112,96},{1... | collective-permute-start | bytes 76808 | tf_op jit(solution)/shard_map/ppermute | solution.py:175
  25.7 0.0 collective-permute-start.3
  25.7 2.2 %collective-permute-done.4 = f32[5,40,32]{2,1,0:T(8,128)S(1)} collective-permute-done((f32[5,40,32]{2,1,0:T(8,128)S(1)}, f32[5,40,32]{2,1,0:T(8,128)S(1)}, u32[]{:S(2)}, u32[]{:S(2)}) %collective-permute-start.4) | collective-permute-done | bytes 25632 | tf_op jit(solution)/shard_map/ppermute | solution.py:175
  28.0 0.0 copy-start.2
  28.0 3.9 %collective-permute-done.3 = f32[5,40,32]{2,1,0:T(8,128)S(1)} collective-permute-done((f32[5,40,32]{2,1,0:T(8,128)S(1)}, f32[5,40,32]{2,1,0:T(8,128)S(1)}, u32[]{:S(2)}, u32[]{:S(2)}) %collective-permute-start.3) | collective-permute-done | bytes 25632 | tf_op jit(solution)/shard_map/ppermute | solution.py:175
  31.9 0.0 copy-start.3
  31.9 0.7 %broadcast_in_dim.13.cor_ref = f32[2,32,256]{2,1,0:T(8,128)} broadcast(f32[2,32]{1,0:T(2,128)S(1)} %maximum_bitcast_fusion), dimensions={0,1} | broadcast | bytes 65792 | tf_op jit(solution)/shard_map/broadcast_in_dim | solution.py:504
  32.6 0.0 copy-done.2
  32.6 0.0 copy-done.3
  32.6 23.6 %shard_map.103 = (f32[32,32,256]{2,1,0:T(8,128)}, f32[32,32,256]{2,1,0:T(8,128)}, f32[32,32,256]{2,1,0:T(8,128)}, f32[32,32,256]{2,1,0:T(8,128)}) custom-call(f32[2,32,256]{2,1,0:T(8,128)} %broadcast_in_dim.13.cor_ref, f32[32,32,256]{2,1,0:T(8,128)} %ub_ref.1, f32[32,32,256]{2,1,0:T(8,128)} %vb_ref.1, f32[32,32,256]{2,1,0:T(8,128)} %tb_ref.1, ...), custom_call_target="tpu_custom_call" | custom-call | tf_op jit(solution)/shard_map/pallas_call | solution.py:517
  (7 shorter events, 0.0 us)
Async XLA Ops:
  5.6 8.0 %collective-permute-start.2 = (f32[5,32,256]{2,1,0:T(8,128)}, f32[5,32,256]{2,1,0:T(8,128)S(1)}, u32[]{:S(2)}, u32[]{:S(2)}) collective-permute-start(f32[5,32,256]{2,1,0:T(8,128)} %get-tuple-element.8), channel_id=1, source_target_pairs={{0,1},{16,17},{32,33},{48,49},{64,65},{80,81},{96,97},{112,113},{1... | collective-permute-start | bytes 491528 | tf_op jit(solution)/shard_map/ppermute | solution.py:175
  6.9 13.1 %collective-permute-start = (f32[5,32,256]{2,1,0:T(8,128)}, f32[5,32,256]{2,1,0:T(8,128)S(1)}, u32[]{:S(2)}, u32[]{:S(2)}) collective-permute-start(f32[5,32,256]{2,1,0:T(8,128)} %get-tuple-element.8), channel_id=1, source_target_pairs={{15,255},{31,239},{47,223},{63,207},{79,191},{95,175},{111,159},{1... | collective-permute-start | bytes 491528 | tf_op jit(solution)/shard_map/ppermute | solution.py:175
  11.9 8.3 %collective-permute-start.1 = (f32[5,32,256]{2,1,0:T(8,128)}, f32[5,32,256]{2,1,0:T(8,128)S(1)}, u32[]{:S(2)}, u32[]{:S(2)}) collective-permute-start(f32[5,32,256]{2,1,0:T(8,128)} %get-tuple-element.9), channel_id=1, source_target_pairs={{1,0},{17,16},{33,32},{49,48},{65,64},{81,80},{97,96},{113,112},{1... | collective-permute-start | bytes 491528 | tf_op jit(solution)/shard_map/ppermute | solution.py:175
  13.6 6.6 %copy-start.1 = (f32[5,32,256]{2,1,0:T(8,128)}, f32[5,32,256]{2,1,0:T(8,128)S(1)}, u32[]{:S(2)}) copy-start(f32[5,32,256]{2,1,0:T(8,128)S(1)} %collective-permute-done.2.rs_ref) | copy-start | bytes 491524
  13.8 6.4 %copy-start.6 = (f32[5]{0:T(128)S(1)}, f32[5]{0:T(128)}, u32[]{:S(2)}) copy-start(f32[5]{0:T(128)} %constant.26.clone) | copy-start | bytes 64
  20.3 1.1 %copy-start = (f32[5,32,256]{2,1,0:T(8,128)}, f32[5,32,256]{2,1,0:T(8,128)S(1)}, u32[]{:S(2)}) copy-start(f32[5,32,256]{2,1,0:T(8,128)S(1)} %multiply_select_fusion.rn_ref) | copy-start | bytes 491524
  20.3 0.9 %copy-start.4 = (f32[5,32,32]{2,1,0:T(8,128)S(1)}, f32[5,32,32]{2,1,0:T(8,128)}, u32[]{:S(2)}) copy-start(f32[5,32,32]{2,1,0:T(8,128)} %get-tuple-element.11) | copy-start | bytes 61444
  20.3 1.0 %copy-start.5 = (f32[5,32,32]{2,1,0:T(8,128)S(1)}, f32[5,32,32]{2,1,0:T(8,128)}, u32[]{:S(2)}) copy-start(f32[5,32,32]{2,1,0:T(8,128)} %get-tuple-element.10) | copy-start | bytes 61444
  21.4 6.5 %collective-permute-start.4 = (f32[5,40,32]{2,1,0:T(8,128)S(1)}, f32[5,40,32]{2,1,0:T(8,128)S(1)}, u32[]{:S(2)}, u32[]{:S(2)}) collective-permute-start(f32[5,40,32]{2,1,0:T(8,128)S(1)} %get-tuple-element.16), channel_id=1, source_target_pairs={{0,240},{16,0},{32,16},{48,32},{64,48},{80,64},{96,80},{112,96},{1... | collective-permute-start | bytes 76808 | tf_op jit(solution)/shard_map/ppermute | solution.py:175
  25.7 6.2 %collective-permute-start.3 = (f32[5,40,32]{2,1,0:T(8,128)S(1)}, f32[5,40,32]{2,1,0:T(8,128)S(1)}, u32[]{:S(2)}, u32[]{:S(2)}) collective-permute-start(f32[5,40,32]{2,1,0:T(8,128)S(1)} %get-tuple-element.17), channel_id=1, source_target_pairs={{0,16},{16,32},{32,48},{48,64},{64,80},{80,96},{96,112},{112,128},... | collective-permute-start | bytes 76808 | tf_op jit(solution)/shard_map/ppermute | solution.py:175
  28.0 4.6 %copy-start.2 = (f32[5,40,32]{2,1,0:T(8,128)}, f32[5,40,32]{2,1,0:T(8,128)S(1)}, u32[]{:S(2)}) copy-start(f32[5,40,32]{2,1,0:T(8,128)S(1)} %collective-permute-done.4) | copy-start | bytes 76804
  31.9 0.7 %copy-start.3 = (f32[5,40,32]{2,1,0:T(8,128)}, f32[5,40,32]{2,1,0:T(8,128)S(1)}, u32[]{:S(2)}) copy-start(f32[5,40,32]{2,1,0:T(8,128)S(1)} %collective-permute-done.3) | copy-start | bytes 76804

commit v7 on v5

--- a/solution.py
+++ b/solution.py
@@ -241,7 +241,7 @@
     row_lane = lax.broadcasted_iota(jnp.int32, (1, cols), 1)
     row_east = row_lane == cols - 1
     row_west = row_lane == 0
-    pick = lax.broadcasted_iota(jnp.int32, (levels, cols), 0)
+    pick_lane = lax.broadcasted_iota(jnp.int32, tw_ref.shape[1:], 1)
     cor_t = cor_ref[0]
     cor_v = cor_ref[1]
     count = clc_ref[...]
@@ -262,17 +262,14 @@
         pres, pres_e, pres_n = carry
         k = step * chunk + r
 
-        onehot = (pick == k).astype(jnp.float32)
         spread = {}
 
         def tall(field):
             if field not in spread:
                 spread[field] = tuple(
-                    jnp.dot(
-                        ref[field],
-                        onehot,
-                        precision=lax.Precision.HIGHEST,
-                        preferred_element_type=jnp.float32,
+                    jnp.broadcast_to(
+                        jnp.sum(jnp.where(pick_lane == k, ref[field], 0.0), axis=1, keepdims=True),
+                        (ref.shape[1], cols),
                     )
                     for ref in (tw_ref, te_ref)
                 )

time: 54.4 us -> 51.6 us (0.949)
  Pallas kernels: 25.7 us -> 22.9 us
    pallas_call x1, Pallas kernels: 20.7 us -> 17.9 us  [per_device(): pl.pallas_call(stencil_kernel, grid=(levels // chunk,), in_specs=[whole((...]
where the time goes in v7:
time: 51.6 us; the launch traced here: 51.3 us
  Pallas kernels  22.9 us (44%)
  starting transfers between devices  11.9 us (23%)
  waiting for transfers between devices  11.1 us (22%)
  local copies, waits for them, and re-layouts  4.44 us (9%)
  between operations  0.74 us (1%)
    pallas_call x1, Pallas kernels, per_device(): pl.pallas_call(stencil_kernel, grid=(levels // chunk,), in_specs=[whole((...  17.9 us
    ppermute x5, starting transfers between devices, shift(): return lax.ppermute(value, ('lon', 'lat'), pairs)  11.9 us
    ppermute x5, waiting for transfers between devices, shift(): return lax.ppermute(value, ('lon', 'lat'), pairs)  11.1 us
    pallas_call x1, Pallas kernels, per_device(): pl.pallas_call(edge_kernel, grid=(levels // chunk,), in_specs=[pl.BlockSp...  4.97 us
    unnamed x14, local copies, waits for them, and re-layouts  1.95 us
  transfers between devices with their start and end apart: 5, of which 4 were waited for; matrix products, arithmetic and copies ran while one was open for 3% of the time, Pallas kernels for 0%

profile of v7, /device:TPU:228, one launch (start us, length us, event | category | flops | bytes accessed | tf_op | source)
XLA Modules:
  0.0 51.3 jit_solution(16316134209852546766)
XLA Ops:
  0.6 5.0 %shard_map.102 = (f32[5,32,256]{2,1,0:T(8,128)}, f32[5,32,256]{2,1,0:T(8,128)}, f32[5,32,32]{2,1,0:T(8,128)}, f32[5,32,32]{2,1,0:T(8,128)}) custom-call(f32[32,32,256]{2,1,0:T(8,128)} %ub_ref.1, f32[32,32,256]{2,1,0:T(8,128)} %vb_ref.1, f32[32,32,256]{2,1,0:T(8,128)} %tb_ref.1, f32[32,32,256]{2,1,0:T(8,128)} %sb_ref.1, s32[32,32,256]{2,1,0:T(8,128)} %wb_ref.1), custom_call_target="tpu_custom_call" | custom-call | tf_op jit(solution)/shard_map/pallas_call | solution.py:451
  5.6 1.3 %collective-permute-start.2 = (f32[5,32,256]{2,1,0:T(8,128)}, f32[5,32,256]{2,1,0:T(8,128)S(1)}, u32[]{:S(2)}, u32[]{:S(2)}) collective-permute-start(f32[5,32,256]{2,1,0:T(8,128)} %get-tuple-element.8), channel_id=1, source_target_pairs={{0,1},{16,17},{32,33},{48,49},{64,65},{80,81},{96,97},{112,113},{1... | collective-permute-start | bytes 491528 | tf_op jit(solution)/shard_map/ppermute | solution.py:175
  6.9 5.0 %collective-permute-start = (f32[5,32,256]{2,1,0:T(8,128)}, f32[5,32,256]{2,1,0:T(8,128)S(1)}, u32[]{:S(2)}, u32[]{:S(2)}) collective-permute-start(f32[5,32,256]{2,1,0:T(8,128)} %get-tuple-element.8), channel_id=1, source_target_pairs={{15,255},{31,239},{47,223},{63,207},{79,191},{95,175},{111,159},{1... | collective-permute-start | bytes 491528 | tf_op jit(solution)/shard_map/ppermute | solution.py:175
  11.9 1.3 %collective-permute-start.1 = (f32[5,32,256]{2,1,0:T(8,128)}, f32[5,32,256]{2,1,0:T(8,128)S(1)}, u32[]{:S(2)}, u32[]{:S(2)}) collective-permute-start(f32[5,32,256]{2,1,0:T(8,128)} %get-tuple-element.9), channel_id=1, source_target_pairs={{1,0},{17,16},{33,32},{49,48},{65,64},{81,80},{97,96},{113,112},{1... | collective-permute-start | bytes 491528 | tf_op jit(solution)/shard_map/ppermute | solution.py:175
  13.2 0.1 pad.7.clone
  13.3 0.3 collective-permute-done.2.rs_ref
  13.6 0.0 copy-start
  13.6 0.1 fusion
  13.7 0.6 %copy-done = f32[5,32,256]{2,1,0:T(8,128)} copy-done((f32[5,32,256]{2,1,0:T(8,128)}, f32[5,32,256]{2,1,0:T(8,128)S(1)}, u32[]{:S(2)}) %copy-start) | copy-done | bytes 163864
  14.3 0.1 copy.22
  14.4 0.1 copy.21
  14.5 5.5 %collective-permute-done = f32[5,32,256]{2,1,0:T(8,128)S(1)} collective-permute-done((f32[5,32,256]{2,1,0:T(8,128)}, f32[5,32,256]{2,1,0:T(8,128)S(1)}, u32[]{:S(2)}, u32[]{:S(2)}) %collective-permute-start) | collective-permute-done | bytes 163872 | tf_op jit(solution)/shard_map/ppermute | solution.py:175
  20.0 0.2 copy.16
  20.2 0.3 rev.3
  20.5 0.0 copy-start.5
  20.6 0.0 collective-permute-done.1
  20.6 0.2 copy.17
  20.8 0.4 copy-done.5
  21.2 0.0 copy-start.3
  21.2 0.0 copy-start.4
  21.2 0.1 multiply_select_fusion
  21.4 0.7 %copy-done.3 = f32[5,32,32]{2,1,0:T(8,128)S(1)} copy-done((f32[5,32,32]{2,1,0:T(8,128)S(1)}, f32[5,32,32]{2,1,0:T(8,128)}, u32[]{:S(2)}) %copy-start.3) | copy-done | bytes 20504
  22.1 0.0 copy-done.4
  22.1 0.1 maximum_maximum_fusion.1
  22.2 4.3 %collective-permute-start.4 = (f32[5,40,32]{2,1,0:T(8,128)S(1)}, f32[5,40,32]{2,1,0:T(8,128)S(1)}, u32[]{:S(2)}, u32[]{:S(2)}) collective-permute-start(f32[5,40,32]{2,1,0:T(8,128)S(1)} %get-tuple-element.16), channel_id=1, source_target_pairs={{0,240},{16,0},{32,16},{48,32},{64,48},{80,64},{96,80},{112,96},{1... | collective-permute-start | bytes 76808 | tf_op jit(solution)/shard_map/ppermute | solution.py:175
  26.5 0.0 collective-permute-start.3
  26.5 0.9 %copy.20.rn_ref = f32[5,32,256]{2,1,0:T(8,128)} copy(f32[5,32,256]{1,2,0:T(8,128)S(1)} %multiply_select_fusion) | data formatting | bytes 327680 | tf_op jit(solution)/shard_map/jit(_where)/select_n | solution.py:484
  27.4 1.4 %collective-permute-done.4.te_ref = f32[5,40,32]{2,1,0:T(8,128)S(1)} collective-permute-done((f32[5,40,32]{2,1,0:T(8,128)S(1)}, f32[5,40,32]{2,1,0:T(8,128)S(1)}, u32[]{:S(2)}, u32[]{:S(2)}) %collective-permute-start.4) | collective-permute-done | bytes 25632 | tf_op jit(solution)/shard_map/ppermute | solution.py:175
  28.8 0.0 copy-start.1
  28.8 3.9 %collective-permute-done.3.tw_ref = f32[5,40,32]{2,1,0:T(8,128)S(1)} collective-permute-done((f32[5,40,32]{2,1,0:T(8,128)S(1)}, f32[5,40,32]{2,1,0:T(8,128)S(1)}, u32[]{:S(2)}, u32[]{:S(2)}) %collective-permute-start.3) | collective-permute-done | bytes 25632 | tf_op jit(solution)/shard_map/ppermute | solution.py:175
  32.7 0.0 copy-start.2
  32.7 0.7 %broadcast_in_dim.13.cor_ref = f32[2,32,256]{2,1,0:T(8,128)} broadcast(f32[2,32]{1,0:T(2,128)S(1)} %maximum_bitcast_fusion), dimensions={0,1} | broadcast | bytes 65792 | tf_op jit(solution)/shard_map/broadcast_in_dim | solution.py:500
  33.4 0.0 copy-done.1
  33.4 0.0 copy-done.2
  33.4 17.9 %shard_map.103 = (f32[32,32,256]{2,1,0:T(8,128)}, f32[32,32,256]{2,1,0:T(8,128)}, f32[32,32,256]{2,1,0:T(8,128)}, f32[32,32,256]{2,1,0:T(8,128)}) custom-call(f32[2,32,256]{2,1,0:T(8,128)} %broadcast_in_dim.13.cor_ref, f32[32,32,256]{2,1,0:T(8,128)} %ub_ref.1, f32[32,32,256]{2,1,0:T(8,128)} %vb_ref.1, f32[32,32,256]{2,1,0:T(8,128)} %tb_ref.1, ...), custom_call_target="tpu_custom_call" | custom-call | tf_op jit(solution)/shard_map/pallas_call | solution.py:513
  (4 shorter events, 0.0 us)
Async XLA Ops:
  5.6 8.0 %collective-permute-start.2 = (f32[5,32,256]{2,1,0:T(8,128)}, f32[5,32,256]{2,1,0:T(8,128)S(1)}, u32[]{:S(2)}, u32[]{:S(2)}) collective-permute-start(f32[5,32,256]{2,1,0:T(8,128)} %get-tuple-element.8), channel_id=1, source_target_pairs={{0,1},{16,17},{32,33},{48,49},{64,65},{80,81},{96,97},{112,113},{1... | collective-permute-start | bytes 491528 | tf_op jit(solution)/shard_map/ppermute | solution.py:175
  6.9 13.1 %collective-permute-start = (f32[5,32,256]{2,1,0:T(8,128)}, f32[5,32,256]{2,1,0:T(8,128)S(1)}, u32[]{:S(2)}, u32[]{:S(2)}) collective-permute-start(f32[5,32,256]{2,1,0:T(8,128)} %get-tuple-element.8), channel_id=1, source_target_pairs={{15,255},{31,239},{47,223},{63,207},{79,191},{95,175},{111,159},{1... | collective-permute-start | bytes 491528 | tf_op jit(solution)/shard_map/ppermute | solution.py:175
  11.9 8.7 %collective-permute-start.1 = (f32[5,32,256]{2,1,0:T(8,128)}, f32[5,32,256]{2,1,0:T(8,128)S(1)}, u32[]{:S(2)}, u32[]{:S(2)}) collective-permute-start(f32[5,32,256]{2,1,0:T(8,128)} %get-tuple-element.9), channel_id=1, source_target_pairs={{1,0},{17,16},{33,32},{49,48},{65,64},{81,80},{97,96},{113,112},{1... | collective-permute-start | bytes 491528 | tf_op jit(solution)/shard_map/ppermute | solution.py:175
  13.6 0.7 %copy-start = (f32[5,32,256]{2,1,0:T(8,128)}, f32[5,32,256]{2,1,0:T(8,128)S(1)}, u32[]{:S(2)}) copy-start(f32[5,32,256]{2,1,0:T(8,128)S(1)} %collective-permute-done.2.rs_ref) | copy-start | bytes 491524
  20.5 0.7 %copy-start.5 = (f32[5]{0:T(128)S(1)}, f32[5]{0:T(128)}, u32[]{:S(2)}) copy-start(f32[5]{0:T(128)} %constant.26.clone) | copy-start | bytes 64
  21.2 0.9 %copy-start.3 = (f32[5,32,32]{2,1,0:T(8,128)S(1)}, f32[5,32,32]{2,1,0:T(8,128)}, u32[]{:S(2)}) copy-start(f32[5,32,32]{2,1,0:T(8,128)} %get-tuple-element.11) | copy-start | bytes 61444
  21.2 0.9 %copy-start.4 = (f32[5,32,32]{2,1,0:T(8,128)S(1)}, f32[5,32,32]{2,1,0:T(8,128)}, u32[]{:S(2)}) copy-start(f32[5,32,32]{2,1,0:T(8,128)} %get-tuple-element.10) | copy-start | bytes 61444
  22.2 6.5 %collective-permute-start.4 = (f32[5,40,32]{2,1,0:T(8,128)S(1)}, f32[5,40,32]{2,1,0:T(8,128)S(1)}, u32[]{:S(2)}, u32[]{:S(2)}) collective-permute-start(f32[5,40,32]{2,1,0:T(8,128)S(1)} %get-tuple-element.16), channel_id=1, source_target_pairs={{0,240},{16,0},{32,16},{48,32},{64,48},{80,64},{96,80},{112,96},{1... | collective-permute-start | bytes 76808 | tf_op jit(solution)/shard_map/ppermute | solution.py:175
  26.5 6.2 %collective-permute-start.3 = (f32[5,40,32]{2,1,0:T(8,128)S(1)}, f32[5,40,32]{2,1,0:T(8,128)S(1)}, u32[]{:S(2)}, u32[]{:S(2)}) collective-permute-start(f32[5,40,32]{2,1,0:T(8,128)S(1)} %get-tuple-element.17), channel_id=1, source_target_pairs={{0,16},{16,32},{32,48},{48,64},{64,80},{80,96},{96,112},{112,128},... | collective-permute-start | bytes 76808 | tf_op jit(solution)/shard_map/ppermute | solution.py:175
  28.8 4.6 %copy-start.1 = (f32[5,40,32]{2,1,0:T(8,128)}, f32[5,40,32]{2,1,0:T(8,128)S(1)}, u32[]{:S(2)}) copy-start(f32[5,40,32]{2,1,0:T(8,128)S(1)} %collective-permute-done.4.te_ref) | copy-start | bytes 76804
  32.7 0.7 %copy-start.2 = (f32[5,40,32]{2,1,0:T(8,128)}, f32[5,40,32]{2,1,0:T(8,128)S(1)}, u32[]{:S(2)}) copy-start(f32[5,40,32]{2,1,0:T(8,128)S(1)} %collective-permute-done.3.tw_ref) | copy-start | bytes 76804

commit v8 on v7

--- a/solution.py
+++ b/solution.py
@@ -267,10 +267,7 @@
         def tall(field):
             if field not in spread:
                 spread[field] = tuple(
-                    jnp.broadcast_to(
-                        jnp.sum(jnp.where(pick_lane == k, ref[field], 0.0), axis=1, keepdims=True),
-                        (ref.shape[1], cols),
-                    )
+                    jnp.sum(jnp.where(pick_lane == k, ref[field], 0.0), axis=1, keepdims=True)
                     for ref in (tw_ref, te_ref)
                 )
             return spread[field]
@@ -522,7 +519,7 @@
         out_shape=(block, block, block, block),
         scratch_shapes=[
             pltpu.VMEM((rows, cols), jnp.float32),
-            pltpu.VMEM((rows, cols), jnp.float32),
+            pltpu.VMEM((rows, 1), jnp.float32),
             pltpu.VMEM((1, cols), jnp.float32),
         ],
     )(

time: 51.6 us -> 53.8 us (1.043)
  Pallas kernels: 22.9 us -> 25.1 us
    pallas_call x1, Pallas kernels: 17.9 us -> 20.2 us  [per_device(): pl.pallas_call(stencil_kernel, grid=(levels // chunk,), in_specs=[whole((...]
where the time goes in v8:
time: 53.8 us; the launch traced here: 53.6 us
  Pallas kernels  25.1 us (47%)
  starting transfers between devices  11.9 us (22%)
  waiting for transfers between devices  11.1 us (21%)
  local copies, waits for them, and re-layouts  4.44 us (8%)
  between operations  0.74 us (1%)
    pallas_call x1, Pallas kernels, per_device(): pl.pallas_call(stencil_kernel, grid=(levels // chunk,), in_specs=[whole((...  20.2 us
    ppermute x5, starting transfers between devices, shift(): return lax.ppermute(value, ('lon', 'lat'), pairs)  11.9 us
    ppermute x5, waiting for transfers between devices, shift(): return lax.ppermute(value, ('lon', 'lat'), pairs)  11.1 us
    pallas_call x1, Pallas kernels, per_device(): pl.pallas_call(edge_kernel, grid=(levels // chunk,), in_specs=[pl.BlockSp...  4.97 us
    unnamed x14, local copies, waits for them, and re-layouts  1.95 us
  transfers between devices with their start and end apart: 5, of which 4 were waited for; matrix products, arithmetic and copies ran while one was open for 3% of the time, Pallas kernels for 0%

profile of v8, /device:TPU:228, one launch (start us, length us, event | category | flops | bytes accessed | tf_op | source)
XLA Modules:
  0.0 53.6 jit_solution(8771050137444057467)
XLA Ops:
  0.6 5.0 %shard_map.102 = (f32[5,32,256]{2,1,0:T(8,128)}, f32[5,32,256]{2,1,0:T(8,128)}, f32[5,32,32]{2,1,0:T(8,128)}, f32[5,32,32]{2,1,0:T(8,128)}) custom-call(f32[32,32,256]{2,1,0:T(8,128)} %ub_ref.1, f32[32,32,256]{2,1,0:T(8,128)} %vb_ref.1, f32[32,32,256]{2,1,0:T(8,128)} %tb_ref.1, f32[32,32,256]{2,1,0:T(8,128)} %sb_ref.1, s32[32,32,256]{2,1,0:T(8,128)} %wb_ref.1), custom_call_target="tpu_custom_call" | custom-call | tf_op jit(solution)/shard_map/pallas_call | solution.py:448
  5.6 1.3 %collective-permute-start.2 = (f32[5,32,256]{2,1,0:T(8,128)}, f32[5,32,256]{2,1,0:T(8,128)S(1)}, u32[]{:S(2)}, u32[]{:S(2)}) collective-permute-start(f32[5,32,256]{2,1,0:T(8,128)} %get-tuple-element.8), channel_id=1, source_target_pairs={{0,1},{16,17},{32,33},{48,49},{64,65},{80,81},{96,97},{112,113},{1... | collective-permute-start | bytes 491528 | tf_op jit(solution)/shard_map/ppermute | solution.py:175
  6.9 5.0 %collective-permute-start = (f32[5,32,256]{2,1,0:T(8,128)}, f32[5,32,256]{2,1,0:T(8,128)S(1)}, u32[]{:S(2)}, u32[]{:S(2)}) collective-permute-start(f32[5,32,256]{2,1,0:T(8,128)} %get-tuple-element.8), channel_id=1, source_target_pairs={{15,255},{31,239},{47,223},{63,207},{79,191},{95,175},{111,159},{1... | collective-permute-start | bytes 491528 | tf_op jit(solution)/shard_map/ppermute | solution.py:175
  11.9 1.3 %collective-permute-start.1 = (f32[5,32,256]{2,1,0:T(8,128)}, f32[5,32,256]{2,1,0:T(8,128)S(1)}, u32[]{:S(2)}, u32[]{:S(2)}) collective-permute-start(f32[5,32,256]{2,1,0:T(8,128)} %get-tuple-element.9), channel_id=1, source_target_pairs={{1,0},{17,16},{33,32},{49,48},{65,64},{81,80},{97,96},{113,112},{1... | collective-permute-start | bytes 491528 | tf_op jit(solution)/shard_map/ppermute | solution.py:175
  13.2 0.1 pad.7.clone
  13.3 0.3 collective-permute-done.2.rs_ref
  13.6 0.0 copy-start
  13.6 0.1 fusion
  13.7 0.6 %copy-done = f32[5,32,256]{2,1,0:T(8,128)} copy-done((f32[5,32,256]{2,1,0:T(8,128)}, f32[5,32,256]{2,1,0:T(8,128)S(1)}, u32[]{:S(2)}) %copy-start) | copy-done | bytes 163864
  14.3 0.1 copy.22
  14.4 0.1 copy.21
  14.5 5.5 %collective-permute-done = f32[5,32,256]{2,1,0:T(8,128)S(1)} collective-permute-done((f32[5,32,256]{2,1,0:T(8,128)}, f32[5,32,256]{2,1,0:T(8,128)S(1)}, u32[]{:S(2)}, u32[]{:S(2)}) %collective-permute-start) | collective-permute-done | bytes 163872 | tf_op jit(solution)/shard_map/ppermute | solution.py:175
  20.0 0.2 copy.16
  20.2 0.3 rev.3
  20.5 0.0 copy-start.5
  20.6 0.0 collective-permute-done.1
  20.6 0.2 copy.17
  20.8 0.4 copy-done.5
  21.2 0.0 copy-start.3
  21.2 0.0 copy-start.4
  21.2 0.1 multiply_select_fusion
  21.4 0.7 %copy-done.3 = f32[5,32,32]{2,1,0:T(8,128)S(1)} copy-done((f32[5,32,32]{2,1,0:T(8,128)S(1)}, f32[5,32,32]{2,1,0:T(8,128)}, u32[]{:S(2)}) %copy-start.3) | copy-done | bytes 20504
  22.1 0.0 copy-done.4
  22.1 0.1 maximum_maximum_fusion.1
  22.2 4.3 %collective-permute-start.4 = (f32[5,40,32]{2,1,0:T(8,128)S(1)}, f32[5,40,32]{2,1,0:T(8,128)S(1)}, u32[]{:S(2)}, u32[]{:S(2)}) collective-permute-start(f32[5,40,32]{2,1,0:T(8,128)S(1)} %get-tuple-element.16), channel_id=1, source_target_pairs={{0,240},{16,0},{32,16},{48,32},{64,48},{80,64},{96,80},{112,96},{1... | collective-permute-start | bytes 76808 | tf_op jit(solution)/shard_map/ppermute | solution.py:175
  26.5 0.0 collective-permute-start.3
  26.5 0.9 %copy.20.rn_ref = f32[5,32,256]{2,1,0:T(8,128)} copy(f32[5,32,256]{1,2,0:T(8,128)S(1)} %multiply_select_fusion) | data formatting | bytes 327680 | tf_op jit(solution)/shard_map/jit(_where)/select_n | solution.py:481
  27.4 1.4 %collective-permute-done.4.te_ref = f32[5,40,32]{2,1,0:T(8,128)S(1)} collective-permute-done((f32[5,40,32]{2,1,0:T(8,128)S(1)}, f32[5,40,32]{2,1,0:T(8,128)S(1)}, u32[]{:S(2)}, u32[]{:S(2)}) %collective-permute-start.4) | collective-permute-done | bytes 25632 | tf_op jit(solution)/shard_map/ppermute | solution.py:175
  28.8 0.0 copy-start.1
  28.8 3.9 %collective-permute-done.3.tw_ref = f32[5,40,32]{2,1,0:T(8,128)S(1)} collective-permute-done((f32[5,40,32]{2,1,0:T(8,128)S(1)}, f32[5,40,32]{2,1,0:T(8,128)S(1)}, u32[]{:S(2)}, u32[]{:S(2)}) %collective-permute-start.3) | collective-permute-done | bytes 25632 | tf_op jit(solution)/shard_map/ppermute | solution.py:175
  32.7 0.0 copy-start.2
  32.7 0.7 %broadcast_in_dim.13.cor_ref = f32[2,32,256]{2,1,0:T(8,128)} broadcast(f32[2,32]{1,0:T(2,128)S(1)} %maximum_bitcast_fusion), dimensions={0,1} | broadcast | bytes 65792 | tf_op jit(solution)/shard_map/broadcast_in_dim | solution.py:497
  33.4 0.0 copy-done.1
  33.4 0.0 copy-done.2
  33.4 20.2 %shard_map.103 = (f32[32,32,256]{2,1,0:T(8,128)}, f32[32,32,256]{2,1,0:T(8,128)}, f32[32,32,256]{2,1,0:T(8,128)}, f32[32,32,256]{2,1,0:T(8,128)}) custom-call(f32[2,32,256]{2,1,0:T(8,128)} %broadcast_in_dim.13.cor_ref, f32[32,32,256]{2,1,0:T(8,128)} %ub_ref.1, f32[32,32,256]{2,1,0:T(8,128)} %vb_ref.1, f32[32,32,256]{2,1,0:T(8,128)} %tb_ref.1, ...), custom_call_target="tpu_custom_call" | custom-call | tf_op jit(solution)/shard_map/pallas_call | solution.py:510
  (4 shorter events, 0.0 us)
Async XLA Ops:
  5.6 8.0 %collective-permute-start.2 = (f32[5,32,256]{2,1,0:T(8,128)}, f32[5,32,256]{2,1,0:T(8,128)S(1)}, u32[]{:S(2)}, u32[]{:S(2)}) collective-permute-start(f32[5,32,256]{2,1,0:T(8,128)} %get-tuple-element.8), channel_id=1, source_target_pairs={{0,1},{16,17},{32,33},{48,49},{64,65},{80,81},{96,97},{112,113},{1... | collective-permute-start | bytes 491528 | tf_op jit(solution)/shard_map/ppermute | solution.py:175
  6.9 13.1 %collective-permute-start = (f32[5,32,256]{2,1,0:T(8,128)}, f32[5,32,256]{2,1,0:T(8,128)S(1)}, u32[]{:S(2)}, u32[]{:S(2)}) collective-permute-start(f32[5,32,256]{2,1,0:T(8,128)} %get-tuple-element.8), channel_id=1, source_target_pairs={{15,255},{31,239},{47,223},{63,207},{79,191},{95,175},{111,159},{1... | collective-permute-start | bytes 491528 | tf_op jit(solution)/shard_map/ppermute | solution.py:175
  11.9 8.7 %collective-permute-start.1 = (f32[5,32,256]{2,1,0:T(8,128)}, f32[5,32,256]{2,1,0:T(8,128)S(1)}, u32[]{:S(2)}, u32[]{:S(2)}) collective-permute-start(f32[5,32,256]{2,1,0:T(8,128)} %get-tuple-element.9), channel_id=1, source_target_pairs={{1,0},{17,16},{33,32},{49,48},{65,64},{81,80},{97,96},{113,112},{1... | collective-permute-start | bytes 491528 | tf_op jit(solution)/shard_map/ppermute | solution.py:175
  13.6 0.7 %copy-start = (f32[5,32,256]{2,1,0:T(8,128)}, f32[5,32,256]{2,1,0:T(8,128)S(1)}, u32[]{:S(2)}) copy-start(f32[5,32,256]{2,1,0:T(8,128)S(1)} %collective-permute-done.2.rs_ref) | copy-start | bytes 491524
  20.5 0.7 %copy-start.5 = (f32[5]{0:T(128)S(1)}, f32[5]{0:T(128)}, u32[]{:S(2)}) copy-start(f32[5]{0:T(128)} %constant.26.clone) | copy-start | bytes 64
  21.2 0.9 %copy-start.3 = (f32[5,32,32]{2,1,0:T(8,128)S(1)}, f32[5,32,32]{2,1,0:T(8,128)}, u32[]{:S(2)}) copy-start(f32[5,32,32]{2,1,0:T(8,128)} %get-tuple-element.11) | copy-start | bytes 61444
  21.2 0.9 %copy-start.4 = (f32[5,32,32]{2,1,0:T(8,128)S(1)}, f32[5,32,32]{2,1,0:T(8,128)}, u32[]{:S(2)}) copy-start(f32[5,32,32]{2,1,0:T(8,128)} %get-tuple-element.10) | copy-start | bytes 61444
  22.2 6.5 %collective-permute-start.4 = (f32[5,40,32]{2,1,0:T(8,128)S(1)}, f32[5,40,32]{2,1,0:T(8,128)S(1)}, u32[]{:S(2)}, u32[]{:S(2)}) collective-permute-start(f32[5,40,32]{2,1,0:T(8,128)S(1)} %get-tuple-element.16), channel_id=1, source_target_pairs={{0,240},{16,0},{32,16},{48,32},{64,48},{80,64},{96,80},{112,96},{1... | collective-permute-start | bytes 76808 | tf_op jit(solution)/shard_map/ppermute | solution.py:175
  26.5 6.2 %collective-permute-start.3 = (f32[5,40,32]{2,1,0:T(8,128)S(1)}, f32[5,40,32]{2,1,0:T(8,128)S(1)}, u32[]{:S(2)}, u32[]{:S(2)}) collective-permute-start(f32[5,40,32]{2,1,0:T(8,128)S(1)} %get-tuple-element.17), channel_id=1, source_target_pairs={{0,16},{16,32},{32,48},{48,64},{64,80},{80,96},{96,112},{112,128},... | collective-permute-start | bytes 76808 | tf_op jit(solution)/shard_map/ppermute | solution.py:175
  28.8 4.6 %copy-start.1 = (f32[5,40,32]{2,1,0:T(8,128)}, f32[5,40,32]{2,1,0:T(8,128)S(1)}, u32[]{:S(2)}) copy-start(f32[5,40,32]{2,1,0:T(8,128)S(1)} %collective-permute-done.4.te_ref) | copy-start | bytes 76804
  32.7 0.7 %copy-start.2 = (f32[5,40,32]{2,1,0:T(8,128)}, f32[5,40,32]{2,1,0:T(8,128)S(1)}, u32[]{:S(2)}) copy-start(f32[5,40,32]{2,1,0:T(8,128)S(1)} %collective-permute-done.3.tw_ref) | copy-start | bytes 76804

commit v9 on v7

--- a/solution.py
+++ b/solution.py
@@ -497,7 +497,7 @@
     row_index = (row_start + jnp.arange(rows, dtype=jnp.int32)).astype(jnp.float32)[:, None]
     coriolis_t = coriolis_max * (2.0 * (row_index + 0.5) / total_rows - 1.0)
     coriolis_v = coriolis_max * (2.0 * (row_index + 1.0) / total_rows - 1.0)
-    coriolis = jnp.broadcast_to(jnp.stack([coriolis_t, coriolis_v]), (2, rows, cols))
+    coriolis = jnp.stack([coriolis_t, coriolis_v])
 
     block = jax.ShapeDtypeStruct((levels, rows, cols), jnp.float32)
     main = pl.BlockSpec((chunk, rows, cols), lambda c: (c, 0, 0))
@@ -513,7 +513,7 @@
     return pl.pallas_call(
         stencil_kernel,
         grid=(levels // chunk,),
-        in_specs=[whole((2, rows, cols))]
+        in_specs=[whole((2, rows, 1))]
         + [main] * fields
         + [above] * fields
         + [below] * fields

time: 51.6 us -> 53.3 us (1.033)
  Pallas kernels: 22.9 us -> 24.7 us
  waiting for transfers between devices: 11.1 us -> 10.4 us
  local copies, waits for them, and re-layouts: 4.44 us -> 5.08 us
    pallas_call x1, Pallas kernels: 17.9 us -> 19.7 us  [per_device(): pl.pallas_call(stencil_kernel, grid=(levels // chunk,), in_specs=[whole((...]
    another operation x0 -> x1, local copies, waits for them, and re-layouts: none -> 0.7 us  [per_device(): coriolis = jnp.stack([coriolis_t, coriolis_v])]
    ppermute x5, waiting for transfers between devices: 11.1 us -> 10.4 us  [shift(): return lax.ppermute(value, ('lon', 'lat'), pairs)]
    broadcast_in_dim x1 -> x0, local copies, waits for them, and re-layouts: 0.69 us -> none  [per_device(): jnp.broadcast_to(jnp.stack([coriolis_t, coriolis_v]), (2, rows, cols))]
    unnamed x14, local copies, waits for them, and re-layouts: 1.95 us -> 2.58 us
  transfers between devices with their start and end apart: 5 -> 5, of which waited for: 4 -> 4; matrix products, arithmetic and copies ran while one was open for 3% -> 5% of each run, Pallas kernels for 0% -> 0%
where the time goes in v9:
time: 53.3 us; the launch traced here: 53 us
  Pallas kernels  24.7 us (46%)
  starting transfers between devices  11.9 us (22%)
  waiting for transfers between devices  10.4 us (20%)
  local copies, waits for them, and re-layouts  5.08 us (10%)
  between operations  0.74 us (1%)
    pallas_call x1, Pallas kernels, per_device(): pl.pallas_call(stencil_kernel, grid=(levels // chunk,), in_specs=[whole((...  19.7 us
    ppermute x5, starting transfers between devices, shift(): return lax.ppermute(value, ('lon', 'lat'), pairs)  11.9 us
    ppermute x5, waiting for transfers between devices, shift(): return lax.ppermute(value, ('lon', 'lat'), pairs)  10.4 us
    pallas_call x1, Pallas kernels, per_device(): pl.pallas_call(edge_kernel, grid=(levels // chunk,), in_specs=[pl.BlockSp...  4.97 us
    unnamed x14, local copies, waits for them, and re-layouts  2.58 us
  transfers between devices with their start and end apart: 5, of which 4 were waited for; matrix products, arithmetic and copies ran while one was open for 5% of the time, Pallas kernels for 0%

profile of v9, /device:TPU:228, one launch (start us, length us, event | category | flops | bytes accessed | tf_op | source)
XLA Modules:
  0.0 53.0 jit_solution(8148274716177635361)
XLA Ops:
  0.6 5.0 %shard_map.102 = (f32[5,32,256]{2,1,0:T(8,128)}, f32[5,32,256]{2,1,0:T(8,128)}, f32[5,32,32]{2,1,0:T(8,128)}, f32[5,32,32]{2,1,0:T(8,128)}) custom-call(f32[32,32,256]{2,1,0:T(8,128)} %ub_ref.1, f32[32,32,256]{2,1,0:T(8,128)} %vb_ref.1, f32[32,32,256]{2,1,0:T(8,128)} %tb_ref.1, f32[32,32,256]{2,1,0:T(8,128)} %sb_ref.1, s32[32,32,256]{2,1,0:T(8,128)} %wb_ref.1), custom_call_target="tpu_custom_call" | custom-call | tf_op jit(solution)/shard_map/pallas_call | solution.py:451
  5.6 1.3 %collective-permute-start.2 = (f32[5,32,256]{2,1,0:T(8,128)}, f32[5,32,256]{2,1,0:T(8,128)S(1)}, u32[]{:S(2)}, u32[]{:S(2)}) collective-permute-start(f32[5,32,256]{2,1,0:T(8,128)} %get-tuple-element.8), channel_id=1, source_target_pairs={{0,1},{16,17},{32,33},{48,49},{64,65},{80,81},{96,97},{112,113},{1... | collective-permute-start | bytes 491528 | tf_op jit(solution)/shard_map/ppermute | solution.py:175
  6.9 5.0 %collective-permute-start = (f32[5,32,256]{2,1,0:T(8,128)}, f32[5,32,256]{2,1,0:T(8,128)S(1)}, u32[]{:S(2)}, u32[]{:S(2)}) collective-permute-start(f32[5,32,256]{2,1,0:T(8,128)} %get-tuple-element.8), channel_id=1, source_target_pairs={{15,255},{31,239},{47,223},{63,207},{79,191},{95,175},{111,159},{1... | collective-permute-start | bytes 491528 | tf_op jit(solution)/shard_map/ppermute | solution.py:175
  11.9 1.3 %collective-permute-start.1 = (f32[5,32,256]{2,1,0:T(8,128)}, f32[5,32,256]{2,1,0:T(8,128)S(1)}, u32[]{:S(2)}, u32[]{:S(2)}) collective-permute-start(f32[5,32,256]{2,1,0:T(8,128)} %get-tuple-element.9), channel_id=1, source_target_pairs={{1,0},{17,16},{33,32},{49,48},{65,64},{81,80},{97,96},{113,112},{1... | collective-permute-start | bytes 491528 | tf_op jit(solution)/shard_map/ppermute | solution.py:175
  13.2 0.1 pad.7.clone
  13.3 0.3 collective-permute-done.2.rs_ref
  13.6 0.0 copy-start
  13.6 0.1 fusion
  13.7 0.6 %copy-done = f32[5,32,256]{2,1,0:T(8,128)} copy-done((f32[5,32,256]{2,1,0:T(8,128)}, f32[5,32,256]{2,1,0:T(8,128)S(1)}, u32[]{:S(2)}) %copy-start) | copy-done | bytes 163864
  14.3 0.1 copy.23
  14.4 0.1 copy.22
  14.5 5.5 %collective-permute-done = f32[5,32,256]{2,1,0:T(8,128)S(1)} collective-permute-done((f32[5,32,256]{2,1,0:T(8,128)}, f32[5,32,256]{2,1,0:T(8,128)S(1)}, u32[]{:S(2)}, u32[]{:S(2)}) %collective-permute-start) | collective-permute-done | bytes 163872 | tf_op jit(solution)/shard_map/ppermute | solution.py:175
  20.0 0.2 copy.16
  20.2 0.3 rev.3
  20.5 0.0 copy-start.5
  20.6 0.0 collective-permute-done.1
  20.6 0.2 copy.17
  20.8 0.4 copy-done.5
  21.2 0.0 copy-start.3
  21.2 0.0 copy-start.4
  21.2 0.1 multiply_select_fusion
  21.4 0.7 %copy-done.3 = f32[5,32,32]{2,1,0:T(8,128)S(1)} copy-done((f32[5,32,32]{2,1,0:T(8,128)S(1)}, f32[5,32,32]{2,1,0:T(8,128)}, u32[]{:S(2)}) %copy-start.3) | copy-done | bytes 20504
  22.1 0.0 copy-done.4
  22.1 0.1 maximum_maximum_fusion.1
  22.2 4.3 %collective-permute-start.4 = (f32[5,40,32]{2,1,0:T(8,128)S(1)}, f32[5,40,32]{2,1,0:T(8,128)S(1)}, u32[]{:S(2)}, u32[]{:S(2)}) collective-permute-start(f32[5,40,32]{2,1,0:T(8,128)S(1)} %get-tuple-element.16), channel_id=1, source_target_pairs={{0,240},{16,0},{32,16},{48,32},{64,48},{80,64},{96,80},{112,96},{1... | collective-permute-start | bytes 76808 | tf_op jit(solution)/shard_map/ppermute | solution.py:175
  26.5 0.0 collective-permute-start.3
  26.5 0.7 %copy.20.cor_ref = f32[2,32,1]{2,1,0:T(8,128)} copy(f32[2,32,1]{1,0,2:T(2,128)S(1)} %pad_maximum_fusion) | data formatting | bytes 512 | tf_op jit(solution)/shard_map/stack | solution.py:500
  27.2 0.9 %copy.21.rn_ref = f32[5,32,256]{2,1,0:T(8,128)} copy(f32[5,32,256]{1,2,0:T(8,128)S(1)} %multiply_select_fusion) | data formatting | bytes 327680 | tf_op jit(solution)/shard_map/jit(_where)/select_n | solution.py:484
  28.1 0.7 %collective-permute-done.4.te_ref = f32[5,40,32]{2,1,0:T(8,128)S(1)} collective-permute-done((f32[5,40,32]{2,1,0:T(8,128)S(1)}, f32[5,40,32]{2,1,0:T(8,128)S(1)}, u32[]{:S(2)}, u32[]{:S(2)}) %collective-permute-start.4) | collective-permute-done | bytes 25632 | tf_op jit(solution)/shard_map/ppermute | solution.py:175
  28.8 0.0 copy-start.1
  28.8 3.9 %collective-permute-done.3.tw_ref = f32[5,40,32]{2,1,0:T(8,128)S(1)} collective-permute-done((f32[5,40,32]{2,1,0:T(8,128)S(1)}, f32[5,40,32]{2,1,0:T(8,128)S(1)}, u32[]{:S(2)}, u32[]{:S(2)}) %collective-permute-start.3) | collective-permute-done | bytes 25632 | tf_op jit(solution)/shard_map/ppermute | solution.py:175
  32.7 0.0 copy-done.1
  32.7 0.0 copy-start.2
  32.7 0.6 %copy-done.2 = f32[5,40,32]{2,1,0:T(8,128)} copy-done((f32[5,40,32]{2,1,0:T(8,128)}, f32[5,40,32]{2,1,0:T(8,128)S(1)}, u32[]{:S(2)}) %copy-start.2) | copy-done | bytes 25624
  33.3 19.7 %shard_map.103 = (f32[32,32,256]{2,1,0:T(8,128)}, f32[32,32,256]{2,1,0:T(8,128)}, f32[32,32,256]{2,1,0:T(8,128)}, f32[32,32,256]{2,1,0:T(8,128)}) custom-call(f32[2,32,1]{2,1,0:T(8,128)} %copy.20.cor_ref, f32[32,32,256]{2,1,0:T(8,128)} %ub_ref.1, f32[32,32,256]{2,1,0:T(8,128)} %vb_ref.1, f32[32,32,256]{2,1,0:T(8,128)} %tb_ref.1, f32[32,32,256]{2,1,0:T(8,128)} %sb_ref.1, ...), custom_call_target="tpu_custom_call" | custom-call | tf_op jit(solution)/shard_map/pallas_call | solution.py:513
  (4 shorter events, 0.0 us)
Async XLA Ops:
  5.6 8.0 %collective-permute-start.2 = (f32[5,32,256]{2,1,0:T(8,128)}, f32[5,32,256]{2,1,0:T(8,128)S(1)}, u32[]{:S(2)}, u32[]{:S(2)}) collective-permute-start(f32[5,32,256]{2,1,0:T(8,128)} %get-tuple-element.8), channel_id=1, source_target_pairs={{0,1},{16,17},{32,33},{48,49},{64,65},{80,81},{96,97},{112,113},{1... | collective-permute-start | bytes 491528 | tf_op jit(solution)/shard_map/ppermute | solution.py:175
  6.9 13.1 %collective-permute-start = (f32[5,32,256]{2,1,0:T(8,128)}, f32[5,32,256]{2,1,0:T(8,128)S(1)}, u32[]{:S(2)}, u32[]{:S(2)}) collective-permute-start(f32[5,32,256]{2,1,0:T(8,128)} %get-tuple-element.8), channel_id=1, source_target_pairs={{15,255},{31,239},{47,223},{63,207},{79,191},{95,175},{111,159},{1... | collective-permute-start | bytes 491528 | tf_op jit(solution)/shard_map/ppermute | solution.py:175
  11.9 8.7 %collective-permute-start.1 = (f32[5,32,256]{2,1,0:T(8,128)}, f32[5,32,256]{2,1,0:T(8,128)S(1)}, u32[]{:S(2)}, u32[]{:S(2)}) collective-permute-start(f32[5,32,256]{2,1,0:T(8,128)} %get-tuple-element.9), channel_id=1, source_target_pairs={{1,0},{17,16},{33,32},{49,48},{65,64},{81,80},{97,96},{113,112},{1... | collective-permute-start | bytes 491528 | tf_op jit(solution)/shard_map/ppermute | solution.py:175
  13.6 0.7 %copy-start = (f32[5,32,256]{2,1,0:T(8,128)}, f32[5,32,256]{2,1,0:T(8,128)S(1)}, u32[]{:S(2)}) copy-start(f32[5,32,256]{2,1,0:T(8,128)S(1)} %collective-permute-done.2.rs_ref) | copy-start | bytes 491524
  20.5 0.7 %copy-start.5 = (f32[5]{0:T(128)S(1)}, f32[5]{0:T(128)}, u32[]{:S(2)}) copy-start(f32[5]{0:T(128)} %constant.26.clone) | copy-start | bytes 64
  21.2 0.9 %copy-start.3 = (f32[5,32,32]{2,1,0:T(8,128)S(1)}, f32[5,32,32]{2,1,0:T(8,128)}, u32[]{:S(2)}) copy-start(f32[5,32,32]{2,1,0:T(8,128)} %get-tuple-element.11) | copy-start | bytes 61444
  21.2 0.9 %copy-start.4 = (f32[5,32,32]{2,1,0:T(8,128)S(1)}, f32[5,32,32]{2,1,0:T(8,128)}, u32[]{:S(2)}) copy-start(f32[5,32,32]{2,1,0:T(8,128)} %get-tuple-element.10) | copy-start | bytes 61444
  22.2 6.5 %collective-permute-start.4 = (f32[5,40,32]{2,1,0:T(8,128)S(1)}, f32[5,40,32]{2,1,0:T(8,128)S(1)}, u32[]{:S(2)}, u32[]{:S(2)}) collective-permute-start(f32[5,40,32]{2,1,0:T(8,128)S(1)} %get-tuple-element.16), channel_id=1, source_target_pairs={{0,240},{16,0},{32,16},{48,32},{64,48},{80,64},{96,80},{112,96},{1... | collective-permute-start | bytes 76808 | tf_op jit(solution)/shard_map/ppermute | solution.py:175
  26.5 6.2 %collective-permute-start.3 = (f32[5,40,32]{2,1,0:T(8,128)S(1)}, f32[5,40,32]{2,1,0:T(8,128)S(1)}, u32[]{:S(2)}, u32[]{:S(2)}) collective-permute-start(f32[5,40,32]{2,1,0:T(8,128)S(1)} %get-tuple-element.17), channel_id=1, source_target_pairs={{0,16},{16,32},{32,48},{48,64},{64,80},{80,96},{96,112},{112,128},... | collective-permute-start | bytes 76808 | tf_op jit(solution)/shard_map/ppermute | solution.py:175
  28.8 3.9 %copy-start.1 = (f32[5,40,32]{2,1,0:T(8,128)}, f32[5,40,32]{2,1,0:T(8,128)S(1)}, u32[]{:S(2)}) copy-start(f32[5,40,32]{2,1,0:T(8,128)S(1)} %collective-permute-done.4.te_ref) | copy-start | bytes 76804
  32.7 0.6 %copy-start.2 = (f32[5,40,32]{2,1,0:T(8,128)}, f32[5,40,32]{2,1,0:T(8,128)S(1)}, u32[]{:S(2)}) copy-start(f32[5,40,32]{2,1,0:T(8,128)S(1)} %collective-permute-done.3.tw_ref) | copy-start | bytes 76804

commit v10 on v7

--- a/solution.py
+++ b/solution.py
@@ -175,10 +175,22 @@
     return lax.ppermute(value, ("lon", "lat"), pairs)
 
 
+def row_kernel(*refs):
+    fields = (len(refs) - 2) // 2
+    lows = refs[:fields]
+    highs = refs[fields : 2 * fields]
+    top_ref, bottom_ref = refs[2 * fields :]
+    chunk, tile, cols = lows[0].shape
+    for field in range(fields):
+        for r in range(chunk):
+            top_ref[field, r : r + 1, :] = highs[field][r][tile - 1 : tile, :].astype(jnp.float32)
+            bottom_ref[field, r : r + 1, :] = lows[field][r][0:1, :].astype(jnp.float32)
+
+
 def edge_kernel(*refs):
-    fields = len(refs) - 4
+    fields = len(refs) - 2
     sources = refs[:fields]
-    top_ref, bottom_ref, west_ref, east_ref = refs[fields:]
+    west_ref, east_ref = refs[fields:]
     chunk, rows, cols = sources[0].shape
     levels = west_ref.shape[2]
     step = pl.program_id(0)
@@ -194,8 +206,6 @@
         east = east_ref[field]
         for r in range(chunk):
             x = source[r].astype(jnp.float32)
-            top_ref[field, r : r + 1, :] = x[rows - 1 : rows, :]
-            bottom_ref[field, r : r + 1, :] = x[0:1, :]
             here = lane == step * chunk + r
             west = jnp.where(here, x[:, 0:1], west)
             east = jnp.where(here, x[:, cols - 1 : cols], east)
@@ -448,14 +458,24 @@
     chunk = 8 if levels % 8 == 0 else levels
     row_block = pl.BlockSpec((fields, chunk, cols), lambda c: (0, c, 0))
     col_block = pl.BlockSpec((fields, rows, levels), lambda c: (0, 0, 0))
-    top, bottom, west_col, east_col = pl.pallas_call(
+    tile = 8
+    top, bottom = pl.pallas_call(
+        row_kernel,
+        grid=(levels // chunk,),
+        in_specs=[pl.BlockSpec((chunk, tile, cols), lambda c: (c, 0, 0))] * fields
+        + [pl.BlockSpec((chunk, tile, cols), lambda c: (c, rows // tile - 1, 0))] * fields,
+        out_specs=(row_block, row_block),
+        out_shape=(
+            jax.ShapeDtypeStruct((fields, levels, cols), jnp.float32),
+            jax.ShapeDtypeStruct((fields, levels, cols), jnp.float32),
+        ),
+    )(*inputs, *inputs)
+    west_col, east_col = pl.pallas_call(
         edge_kernel,
         grid=(levels // chunk,),
         in_specs=[pl.BlockSpec((chunk, rows, cols), lambda c: (c, 0, 0))] * fields,
-        out_specs=(row_block, row_block, col_block, col_block),
+        out_specs=(col_block, col_block),
         out_shape=(
-            jax.ShapeDtypeStruct((fields, levels, cols), jnp.float32),
-            jax.ShapeDtypeStruct((fields, levels, cols), jnp.float32),
             jax.ShapeDtypeStruct((fields, rows, levels), jnp.float32),
             jax.ShapeDtypeStruct((fields, rows, levels), jnp.float32),
         ),

time: 51.6 us -> 51.8 us (level)
  the two profiles are of different devices: /device:TPU:228 before, /device:TPU:4 now
where the time goes in v10:
time: 51.8 us; the launch traced here: 51.3 us
  Pallas kernels  26.5 us (51%)
  starting transfers between devices  14.1 us (27%)
  waiting for transfers between devices  5.3 us (10%)
  local copies, waits for them, and re-layouts  4.5 us (9%)
  between operations  0.74 us (1%)
    pallas_call x1, Pallas kernels, per_device(): pl.pallas_call(stencil_kernel, grid=(levels // chunk,), in_specs=[whole((...  17.9 us
    ppermute x5, starting transfers between devices, shift(): return lax.ppermute(value, ('lon', 'lat'), pairs)  14.1 us
    ppermute x5, waiting for transfers between devices, shift(): return lax.ppermute(value, ('lon', 'lat'), pairs)  5.3 us
    pallas_call x1, Pallas kernels, per_device(): pl.pallas_call(edge_kernel, grid=(levels // chunk,), in_specs=[pl.BlockSp...  4.94 us
    pallas_call x1, Pallas kernels, per_device(): pl.pallas_call(row_kernel, grid=(levels // chunk,), in_specs=[pl.BlockSpe...  3.59 us
    unnamed x14, local copies, waits for them, and re-layouts  1.96 us
  transfers between devices with their start and end apart: 5, of which 2 were waited for; matrix products, arithmetic and copies ran while one was open for 4% of the time, Pallas kernels for 10%

profile of v10, /device:TPU:4, one launch (start us, length us, event | category | flops | bytes accessed | tf_op | source)
XLA Modules:
  0.0 51.3 jit_solution(12893769060411507492)
XLA Ops:
  0.6 3.6 %shard_map.102 = (f32[5,32,256]{2,1,0:T(8,128)}, f32[5,32,256]{2,1,0:T(8,128)}) custom-call(f32[32,32,256]{2,1,0:T(8,128)} %ub_ref.1, f32[32,32,256]{2,1,0:T(8,128)} %vb_ref.1, f32[32,32,256]{2,1,0:T(8,128)} %tb_ref.1, f32[32,32,256]{2,1,0:T(8,128)} %sb_ref.1, s32[32,32,256]{2,1,0:T(8,128)} %wb_ref.1, f32[32,32,256]{2,1,0:T(8,128)} %ub_ref.1, ...), custom_call_target="tpu_custom_call" | custom-call | tf_op jit(solution)/shard_map/pallas_call | solution.py:462
  4.2 3.8 %collective-permute-start.2 = (f32[5,32,256]{2,1,0:T(8,128)}, f32[5,32,256]{2,1,0:T(8,128)S(1)}, u32[]{:S(2)}, u32[]{:S(2)}) collective-permute-start(f32[5,32,256]{2,1,0:T(8,128)} %get-tuple-element.8), channel_id=1, source_target_pairs={{0,1},{16,17},{32,33},{48,49},{64,65},{80,81},{96,97},{112,113},{1... | collective-permute-start | bytes 491528 | tf_op jit(solution)/shard_map/ppermute | solution.py:175
  8.1 0.7 %collective-permute-start = (f32[5,32,256]{2,1,0:T(8,128)}, f32[5,32,256]{2,1,0:T(8,128)S(1)}, u32[]{:S(2)}, u32[]{:S(2)}) collective-permute-start(f32[5,32,256]{2,1,0:T(8,128)} %get-tuple-element.8), channel_id=1, source_target_pairs={{15,255},{31,239},{47,223},{63,207},{79,191},{95,175},{111,159},{1... | collective-permute-start | bytes 491528 | tf_op jit(solution)/shard_map/ppermute | solution.py:175
  8.7 5.8 %collective-permute-start.1 = (f32[5,32,256]{2,1,0:T(8,128)}, f32[5,32,256]{2,1,0:T(8,128)S(1)}, u32[]{:S(2)}, u32[]{:S(2)}) collective-permute-start(f32[5,32,256]{2,1,0:T(8,128)} %get-tuple-element.9), channel_id=1, source_target_pairs={{1,0},{17,16},{33,32},{49,48},{65,64},{81,80},{97,96},{113,112},{1... | collective-permute-start | bytes 491528 | tf_op jit(solution)/shard_map/ppermute | solution.py:175
  14.5 4.9 %shard_map.103 = (f32[5,32,32]{2,1,0:T(8,128)}, f32[5,32,32]{2,1,0:T(8,128)}) custom-call(f32[32,32,256]{2,1,0:T(8,128)} %ub_ref.1, f32[32,32,256]{2,1,0:T(8,128)} %vb_ref.1, f32[32,32,256]{2,1,0:T(8,128)} %tb_ref.1, f32[32,32,256]{2,1,0:T(8,128)} %sb_ref.1, s32[32,32,256]{2,1,0:T(8,128)} %wb_ref.1), custom_call_target="tpu_custom_call" | custom-call | tf_op jit(solution)/shard_map/pallas_call | solution.py:473
  19.5 0.1 pad.7.clone
  19.6 0.0 collective-permute-done.2.rs_ref
  19.6 0.0 copy-start
  19.6 0.1 fusion
  19.7 0.6 %copy-done = f32[5,32,256]{2,1,0:T(8,128)} copy-done((f32[5,32,256]{2,1,0:T(8,128)}, f32[5,32,256]{2,1,0:T(8,128)S(1)}, u32[]{:S(2)}) %copy-start) | copy-done | bytes 163864
  20.2 0.1 copy.22
  20.3 0.1 copy.21
  20.4 0.0 collective-permute-done
  20.4 0.2 copy.16
  20.7 0.3 rev.3
  21.0 0.0 copy-start.5
  21.0 0.0 collective-permute-done.1
  21.0 0.2 copy.17
  21.3 0.4 copy-done.5
  21.7 0.0 copy-start.3
  21.7 0.0 copy-start.4
  21.7 0.1 multiply_select_fusion
  21.8 0.7 %copy-done.3 = f32[5,32,32]{2,1,0:T(8,128)S(1)} copy-done((f32[5,32,32]{2,1,0:T(8,128)S(1)}, f32[5,32,32]{2,1,0:T(8,128)}, u32[]{:S(2)}) %copy-start.3) | copy-done | bytes 20504
  22.6 0.0 copy-done.4
  22.6 0.1 maximum_maximum_fusion.1
  22.7 3.8 %collective-permute-start.4 = (f32[5,40,32]{2,1,0:T(8,128)S(1)}, f32[5,40,32]{2,1,0:T(8,128)S(1)}, u32[]{:S(2)}, u32[]{:S(2)}) collective-permute-start(f32[5,40,32]{2,1,0:T(8,128)S(1)} %get-tuple-element.16), channel_id=1, source_target_pairs={{0,240},{16,0},{32,16},{48,32},{64,48},{80,64},{96,80},{112,96},{1... | collective-permute-start | bytes 76808 | tf_op jit(solution)/shard_map/ppermute | solution.py:175
  26.5 0.0 collective-permute-start.3
  26.5 0.9 %copy.20.rn_ref = f32[5,32,256]{2,1,0:T(8,128)} copy(f32[5,32,256]{1,2,0:T(8,128)S(1)} %multiply_select_fusion) | data formatting | bytes 327680 | tf_op jit(solution)/shard_map/jit(_where)/select_n | solution.py:504
  27.4 1.4 %collective-permute-done.4.te_ref = f32[5,40,32]{2,1,0:T(8,128)S(1)} collective-permute-done((f32[5,40,32]{2,1,0:T(8,128)S(1)}, f32[5,40,32]{2,1,0:T(8,128)S(1)}, u32[]{:S(2)}, u32[]{:S(2)}) %collective-permute-start.4) | collective-permute-done | bytes 25632 | tf_op jit(solution)/shard_map/ppermute | solution.py:175
  28.7 0.0 copy-start.1
  28.7 3.9 %collective-permute-done.3.tw_ref = f32[5,40,32]{2,1,0:T(8,128)S(1)} collective-permute-done((f32[5,40,32]{2,1,0:T(8,128)S(1)}, f32[5,40,32]{2,1,0:T(8,128)S(1)}, u32[]{:S(2)}, u32[]{:S(2)}) %collective-permute-start.3) | collective-permute-done | bytes 25632 | tf_op jit(solution)/shard_map/ppermute | solution.py:175
  32.7 0.0 copy-start.2
  32.7 0.7 %broadcast_in_dim.13.cor_ref = f32[2,32,256]{2,1,0:T(8,128)} broadcast(f32[2,32]{1,0:T(2,128)S(1)} %maximum_bitcast_fusion), dimensions={0,1} | broadcast | bytes 65792 | tf_op jit(solution)/shard_map/broadcast_in_dim | solution.py:520
  33.4 0.0 copy-done.1
  33.4 0.0 copy-done.2
  33.4 17.9 %shard_map.104 = (f32[32,32,256]{2,1,0:T(8,128)}, f32[32,32,256]{2,1,0:T(8,128)}, f32[32,32,256]{2,1,0:T(8,128)}, f32[32,32,256]{2,1,0:T(8,128)}) custom-call(f32[2,32,256]{2,1,0:T(8,128)} %broadcast_in_dim.13.cor_ref, f32[32,32,256]{2,1,0:T(8,128)} %ub_ref.1, f32[32,32,256]{2,1,0:T(8,128)} %vb_ref.1, f32[32,32,256]{2,1,0:T(8,128)} %tb_ref.1, ...), custom_call_target="tpu_custom_call" | custom-call | tf_op jit(solution)/shard_map/pallas_call | solution.py:533
  (4 shorter events, 0.0 us)
Async XLA Ops:
  4.2 15.4 %collective-permute-start.2 = (f32[5,32,256]{2,1,0:T(8,128)}, f32[5,32,256]{2,1,0:T(8,128)S(1)}, u32[]{:S(2)}, u32[]{:S(2)}) collective-permute-start(f32[5,32,256]{2,1,0:T(8,128)} %get-tuple-element.8), channel_id=1, source_target_pairs={{0,1},{16,17},{32,33},{48,49},{64,65},{80,81},{96,97},{112,113},{1... | collective-permute-start | bytes 491528 | tf_op jit(solution)/shard_map/ppermute | solution.py:175
  8.1 12.4 %collective-permute-start = (f32[5,32,256]{2,1,0:T(8,128)}, f32[5,32,256]{2,1,0:T(8,128)S(1)}, u32[]{:S(2)}, u32[]{:S(2)}) collective-permute-start(f32[5,32,256]{2,1,0:T(8,128)} %get-tuple-element.8), channel_id=1, source_target_pairs={{15,255},{31,239},{47,223},{63,207},{79,191},{95,175},{111,159},{1... | collective-permute-start | bytes 491528 | tf_op jit(solution)/shard_map/ppermute | solution.py:175
  8.7 12.3 %collective-permute-start.1 = (f32[5,32,256]{2,1,0:T(8,128)}, f32[5,32,256]{2,1,0:T(8,128)S(1)}, u32[]{:S(2)}, u32[]{:S(2)}) collective-permute-start(f32[5,32,256]{2,1,0:T(8,128)} %get-tuple-element.9), channel_id=1, source_target_pairs={{1,0},{17,16},{33,32},{49,48},{65,64},{81,80},{97,96},{113,112},{1... | collective-permute-start | bytes 491528 | tf_op jit(solution)/shard_map/ppermute | solution.py:175
  19.6 0.7 %copy-start = (f32[5,32,256]{2,1,0:T(8,128)}, f32[5,32,256]{2,1,0:T(8,128)S(1)}, u32[]{:S(2)}) copy-start(f32[5,32,256]{2,1,0:T(8,128)S(1)} %collective-permute-done.2.rs_ref) | copy-start | bytes 491524
  21.0 0.7 %copy-start.5 = (f32[5]{0:T(128)S(1)}, f32[5]{0:T(128)}, u32[]{:S(2)}) copy-start(f32[5]{0:T(128)} %constant.26.clone) | copy-start | bytes 64
  21.7 0.9 %copy-start.3 = (f32[5,32,32]{2,1,0:T(8,128)S(1)}, f32[5,32,32]{2,1,0:T(8,128)}, u32[]{:S(2)}) copy-start(f32[5,32,32]{2,1,0:T(8,128)} %get-tuple-element.11) | copy-start | bytes 61444
  21.7 0.9 %copy-start.4 = (f32[5,32,32]{2,1,0:T(8,128)S(1)}, f32[5,32,32]{2,1,0:T(8,128)}, u32[]{:S(2)}) copy-start(f32[5,32,32]{2,1,0:T(8,128)} %get-tuple-element.10) | copy-start | bytes 61444
  22.7 6.0 %collective-permute-start.4 = (f32[5,40,32]{2,1,0:T(8,128)S(1)}, f32[5,40,32]{2,1,0:T(8,128)S(1)}, u32[]{:S(2)}, u32[]{:S(2)}) collective-permute-start(f32[5,40,32]{2,1,0:T(8,128)S(1)} %get-tuple-element.16), channel_id=1, source_target_pairs={{0,240},{16,0},{32,16},{48,32},{64,48},{80,64},{96,80},{112,96},{1... | collective-permute-start | bytes 76808 | tf_op jit(solution)/shard_map/ppermute | solution.py:175
  26.5 6.2 %collective-permute-start.3 = (f32[5,40,32]{2,1,0:T(8,128)S(1)}, f32[5,40,32]{2,1,0:T(8,128)S(1)}, u32[]{:S(2)}, u32[]{:S(2)}) collective-permute-start(f32[5,40,32]{2,1,0:T(8,128)S(1)} %get-tuple-element.17), channel_id=1, source_target_pairs={{0,16},{16,32},{32,48},{48,64},{64,80},{80,96},{96,112},{112,128},... | collective-permute-start | bytes 76808 | tf_op jit(solution)/shard_map/ppermute | solution.py:175
  28.7 4.7 %copy-start.1 = (f32[5,40,32]{2,1,0:T(8,128)}, f32[5,40,32]{2,1,0:T(8,128)S(1)}, u32[]{:S(2)}) copy-start(f32[5,40,32]{2,1,0:T(8,128)S(1)} %collective-permute-done.4.te_ref) | copy-start | bytes 76804
  32.7 0.7 %copy-start.2 = (f32[5,40,32]{2,1,0:T(8,128)}, f32[5,40,32]{2,1,0:T(8,128)S(1)}, u32[]{:S(2)}) copy-start(f32[5,40,32]{2,1,0:T(8,128)S(1)} %collective-permute-done.3.tw_ref) | copy-start | bytes 76804

commit v11 on v10

--- a/solution.py
+++ b/solution.py
@@ -461,10 +461,13 @@
     tile = 8
     top, bottom = pl.pallas_call(
         row_kernel,
-        grid=(levels // chunk,),
-        in_specs=[pl.BlockSpec((chunk, tile, cols), lambda c: (c, 0, 0))] * fields
-        + [pl.BlockSpec((chunk, tile, cols), lambda c: (c, rows // tile - 1, 0))] * fields,
-        out_specs=(row_block, row_block),
+        grid=(1,),
+        in_specs=[pl.BlockSpec((levels, tile, cols), lambda c: (0, 0, 0))] * fields
+        + [pl.BlockSpec((levels, tile, cols), lambda c: (0, rows // tile - 1, 0))] * fields,
+        out_specs=(
+            pl.BlockSpec((fields, levels, cols), lambda c: (0, 0, 0)),
+            pl.BlockSpec((fields, levels, cols), lambda c: (0, 0, 0)),
+        ),
         out_shape=(
             jax.ShapeDtypeStruct((fields, levels, cols), jnp.float32),
             jax.ShapeDtypeStruct((fields, levels, cols), jnp.float32),

time: 51.8 us -> 50.6 us (0.977)
  Pallas kernels: 26.5 us -> 25.5 us
    pallas_call x1, Pallas kernels: 3.59 us -> 2.6 us  [per_device(): pl.pallas_call(row_kernel, grid=(1,), in_specs=[pl.BlockSpec((levels, til...]
where the time goes in v11:
time: 50.6 us; the launch traced here: 50.3 us
  Pallas kernels  25.5 us (50%)
  starting transfers between devices  14.1 us (28%)
  waiting for transfers between devices  5.3 us (10%)
  local copies, waits for them, and re-layouts  4.5 us (9%)
  between operations  0.74 us (1%)
    pallas_call x1, Pallas kernels, per_device(): pl.pallas_call(stencil_kernel, grid=(levels // chunk,), in_specs=[whole((...  17.9 us
    ppermute x5, starting transfers between devices, shift(): return lax.ppermute(value, ('lon', 'lat'), pairs)  14.1 us
    ppermute x5, waiting for transfers between devices, shift(): return lax.ppermute(value, ('lon', 'lat'), pairs)  5.3 us
    pallas_call x1, Pallas kernels, per_device(): pl.pallas_call(edge_kernel, grid=(levels // chunk,), in_specs=[pl.BlockSp...  4.94 us
    pallas_call x1, Pallas kernels, per_device(): pl.pallas_call(row_kernel, grid=(1,), in_specs=[pl.BlockSpec((levels, til...  2.6 us
    unnamed x14, local copies, waits for them, and re-layouts  1.96 us
  transfers between devices with their start and end apart: 5, of which 2 were waited for; matrix products, arithmetic and copies ran while one was open for 4% of the time, Pallas kernels for 10%

profile of v11, /device:TPU:4, one launch (start us, length us, event | category | flops | bytes accessed | tf_op | source)
XLA Modules:
  0.0 50.3 jit_solution(15065257429080130665)
XLA Ops:
  0.6 2.6 %shard_map.102 = (f32[5,32,256]{2,1,0:T(8,128)}, f32[5,32,256]{2,1,0:T(8,128)}) custom-call(f32[32,32,256]{2,1,0:T(8,128)} %ub_ref.1, f32[32,32,256]{2,1,0:T(8,128)} %vb_ref.1, f32[32,32,256]{2,1,0:T(8,128)} %tb_ref.1, f32[32,32,256]{2,1,0:T(8,128)} %sb_ref.1, s32[32,32,256]{2,1,0:T(8,128)} %wb_ref.1, f32[32,32,256]{2,1,0:T(8,128)} %ub_ref.1, ...), custom_call_target="tpu_custom_call" | custom-call | tf_op jit(solution)/shard_map/pallas_call | solution.py:462
  3.2 3.8 %collective-permute-start.2 = (f32[5,32,256]{2,1,0:T(8,128)}, f32[5,32,256]{2,1,0:T(8,128)S(1)}, u32[]{:S(2)}, u32[]{:S(2)}) collective-permute-start(f32[5,32,256]{2,1,0:T(8,128)} %get-tuple-element.8), channel_id=1, source_target_pairs={{0,1},{16,17},{32,33},{48,49},{64,65},{80,81},{96,97},{112,113},{1... | collective-permute-start | bytes 491528 | tf_op jit(solution)/shard_map/ppermute | solution.py:175
  7.1 0.7 %collective-permute-start = (f32[5,32,256]{2,1,0:T(8,128)}, f32[5,32,256]{2,1,0:T(8,128)S(1)}, u32[]{:S(2)}, u32[]{:S(2)}) collective-permute-start(f32[5,32,256]{2,1,0:T(8,128)} %get-tuple-element.8), channel_id=1, source_target_pairs={{15,255},{31,239},{47,223},{63,207},{79,191},{95,175},{111,159},{1... | collective-permute-start | bytes 491528 | tf_op jit(solution)/shard_map/ppermute | solution.py:175
  7.7 5.8 %collective-permute-start.1 = (f32[5,32,256]{2,1,0:T(8,128)}, f32[5,32,256]{2,1,0:T(8,128)S(1)}, u32[]{:S(2)}, u32[]{:S(2)}) collective-permute-start(f32[5,32,256]{2,1,0:T(8,128)} %get-tuple-element.9), channel_id=1, source_target_pairs={{1,0},{17,16},{33,32},{49,48},{65,64},{81,80},{97,96},{113,112},{1... | collective-permute-start | bytes 491528 | tf_op jit(solution)/shard_map/ppermute | solution.py:175
  13.5 4.9 %shard_map.103 = (f32[5,32,32]{2,1,0:T(8,128)}, f32[5,32,32]{2,1,0:T(8,128)}) custom-call(f32[32,32,256]{2,1,0:T(8,128)} %ub_ref.1, f32[32,32,256]{2,1,0:T(8,128)} %vb_ref.1, f32[32,32,256]{2,1,0:T(8,128)} %tb_ref.1, f32[32,32,256]{2,1,0:T(8,128)} %sb_ref.1, s32[32,32,256]{2,1,0:T(8,128)} %wb_ref.1), custom_call_target="tpu_custom_call" | custom-call | tf_op jit(solution)/shard_map/pallas_call | solution.py:476
  18.5 0.1 pad.7.clone
  18.6 0.0 collective-permute-done.2.rs_ref
  18.6 0.0 copy-start
  18.6 0.1 fusion
  18.7 0.6 %copy-done = f32[5,32,256]{2,1,0:T(8,128)} copy-done((f32[5,32,256]{2,1,0:T(8,128)}, f32[5,32,256]{2,1,0:T(8,128)S(1)}, u32[]{:S(2)}) %copy-start) | copy-done | bytes 163864
  19.2 0.1 copy.22
  19.3 0.1 copy.21
  19.4 0.0 collective-permute-done
  19.4 0.2 copy.16
  19.7 0.3 rev.3
  20.0 0.0 copy-start.5
  20.0 0.0 collective-permute-done.1
  20.0 0.2 copy.17
  20.3 0.4 copy-done.5
  20.7 0.0 copy-start.3
  20.7 0.0 copy-start.4
  20.7 0.1 multiply_select_fusion
  20.8 0.7 %copy-done.3 = f32[5,32,32]{2,1,0:T(8,128)S(1)} copy-done((f32[5,32,32]{2,1,0:T(8,128)S(1)}, f32[5,32,32]{2,1,0:T(8,128)}, u32[]{:S(2)}) %copy-start.3) | copy-done | bytes 20504
  21.6 0.0 copy-done.4
  21.6 0.1 maximum_maximum_fusion.1
  21.7 3.8 %collective-permute-start.4 = (f32[5,40,32]{2,1,0:T(8,128)S(1)}, f32[5,40,32]{2,1,0:T(8,128)S(1)}, u32[]{:S(2)}, u32[]{:S(2)}) collective-permute-start(f32[5,40,32]{2,1,0:T(8,128)S(1)} %get-tuple-element.16), channel_id=1, source_target_pairs={{0,240},{16,0},{32,16},{48,32},{64,48},{80,64},{96,80},{112,96},{1... | collective-permute-start | bytes 76808 | tf_op jit(solution)/shard_map/ppermute | solution.py:175
  25.5 0.0 collective-permute-start.3
  25.5 0.9 %copy.20.rn_ref = f32[5,32,256]{2,1,0:T(8,128)} copy(f32[5,32,256]{1,2,0:T(8,128)S(1)} %multiply_select_fusion) | data formatting | bytes 327680 | tf_op jit(solution)/shard_map/jit(_where)/select_n | solution.py:507
  26.4 1.4 %collective-permute-done.4.te_ref = f32[5,40,32]{2,1,0:T(8,128)S(1)} collective-permute-done((f32[5,40,32]{2,1,0:T(8,128)S(1)}, f32[5,40,32]{2,1,0:T(8,128)S(1)}, u32[]{:S(2)}, u32[]{:S(2)}) %collective-permute-start.4) | collective-permute-done | bytes 25632 | tf_op jit(solution)/shard_map/ppermute | solution.py:175
  27.7 0.0 copy-start.1
  27.7 3.9 %collective-permute-done.3.tw_ref = f32[5,40,32]{2,1,0:T(8,128)S(1)} collective-permute-done((f32[5,40,32]{2,1,0:T(8,128)S(1)}, f32[5,40,32]{2,1,0:T(8,128)S(1)}, u32[]{:S(2)}, u32[]{:S(2)}) %collective-permute-start.3) | collective-permute-done | bytes 25632 | tf_op jit(solution)/shard_map/ppermute | solution.py:175
  31.7 0.0 copy-start.2
  31.7 0.7 %broadcast_in_dim.13.cor_ref = f32[2,32,256]{2,1,0:T(8,128)} broadcast(f32[2,32]{1,0:T(2,128)S(1)} %maximum_bitcast_fusion), dimensions={0,1} | broadcast | bytes 65792 | tf_op jit(solution)/shard_map/broadcast_in_dim | solution.py:523
  32.4 0.0 copy-done.1
  32.4 0.0 copy-done.2
  32.4 17.9 %shard_map.104 = (f32[32,32,256]{2,1,0:T(8,128)}, f32[32,32,256]{2,1,0:T(8,128)}, f32[32,32,256]{2,1,0:T(8,128)}, f32[32,32,256]{2,1,0:T(8,128)}) custom-call(f32[2,32,256]{2,1,0:T(8,128)} %broadcast_in_dim.13.cor_ref, f32[32,32,256]{2,1,0:T(8,128)} %ub_ref.1, f32[32,32,256]{2,1,0:T(8,128)} %vb_ref.1, f32[32,32,256]{2,1,0:T(8,128)} %tb_ref.1, ...), custom_call_target="tpu_custom_call" | custom-call | tf_op jit(solution)/shard_map/pallas_call | solution.py:536
  (4 shorter events, 0.0 us)
Async XLA Ops:
  3.2 15.3 %collective-permute-start.2 = (f32[5,32,256]{2,1,0:T(8,128)}, f32[5,32,256]{2,1,0:T(8,128)S(1)}, u32[]{:S(2)}, u32[]{:S(2)}) collective-permute-start(f32[5,32,256]{2,1,0:T(8,128)} %get-tuple-element.8), channel_id=1, source_target_pairs={{0,1},{16,17},{32,33},{48,49},{64,65},{80,81},{96,97},{112,113},{1... | collective-permute-start | bytes 491528 | tf_op jit(solution)/shard_map/ppermute | solution.py:175
  7.1 12.4 %collective-permute-start = (f32[5,32,256]{2,1,0:T(8,128)}, f32[5,32,256]{2,1,0:T(8,128)S(1)}, u32[]{:S(2)}, u32[]{:S(2)}) collective-permute-start(f32[5,32,256]{2,1,0:T(8,128)} %get-tuple-element.8), channel_id=1, source_target_pairs={{15,255},{31,239},{47,223},{63,207},{79,191},{95,175},{111,159},{1... | collective-permute-start | bytes 491528 | tf_op jit(solution)/shard_map/ppermute | solution.py:175
  7.7 12.3 %collective-permute-start.1 = (f32[5,32,256]{2,1,0:T(8,128)}, f32[5,32,256]{2,1,0:T(8,128)S(1)}, u32[]{:S(2)}, u32[]{:S(2)}) collective-permute-start(f32[5,32,256]{2,1,0:T(8,128)} %get-tuple-element.9), channel_id=1, source_target_pairs={{1,0},{17,16},{33,32},{49,48},{65,64},{81,80},{97,96},{113,112},{1... | collective-permute-start | bytes 491528 | tf_op jit(solution)/shard_map/ppermute | solution.py:175
  18.6 0.7 %copy-start = (f32[5,32,256]{2,1,0:T(8,128)}, f32[5,32,256]{2,1,0:T(8,128)S(1)}, u32[]{:S(2)}) copy-start(f32[5,32,256]{2,1,0:T(8,128)S(1)} %collective-permute-done.2.rs_ref) | copy-start | bytes 491524
  20.0 0.7 %copy-start.5 = (f32[5]{0:T(128)S(1)}, f32[5]{0:T(128)}, u32[]{:S(2)}) copy-start(f32[5]{0:T(128)} %constant.26.clone) | copy-start | bytes 64
  20.7 0.9 %copy-start.3 = (f32[5,32,32]{2,1,0:T(8,128)S(1)}, f32[5,32,32]{2,1,0:T(8,128)}, u32[]{:S(2)}) copy-start(f32[5,32,32]{2,1,0:T(8,128)} %get-tuple-element.11) | copy-start | bytes 61444
  20.7 0.9 %copy-start.4 = (f32[5,32,32]{2,1,0:T(8,128)S(1)}, f32[5,32,32]{2,1,0:T(8,128)}, u32[]{:S(2)}) copy-start(f32[5,32,32]{2,1,0:T(8,128)} %get-tuple-element.10) | copy-start | bytes 61444
  21.7 6.0 %collective-permute-start.4 = (f32[5,40,32]{2,1,0:T(8,128)S(1)}, f32[5,40,32]{2,1,0:T(8,128)S(1)}, u32[]{:S(2)}, u32[]{:S(2)}) collective-permute-start(f32[5,40,32]{2,1,0:T(8,128)S(1)} %get-tuple-element.16), channel_id=1, source_target_pairs={{0,240},{16,0},{32,16},{48,32},{64,48},{80,64},{96,80},{112,96},{1... | collective-permute-start | bytes 76808 | tf_op jit(solution)/shard_map/ppermute | solution.py:175
  25.5 6.2 %collective-permute-start.3 = (f32[5,40,32]{2,1,0:T(8,128)S(1)}, f32[5,40,32]{2,1,0:T(8,128)S(1)}, u32[]{:S(2)}, u32[]{:S(2)}) collective-permute-start(f32[5,40,32]{2,1,0:T(8,128)S(1)} %get-tuple-element.17), channel_id=1, source_target_pairs={{0,16},{16,32},{32,48},{48,64},{64,80},{80,96},{96,112},{112,128},... | collective-permute-start | bytes 76808 | tf_op jit(solution)/shard_map/ppermute | solution.py:175
  27.7 4.7 %copy-start.1 = (f32[5,40,32]{2,1,0:T(8,128)}, f32[5,40,32]{2,1,0:T(8,128)S(1)}, u32[]{:S(2)}) copy-start(f32[5,40,32]{2,1,0:T(8,128)S(1)} %collective-permute-done.4.te_ref) | copy-start | bytes 76804
  31.7 0.7 %copy-start.2 = (f32[5,40,32]{2,1,0:T(8,128)}, f32[5,40,32]{2,1,0:T(8,128)S(1)}, u32[]{:S(2)}) copy-start(f32[5,40,32]{2,1,0:T(8,128)S(1)} %collective-permute-done.3.tw_ref) | copy-start | bytes 76804

commit v12 on v11

--- a/solution.py
+++ b/solution.py
@@ -214,9 +214,9 @@
 
 
 def stencil_kernel(
-    cor_ref, u_ref, v_ref, t_ref, s_ref, wet_ref, ua_ref, va_ref, ta_ref, sa_ref, wa_ref,
-    ub_ref, vb_ref, tb_ref, sb_ref, wb_ref, clc_ref, rn_ref, rs_ref, tw_ref, te_ref,
-    east_ref, north_ref, temp_ref, salt_ref, p_ref, pe_ref, pn_ref,
+    top_ref, cor_ref, u_ref, v_ref, t_ref, s_ref, wet_ref, ua_ref, va_ref, ta_ref, sa_ref, wa_ref,
+    ub_ref, vb_ref, tb_ref, sb_ref, wb_ref, clc_ref, hn_ref, fold_ref, rs_ref, tw_ref, te_ref,
+    east_ref, north_ref, temp_ref, salt_ref, p_ref, pe_ref, pn_ref, rn_ref,
 ):
     chunk, rows, cols = u_ref.shape
     levels = tw_ref.shape[2]
@@ -252,6 +252,20 @@
     row_east = row_lane == cols - 1
     row_west = row_lane == 0
     pick_lane = lax.broadcasted_iota(jnp.int32, tw_ref.shape[1:], 1)
+    flip = (
+        lax.broadcasted_iota(jnp.int32, (cols, cols), 0)
+        + lax.broadcasted_iota(jnp.int32, (cols, cols), 1)
+        == cols - 1
+    ).astype(jnp.float32)
+    for field in range(rn_ref.shape[0]):
+        mirrored = jnp.dot(
+            fold_ref[field],
+            flip,
+            precision=lax.Precision.HIGHEST,
+            preferred_element_type=jnp.float32,
+        )
+        sign = -1.0 if field < 2 else 1.0
+        rn_ref[field] = jnp.where(top_ref[0] == 1, sign * mirrored, hn_ref[field])
     cor_t = cor_ref[0]
     cor_v = cor_ref[1]
     count = clc_ref[...]
@@ -504,13 +518,14 @@
     fold_row = shift(top, mirror)
     sign = jnp.array([-1.0, -1.0, 1.0, 1.0, 1.0], dtype=jnp.float32)[:, None, None]
     is_top = lax.axis_index("lat") == lax.axis_size("lat") - 1
-    halo_north = jnp.where(is_top, sign * fold_row[:, :, ::-1], halo_north)
+    north_first = jnp.where(is_top, sign[:, :, 0] * fold_row[:, :, -1], halo_north[:, :, 0])
+    north_last = jnp.where(is_top, sign[:, :, 0] * fold_row[:, :, 0], halo_north[:, :, -1])
     pad = jnp.zeros((fields, 6, levels), jnp.float32)
     west_tall = jnp.concatenate(
-        [west_col, halo_south[:, None, :, 0], halo_north[:, None, :, 0], pad], axis=1
+        [west_col, halo_south[:, None, :, 0], north_first[:, None, :], pad], axis=1
     )
     east_tall = jnp.concatenate(
-        [east_col, halo_south[:, None, :, -1], halo_north[:, None, :, -1], pad], axis=1
+        [east_col, halo_south[:, None, :, -1], north_last[:, None, :], pad], axis=1
     )
     halo_west = shift(east_tall, east_of)
     halo_east = shift(west_tall, west_of)
@@ -536,25 +551,29 @@
     return pl.pallas_call(
         stencil_kernel,
         grid=(levels // chunk,),
-        in_specs=[whole((2, rows, cols))]
+        in_specs=[pl.BlockSpec(memory_space=pltpu.SMEM), whole((2, rows, cols))]
         + [main] * fields
         + [above] * fields
         + [below] * fields
-        + [whole((rows, cols)), halo_row, halo_row, whole(halo_west.shape), whole(halo_east.shape)],
+        + [whole((rows, cols)), halo_row, halo_row, halo_row, whole(halo_west.shape)]
+        + [whole(halo_east.shape)],
         out_specs=(main, main, main, main),
         out_shape=(block, block, block, block),
         scratch_shapes=[
             pltpu.VMEM((rows, cols), jnp.float32),
             pltpu.VMEM((rows, cols), jnp.float32),
             pltpu.VMEM((1, cols), jnp.float32),
+            pltpu.VMEM((fields, chunk, cols), jnp.float32),
         ],
     )(
+        is_top.astype(jnp.int32).reshape(1),
         coriolis,
         *inputs,
         *inputs,
         *inputs,
         column_layer_count,
         halo_north,
+        fold_row,
         halo_south,
         halo_west,
         halo_east,

time: 50.6 us -> 56.2 us (1.11)
  waiting for transfers between devices: 5.3 us -> 9.11 us
  Pallas kernels: 25.5 us -> 28.8 us
  starting transfers between devices: 14.1 us -> 13.2 us
    ppermute x5, waiting for transfers between devices: 5.3 us -> 9.11 us  [shift(): return lax.ppermute(value, ('lon', 'lat'), pairs)]
    pallas_call x1, Pallas kernels: 17.9 us -> 21.3 us  [per_device(): pl.pallas_call(stencil_kernel, grid=(levels // chunk,), in_specs=[pl.Bloc...]
    unnamed x14 -> x22, local copies, waits for them, and re-layouts: 1.96 us -> 2.96 us
    ppermute x5, starting transfers between devices: 14.1 us -> 13.2 us  [shift(): return lax.ppermute(value, ('lon', 'lat'), pairs)]
    select_n x1 -> x0, local copies, waits for them, and re-layouts: 0.89 us -> none  [per_device(): halo_north = jnp.where(is_top, sign * fold_row[:, :, ::-1], halo_north)]
  transfers between devices with their start and end apart: 5 -> 5, of which waited for: 2 -> 3; matrix products, arithmetic and copies ran while one was open for 4% -> 1% of each run, Pallas kernels for 10% -> 9%
where the time goes in v12:
time: 56.2 us; the launch traced here: 56 us
  Pallas kernels  28.8 us (51%)
  starting transfers between devices  13.2 us (23%)
  waiting for transfers between devices  9.11 us (16%)
  local copies, waits for them, and re-layouts  4 us (7%)
  between operations  0.71 us (1%)
    pallas_call x1, Pallas kernels, per_device(): pl.pallas_call(stencil_kernel, grid=(levels // chunk,), in_specs=[pl.Bloc...  21.3 us
    ppermute x5, starting transfers between devices, shift(): return lax.ppermute(value, ('lon', 'lat'), pairs)  13.2 us
    ppermute x5, waiting for transfers between devices, shift(): return lax.ppermute(value, ('lon', 'lat'), pairs)  9.11 us
    pallas_call x1, Pallas kernels, per_device(): pl.pallas_call(edge_kernel, grid=(levels // chunk,), in_specs=[pl.BlockSp...  4.94 us
    unnamed x22, local copies, waits for them, and re-layouts  2.96 us
    pallas_call x1, Pallas kernels, per_device(): pl.pallas_call(row_kernel, grid=(1,), in_specs=[pl.BlockSpec((levels, til...  2.6 us
  transfers between devices with their start and end apart: 5, of which 3 were waited for; matrix products, arithmetic and copies ran while one was open for 1% of the time, Pallas kernels for 9%

profile of v12, /device:TPU:4, one launch (start us, length us, event | category | flops | bytes accessed | tf_op | source)
XLA Modules:
  0.0 56.0 jit_solution(6233462600113683984)
XLA Ops:
  0.6 2.6 %shard_map.102 = (f32[5,32,256]{2,1,0:T(8,128)}, f32[5,32,256]{2,1,0:T(8,128)}) custom-call(f32[32,32,256]{2,1,0:T(8,128)} %ub_ref.1, f32[32,32,256]{2,1,0:T(8,128)} %vb_ref.1, f32[32,32,256]{2,1,0:T(8,128)} %tb_ref.1, f32[32,32,256]{2,1,0:T(8,128)} %sb_ref.1, s32[32,32,256]{2,1,0:T(8,128)} %wb_ref.1, f32[32,32,256]{2,1,0:T(8,128)} %ub_ref.1, ...), custom_call_target="tpu_custom_call" | custom-call | tf_op jit(solution)/shard_map/pallas_call | solution.py:476
  3.2 7.7 %collective-permute-start = (f32[5,32,256]{2,1,0:T(8,128)}, f32[5,32,256]{2,1,0:T(8,128)S(1)}, u32[]{:S(2)}, u32[]{:S(2)}) collective-permute-start(f32[5,32,256]{2,1,0:T(8,128)} %get-tuple-element.8), channel_id=1, source_target_pairs={{1,0},{17,16},{33,32},{49,48},{65,64},{81,80},{97,96},{113,112},{1... | collective-permute-start | bytes 491528 | tf_op jit(solution)/shard_map/ppermute | solution.py:175
  10.9 1.9 %collective-permute-start.2 = (f32[5,32,256]{2,1,0:T(8,128)}, f32[5,32,256]{2,1,0:T(8,128)S(1)}, u32[]{:S(2)}, u32[]{:S(2)}) collective-permute-start(f32[5,32,256]{2,1,0:T(8,128)} %get-tuple-element.9), channel_id=1, source_target_pairs={{0,1},{16,17},{32,33},{48,49},{64,65},{80,81},{96,97},{112,113},{1... | collective-permute-start | bytes 491528 | tf_op jit(solution)/shard_map/ppermute | solution.py:175
  12.9 0.7 %collective-permute-start.1 = (f32[5,32,256]{2,1,0:T(8,128)}, f32[5,32,256]{2,1,0:T(8,128)S(1)}, u32[]{:S(2)}, u32[]{:S(2)}) collective-permute-start(f32[5,32,256]{2,1,0:T(8,128)} %get-tuple-element.9), channel_id=1, source_target_pairs={{15,255},{31,239},{47,223},{63,207},{79,191},{95,175},{111,159},{1... | collective-permute-start | bytes 491528 | tf_op jit(solution)/shard_map/ppermute | solution.py:175
  13.5 4.9 %shard_map.103 = (f32[5,32,32]{2,1,0:T(8,128)}, f32[5,32,32]{2,1,0:T(8,128)}) custom-call(f32[32,32,256]{2,1,0:T(8,128)} %ub_ref.1, f32[32,32,256]{2,1,0:T(8,128)} %vb_ref.1, f32[32,32,256]{2,1,0:T(8,128)} %tb_ref.1, f32[32,32,256]{2,1,0:T(8,128)} %sb_ref.1, s32[32,32,256]{2,1,0:T(8,128)} %wb_ref.1), custom_call_target="tpu_custom_call" | custom-call | tf_op jit(solution)/shard_map/pallas_call | solution.py:490
  18.5 0.1 pad.7.clone
  18.6 0.0 collective-permute-done.hn_ref
  18.6 0.0 copy-start
  18.6 0.1 fusion.2
  18.7 0.6 %copy-done = f32[5,32,256]{2,1,0:T(8,128)} copy-done((f32[5,32,256]{2,1,0:T(8,128)}, f32[5,32,256]{2,1,0:T(8,128)S(1)}, u32[]{:S(2)}) %copy-start) | copy-done | bytes 163864
  19.2 0.1 copy.28
  19.3 0.1 copy.25
  19.4 2.9 %collective-permute-done.2.rs_ref = f32[5,32,256]{2,1,0:T(8,128)S(1)} collective-permute-done((f32[5,32,256]{2,1,0:T(8,128)}, f32[5,32,256]{2,1,0:T(8,128)S(1)}, u32[]{:S(2)}, u32[]{:S(2)}) %collective-permute-start.2) | collective-permute-done | bytes 163872 | tf_op jit(solution)/shard_map/ppermute | solution.py:175
  22.4 0.0 copy-start.1
  22.4 0.1 fusion
  22.4 0.6 %copy-done.1 = f32[5,32,256]{2,1,0:T(8,128)} copy-done((f32[5,32,256]{2,1,0:T(8,128)}, f32[5,32,256]{2,1,0:T(8,128)S(1)}, u32[]{:S(2)}) %copy-start.1) | copy-done | bytes 163864
  23.0 0.1 copy.26
  23.1 0.1 copy.23
  23.2 0.0 collective-permute-done.1.fold_ref
  23.2 0.0 copy-start.2
  23.2 0.1 fusion.1
  23.3 0.6 %copy-done.2 = f32[5,32,256]{2,1,0:T(8,128)} copy-done((f32[5,32,256]{2,1,0:T(8,128)}, f32[5,32,256]{2,1,0:T(8,128)S(1)}, u32[]{:S(2)}) %copy-start.2) | copy-done | bytes 163864
  23.9 0.0 copy-start.5
  23.9 0.0 copy-start.6
  23.9 0.1 copy.27
  24.0 0.0 copy-start.7
  24.0 0.1 copy.24
  24.1 0.6 %copy-done.7 = f32[5]{0:T(128)S(1)} copy-done((f32[5]{0:T(128)S(1)}, f32[5]{0:T(128)}, u32[]{:S(2)}) %copy-start.7) | copy-done | bytes 44
  24.7 0.1 broadcast_select_fusion
  24.7 0.0 copy-done.5
  24.8 0.0 copy-done.6
  24.8 0.1 maximum_maximum_fusion.1
  24.9 2.9 %collective-permute-start.4 = (f32[5,40,32]{2,1,0:T(8,128)S(1)}, f32[5,40,32]{2,1,0:T(8,128)S(1)}, u32[]{:S(2)}, u32[]{:S(2)}) collective-permute-start(f32[5,40,32]{2,1,0:T(8,128)S(1)} %get-tuple-element.18), channel_id=1, source_target_pairs={{0,240},{16,0},{32,16},{48,32},{64,48},{80,64},{96,80},{112,96},{1... | collective-permute-start | bytes 76808 | tf_op jit(solution)/shard_map/ppermute | solution.py:175
  27.8 0.0 collective-permute-start.3
  27.8 2.2 %collective-permute-done.4.te_ref = f32[5,40,32]{2,1,0:T(8,128)S(1)} collective-permute-done((f32[5,40,32]{2,1,0:T(8,128)S(1)}, f32[5,40,32]{2,1,0:T(8,128)S(1)}, u32[]{:S(2)}, u32[]{:S(2)}) %collective-permute-start.4) | collective-permute-done | bytes 25632 | tf_op jit(solution)/shard_map/ppermute | solution.py:175
  30.0 0.0 copy-start.3
  30.0 3.9 %collective-permute-done.3.tw_ref = f32[5,40,32]{2,1,0:T(8,128)S(1)} collective-permute-done((f32[5,40,32]{2,1,0:T(8,128)S(1)}, f32[5,40,32]{2,1,0:T(8,128)S(1)}, u32[]{:S(2)}, u32[]{:S(2)}) %collective-permute-start.3) | collective-permute-done | bytes 25632 | tf_op jit(solution)/shard_map/ppermute | solution.py:175
  34.0 0.0 copy-start.4
  34.0 0.7 %broadcast_in_dim.14.cor_ref = f32[2,32,256]{2,1,0:T(8,128)} broadcast(f32[2,32]{1,0:T(2,128)S(1)} %maximum_bitcast_fusion), dimensions={0,1} | broadcast | bytes 65792 | tf_op jit(solution)/shard_map/broadcast_in_dim | solution.py:538
  34.7 0.0 copy-done.3
  34.7 0.0 copy-done.4
  34.7 21.3 %shard_map.104 = (f32[32,32,256]{2,1,0:T(8,128)}, f32[32,32,256]{2,1,0:T(8,128)}, f32[32,32,256]{2,1,0:T(8,128)}, f32[32,32,256]{2,1,0:T(8,128)}) custom-call(s32[1]{0:T(128)} %bitcast.top_ref, f32[2,32,256]{2,1,0:T(8,128)} %broadcast_in_dim.14.cor_ref, f32[32,32,256]{2,1,0:T(8,128)} %ub_ref.1, f32[32,32,256]{2,1,0:T(8,128)} %vb_ref.1, ...), custom_call_target="tpu_custom_call" | custom-call | tf_op jit(solution)/shard_map/pallas_call | solution.py:551
  (3 shorter events, 0.0 us)
Async XLA Ops:
  3.2 15.3 %collective-permute-start = (f32[5,32,256]{2,1,0:T(8,128)}, f32[5,32,256]{2,1,0:T(8,128)S(1)}, u32[]{:S(2)}, u32[]{:S(2)}) collective-permute-start(f32[5,32,256]{2,1,0:T(8,128)} %get-tuple-element.8), channel_id=1, source_target_pairs={{1,0},{17,16},{33,32},{49,48},{65,64},{81,80},{97,96},{113,112},{1... | collective-permute-start | bytes 491528 | tf_op jit(solution)/shard_map/ppermute | solution.py:175
  10.9 11.4 %collective-permute-start.2 = (f32[5,32,256]{2,1,0:T(8,128)}, f32[5,32,256]{2,1,0:T(8,128)S(1)}, u32[]{:S(2)}, u32[]{:S(2)}) collective-permute-start(f32[5,32,256]{2,1,0:T(8,128)} %get-tuple-element.9), channel_id=1, source_target_pairs={{0,1},{16,17},{32,33},{48,49},{64,65},{80,81},{96,97},{112,113},{1... | collective-permute-start | bytes 491528 | tf_op jit(solution)/shard_map/ppermute | solution.py:175
  12.9 10.3 %collective-permute-start.1 = (f32[5,32,256]{2,1,0:T(8,128)}, f32[5,32,256]{2,1,0:T(8,128)S(1)}, u32[]{:S(2)}, u32[]{:S(2)}) collective-permute-start(f32[5,32,256]{2,1,0:T(8,128)} %get-tuple-element.9), channel_id=1, source_target_pairs={{15,255},{31,239},{47,223},{63,207},{79,191},{95,175},{111,159},{1... | collective-permute-start | bytes 491528 | tf_op jit(solution)/shard_map/ppermute | solution.py:175
  18.6 0.7 %copy-start = (f32[5,32,256]{2,1,0:T(8,128)}, f32[5,32,256]{2,1,0:T(8,128)S(1)}, u32[]{:S(2)}) copy-start(f32[5,32,256]{2,1,0:T(8,128)S(1)} %collective-permute-done.hn_ref) | copy-start | bytes 491524
  22.4 0.7 %copy-start.1 = (f32[5,32,256]{2,1,0:T(8,128)}, f32[5,32,256]{2,1,0:T(8,128)S(1)}, u32[]{:S(2)}) copy-start(f32[5,32,256]{2,1,0:T(8,128)S(1)} %collective-permute-done.2.rs_ref) | copy-start | bytes 491524
  23.2 0.7 %copy-start.2 = (f32[5,32,256]{2,1,0:T(8,128)}, f32[5,32,256]{2,1,0:T(8,128)S(1)}, u32[]{:S(2)}) copy-start(f32[5,32,256]{2,1,0:T(8,128)S(1)} %collective-permute-done.1.fold_ref) | copy-start | bytes 491524
  23.9 0.9 %copy-start.5 = (f32[5,32,32]{2,1,0:T(8,128)S(1)}, f32[5,32,32]{2,1,0:T(8,128)}, u32[]{:S(2)}) copy-start(f32[5,32,32]{2,1,0:T(8,128)} %get-tuple-element.11) | copy-start | bytes 61444
  23.9 0.9 %copy-start.6 = (f32[5,32,32]{2,1,0:T(8,128)S(1)}, f32[5,32,32]{2,1,0:T(8,128)}, u32[]{:S(2)}) copy-start(f32[5,32,32]{2,1,0:T(8,128)} %get-tuple-element.10) | copy-start | bytes 61444
  24.0 0.7 %copy-start.7 = (f32[5]{0:T(128)S(1)}, f32[5]{0:T(128)}, u32[]{:S(2)}) copy-start(f32[5]{0:T(128)} %constant.26.clone) | copy-start | bytes 64
  24.9 5.1 %collective-permute-start.4 = (f32[5,40,32]{2,1,0:T(8,128)S(1)}, f32[5,40,32]{2,1,0:T(8,128)S(1)}, u32[]{:S(2)}, u32[]{:S(2)}) collective-permute-start(f32[5,40,32]{2,1,0:T(8,128)S(1)} %get-tuple-element.18), channel_id=1, source_target_pairs={{0,240},{16,0},{32,16},{48,32},{64,48},{80,64},{96,80},{112,96},{1... | collective-permute-start | bytes 76808 | tf_op jit(solution)/shard_map/ppermute | solution.py:175
  27.8 6.2 %collective-permute-start.3 = (f32[5,40,32]{2,1,0:T(8,128)S(1)}, f32[5,40,32]{2,1,0:T(8,128)S(1)}, u32[]{:S(2)}, u32[]{:S(2)}) collective-permute-start(f32[5,40,32]{2,1,0:T(8,128)S(1)} %get-tuple-element.19), channel_id=1, source_target_pairs={{0,16},{16,32},{32,48},{48,64},{64,80},{80,96},{96,112},{112,128},... | collective-permute-start | bytes 76808 | tf_op jit(solution)/shard_map/ppermute | solution.py:175
  30.0 4.7 %copy-start.3 = (f32[5,40,32]{2,1,0:T(8,128)}, f32[5,40,32]{2,1,0:T(8,128)S(1)}, u32[]{:S(2)}) copy-start(f32[5,40,32]{2,1,0:T(8,128)S(1)} %collective-permute-done.4.te_ref) | copy-start | bytes 76804
  34.0 0.7 %copy-start.4 = (f32[5,40,32]{2,1,0:T(8,128)}, f32[5,40,32]{2,1,0:T(8,128)S(1)}, u32[]{:S(2)}) copy-start(f32[5,40,32]{2,1,0:T(8,128)S(1)} %collective-permute-done.3.tw_ref) | copy-start | bytes 76804

commit v13 on v11

--- a/solution.py
+++ b/solution.py
@@ -1,3 +1,5 @@
+import functools
+
 import jax
 import jax.numpy as jnp
 from jax import lax
@@ -214,9 +216,9 @@
 
 
 def stencil_kernel(
-    cor_ref, u_ref, v_ref, t_ref, s_ref, wet_ref, ua_ref, va_ref, ta_ref, sa_ref, wa_ref,
+    meta_ref, u_ref, v_ref, t_ref, s_ref, wet_ref, ua_ref, va_ref, ta_ref, sa_ref, wa_ref,
     ub_ref, vb_ref, tb_ref, sb_ref, wb_ref, clc_ref, rn_ref, rs_ref, tw_ref, te_ref,
-    east_ref, north_ref, temp_ref, salt_ref, p_ref, pe_ref, pn_ref,
+    east_ref, north_ref, temp_ref, salt_ref, p_ref, pe_ref, pn_ref, *, total_rows,
 ):
     chunk, rows, cols = u_ref.shape
     levels = tw_ref.shape[2]
@@ -252,8 +254,15 @@
     row_east = row_lane == cols - 1
     row_west = row_lane == 0
     pick_lane = lax.broadcasted_iota(jnp.int32, tw_ref.shape[1:], 1)
-    cor_t = cor_ref[0]
-    cor_v = cor_ref[1]
+    row_index = (meta_ref[0] * rows + sub).astype(jnp.float32)
+
+    def per_total(x):
+        if total_rows & (total_rows - 1) == 0:
+            return x * (1.0 / total_rows)
+        return x / total_rows
+
+    cor_t = coriolis_max * (per_total(2.0 * (row_index + 0.5)) - 1.0)
+    cor_v = coriolis_max * (per_total(2.0 * (row_index + 1.0)) - 1.0)
     count = clc_ref[...]
 
     def east(x, col):
@@ -520,7 +529,7 @@
     row_index = (row_start + jnp.arange(rows, dtype=jnp.int32)).astype(jnp.float32)[:, None]
     coriolis_t = coriolis_max * (2.0 * (row_index + 0.5) / total_rows - 1.0)
     coriolis_v = coriolis_max * (2.0 * (row_index + 1.0) / total_rows - 1.0)
-    coriolis = jnp.broadcast_to(jnp.stack([coriolis_t, coriolis_v]), (2, rows, cols))
+    meta = lax.axis_index("lat").reshape(1)
 
     block = jax.ShapeDtypeStruct((levels, rows, cols), jnp.float32)
     main = pl.BlockSpec((chunk, rows, cols), lambda c: (c, 0, 0))
@@ -534,9 +543,9 @@
 
     halo_row = pl.BlockSpec((fields, chunk, cols), lambda c: (0, c, 0))
     return pl.pallas_call(
-        stencil_kernel,
+        functools.partial(stencil_kernel, total_rows=total_rows),
         grid=(levels // chunk,),
-        in_specs=[whole((2, rows, cols))]
+        in_specs=[pl.BlockSpec(memory_space=pltpu.SMEM)]
         + [main] * fields
         + [above] * fields
         + [below] * fields
@@ -549,7 +558,7 @@
             pltpu.VMEM((1, cols), jnp.float32),
         ],
     )(
-        coriolis,
+        meta.astype(jnp.int32),
         *inputs,
         *inputs,
         *inputs,

time: 50.6 us -> 50.6 us (level)
    broadcast_in_dim x1 -> x0, local copies, waits for them, and re-layouts: 0.71 us -> none  [per_device(): jnp.broadcast_to(jnp.stack([coriolis_t, coriolis_v]), (2, rows, cols))]
    unnamed x14, local copies, waits for them, and re-layouts: 1.96 us -> 2.58 us
where the time goes in v13:
time: 50.6 us; the launch traced here: 50.3 us
  Pallas kernels  25.5 us (50%)
  starting transfers between devices  14.1 us (28%)
  waiting for transfers between devices  5.32 us (11%)
  local copies, waits for them, and re-layouts  4.4 us (9%)
  between operations  0.73 us (1%)
    pallas_call x1, Pallas kernels, per_device(): pl.pallas_call(functools.partial(stencil_kernel, total_rows=total_rows),...  18 us
    ppermute x5, starting transfers between devices, shift(): return lax.ppermute(value, ('lon', 'lat'), pairs)  14.1 us
    ppermute x5, waiting for transfers between devices, shift(): return lax.ppermute(value, ('lon', 'lat'), pairs)  5.32 us
    pallas_call x1, Pallas kernels, per_device(): pl.pallas_call(edge_kernel, grid=(levels // chunk,), in_specs=[pl.BlockSp...  4.94 us
    pallas_call x1, Pallas kernels, per_device(): pl.pallas_call(row_kernel, grid=(1,), in_specs=[pl.BlockSpec((levels, til...  2.6 us
    unnamed x14, local copies, waits for them, and re-layouts  2.58 us
  transfers between devices with their start and end apart: 5, of which 2 were waited for; matrix products, arithmetic and copies ran while one was open for 4% of the time, Pallas kernels for 10%

profile of v13, /device:TPU:4, one launch (start us, length us, event | category | flops | bytes accessed | tf_op | source)
XLA Modules:
  0.0 50.3 jit_solution(5215102450045511500)
XLA Ops:
  0.6 2.6 %shard_map.102 = (f32[5,32,256]{2,1,0:T(8,128)}, f32[5,32,256]{2,1,0:T(8,128)}) custom-call(f32[32,32,256]{2,1,0:T(8,128)} %ub_ref.1, f32[32,32,256]{2,1,0:T(8,128)} %vb_ref.1, f32[32,32,256]{2,1,0:T(8,128)} %tb_ref.1, f32[32,32,256]{2,1,0:T(8,128)} %sb_ref.1, s32[32,32,256]{2,1,0:T(8,128)} %wb_ref.1, f32[32,32,256]{2,1,0:T(8,128)} %ub_ref.1, ...), custom_call_target="tpu_custom_call" | custom-call | tf_op jit(solution)/shard_map/pallas_call | solution.py:471
  3.2 3.8 %collective-permute-start.2 = (f32[5,32,256]{2,1,0:T(8,128)}, f32[5,32,256]{2,1,0:T(8,128)S(1)}, u32[]{:S(2)}, u32[]{:S(2)}) collective-permute-start(f32[5,32,256]{2,1,0:T(8,128)} %get-tuple-element.8), channel_id=1, source_target_pairs={{0,1},{16,17},{32,33},{48,49},{64,65},{80,81},{96,97},{112,113},{1... | collective-permute-start | bytes 491528 | tf_op jit(solution)/shard_map/ppermute | solution.py:177
  7.1 0.7 %collective-permute-start = (f32[5,32,256]{2,1,0:T(8,128)}, f32[5,32,256]{2,1,0:T(8,128)S(1)}, u32[]{:S(2)}, u32[]{:S(2)}) collective-permute-start(f32[5,32,256]{2,1,0:T(8,128)} %get-tuple-element.8), channel_id=1, source_target_pairs={{15,255},{31,239},{47,223},{63,207},{79,191},{95,175},{111,159},{1... | collective-permute-start | bytes 491528 | tf_op jit(solution)/shard_map/ppermute | solution.py:177
  7.7 5.8 %collective-permute-start.1 = (f32[5,32,256]{2,1,0:T(8,128)}, f32[5,32,256]{2,1,0:T(8,128)S(1)}, u32[]{:S(2)}, u32[]{:S(2)}) collective-permute-start(f32[5,32,256]{2,1,0:T(8,128)} %get-tuple-element.9), channel_id=1, source_target_pairs={{1,0},{17,16},{33,32},{49,48},{65,64},{81,80},{97,96},{113,112},{1... | collective-permute-start | bytes 491528 | tf_op jit(solution)/shard_map/ppermute | solution.py:177
  13.5 4.9 %shard_map.103 = (f32[5,32,32]{2,1,0:T(8,128)}, f32[5,32,32]{2,1,0:T(8,128)}) custom-call(f32[32,32,256]{2,1,0:T(8,128)} %ub_ref.1, f32[32,32,256]{2,1,0:T(8,128)} %vb_ref.1, f32[32,32,256]{2,1,0:T(8,128)} %tb_ref.1, f32[32,32,256]{2,1,0:T(8,128)} %sb_ref.1, s32[32,32,256]{2,1,0:T(8,128)} %wb_ref.1), custom_call_target="tpu_custom_call" | custom-call | tf_op jit(solution)/shard_map/pallas_call | solution.py:485
  18.5 0.1 pad.7.clone
  18.6 0.0 collective-permute-done.2.rs_ref
  18.6 0.0 copy-start
  18.6 0.1 fusion
  18.7 0.6 %copy-done = f32[5,32,256]{2,1,0:T(8,128)} copy-done((f32[5,32,256]{2,1,0:T(8,128)}, f32[5,32,256]{2,1,0:T(8,128)S(1)}, u32[]{:S(2)}) %copy-start) | copy-done | bytes 163864
  19.2 0.1 copy.22
  19.3 0.1 copy.21
  19.4 0.0 collective-permute-done
  19.4 0.2 copy.16
  19.7 0.3 rev.3
  20.0 0.0 copy-start.5
  20.0 0.0 collective-permute-done.1
  20.0 0.2 copy.17
  20.2 0.4 copy-done.5
  20.6 0.0 copy-start.3
  20.6 0.0 copy-start.4
  20.6 0.1 multiply_select_fusion
  20.8 0.7 %copy-done.3 = f32[5,32,32]{2,1,0:T(8,128)S(1)} copy-done((f32[5,32,32]{2,1,0:T(8,128)S(1)}, f32[5,32,32]{2,1,0:T(8,128)}, u32[]{:S(2)}) %copy-start.3) | copy-done | bytes 20504
  21.5 0.0 copy-done.4
  21.6 0.1 maximum_maximum_fusion.1
  21.7 3.8 %collective-permute-start.4 = (f32[5,40,32]{2,1,0:T(8,128)S(1)}, f32[5,40,32]{2,1,0:T(8,128)S(1)}, u32[]{:S(2)}, u32[]{:S(2)}) collective-permute-start(f32[5,40,32]{2,1,0:T(8,128)S(1)} %get-tuple-element.16), channel_id=1, source_target_pairs={{0,240},{16,0},{32,16},{48,32},{64,48},{80,64},{96,80},{112,96},{1... | collective-permute-start | bytes 76808 | tf_op jit(solution)/shard_map/ppermute | solution.py:177
  25.4 0.0 collective-permute-start.3
  25.4 0.9 %copy.20.rn_ref = f32[5,32,256]{2,1,0:T(8,128)} copy(f32[5,32,256]{1,2,0:T(8,128)S(1)} %multiply_select_fusion) | data formatting | bytes 327680 | tf_op jit(solution)/shard_map/jit(_where)/select_n | solution.py:516
  26.3 1.4 %collective-permute-done.4.te_ref = f32[5,40,32]{2,1,0:T(8,128)S(1)} collective-permute-done((f32[5,40,32]{2,1,0:T(8,128)S(1)}, f32[5,40,32]{2,1,0:T(8,128)S(1)}, u32[]{:S(2)}, u32[]{:S(2)}) %collective-permute-start.4) | collective-permute-done | bytes 25632 | tf_op jit(solution)/shard_map/ppermute | solution.py:177
  27.7 0.0 copy-start.1
  27.7 3.9 %collective-permute-done.3.tw_ref = f32[5,40,32]{2,1,0:T(8,128)S(1)} collective-permute-done((f32[5,40,32]{2,1,0:T(8,128)S(1)}, f32[5,40,32]{2,1,0:T(8,128)S(1)}, u32[]{:S(2)}, u32[]{:S(2)}) %collective-permute-start.3) | collective-permute-done | bytes 25632 | tf_op jit(solution)/shard_map/ppermute | solution.py:177
  31.6 0.0 copy-start.2
  31.6 0.0 copy-done.1
  31.6 0.6 %copy-done.2 = f32[5,40,32]{2,1,0:T(8,128)} copy-done((f32[5,40,32]{2,1,0:T(8,128)}, f32[5,40,32]{2,1,0:T(8,128)S(1)}, u32[]{:S(2)}) %copy-start.2) | copy-done | bytes 25624
  32.3 18.0 %shard_map.104 = (f32[32,32,256]{2,1,0:T(8,128)}, f32[32,32,256]{2,1,0:T(8,128)}, f32[32,32,256]{2,1,0:T(8,128)}, f32[32,32,256]{2,1,0:T(8,128)}) custom-call(s32[1]{0:T(128)} %bitcast.meta_ref, f32[32,32,256]{2,1,0:T(8,128)} %ub_ref.1, f32[32,32,256]{2,1,0:T(8,128)} %vb_ref.1, f32[32,32,256]{2,1,0:T(8,128)} %tb_ref.1, f32[32,32,256]{2,1,0:T(8,128)} %sb_ref.1, ...), custom_call_target="tpu_custom_call" | custom-call | tf_op jit(solution)/shard_map/pallas_call | solution.py:545
  (2 shorter events, 0.0 us)
Async XLA Ops:
  3.2 15.3 %collective-permute-start.2 = (f32[5,32,256]{2,1,0:T(8,128)}, f32[5,32,256]{2,1,0:T(8,128)S(1)}, u32[]{:S(2)}, u32[]{:S(2)}) collective-permute-start(f32[5,32,256]{2,1,0:T(8,128)} %get-tuple-element.8), channel_id=1, source_target_pairs={{0,1},{16,17},{32,33},{48,49},{64,65},{80,81},{96,97},{112,113},{1... | collective-permute-start | bytes 491528 | tf_op jit(solution)/shard_map/ppermute | solution.py:177
  7.1 12.4 %collective-permute-start = (f32[5,32,256]{2,1,0:T(8,128)}, f32[5,32,256]{2,1,0:T(8,128)S(1)}, u32[]{:S(2)}, u32[]{:S(2)}) collective-permute-start(f32[5,32,256]{2,1,0:T(8,128)} %get-tuple-element.8), channel_id=1, source_target_pairs={{15,255},{31,239},{47,223},{63,207},{79,191},{95,175},{111,159},{1... | collective-permute-start | bytes 491528 | tf_op jit(solution)/shard_map/ppermute | solution.py:177
  7.7 12.3 %collective-permute-start.1 = (f32[5,32,256]{2,1,0:T(8,128)}, f32[5,32,256]{2,1,0:T(8,128)S(1)}, u32[]{:S(2)}, u32[]{:S(2)}) collective-permute-start(f32[5,32,256]{2,1,0:T(8,128)} %get-tuple-element.9), channel_id=1, source_target_pairs={{1,0},{17,16},{33,32},{49,48},{65,64},{81,80},{97,96},{113,112},{1... | collective-permute-start | bytes 491528 | tf_op jit(solution)/shard_map/ppermute | solution.py:177
  18.6 0.7 %copy-start = (f32[5,32,256]{2,1,0:T(8,128)}, f32[5,32,256]{2,1,0:T(8,128)S(1)}, u32[]{:S(2)}) copy-start(f32[5,32,256]{2,1,0:T(8,128)S(1)} %collective-permute-done.2.rs_ref) | copy-start | bytes 491524
  20.0 0.7 %copy-start.5 = (f32[5]{0:T(128)S(1)}, f32[5]{0:T(128)}, u32[]{:S(2)}) copy-start(f32[5]{0:T(128)} %constant.10.clone) | copy-start | bytes 64
  20.6 0.9 %copy-start.3 = (f32[5,32,32]{2,1,0:T(8,128)S(1)}, f32[5,32,32]{2,1,0:T(8,128)}, u32[]{:S(2)}) copy-start(f32[5,32,32]{2,1,0:T(8,128)} %get-tuple-element.11) | copy-start | bytes 61444
  20.6 0.9 %copy-start.4 = (f32[5,32,32]{2,1,0:T(8,128)S(1)}, f32[5,32,32]{2,1,0:T(8,128)}, u32[]{:S(2)}) copy-start(f32[5,32,32]{2,1,0:T(8,128)} %get-tuple-element.10) | copy-start | bytes 61444
  21.7 6.0 %collective-permute-start.4 = (f32[5,40,32]{2,1,0:T(8,128)S(1)}, f32[5,40,32]{2,1,0:T(8,128)S(1)}, u32[]{:S(2)}, u32[]{:S(2)}) collective-permute-start(f32[5,40,32]{2,1,0:T(8,128)S(1)} %get-tuple-element.16), channel_id=1, source_target_pairs={{0,240},{16,0},{32,16},{48,32},{64,48},{80,64},{96,80},{112,96},{1... | collective-permute-start | bytes 76808 | tf_op jit(solution)/shard_map/ppermute | solution.py:177
  25.4 6.2 %collective-permute-start.3 = (f32[5,40,32]{2,1,0:T(8,128)S(1)}, f32[5,40,32]{2,1,0:T(8,128)S(1)}, u32[]{:S(2)}, u32[]{:S(2)}) collective-permute-start(f32[5,40,32]{2,1,0:T(8,128)S(1)} %get-tuple-element.17), channel_id=1, source_target_pairs={{0,16},{16,32},{32,48},{48,64},{64,80},{80,96},{96,112},{112,128},... | collective-permute-start | bytes 76808 | tf_op jit(solution)/shard_map/ppermute | solution.py:177
  27.7 3.9 %copy-start.1 = (f32[5,40,32]{2,1,0:T(8,128)}, f32[5,40,32]{2,1,0:T(8,128)S(1)}, u32[]{:S(2)}) copy-start(f32[5,40,32]{2,1,0:T(8,128)S(1)} %collective-permute-done.4.te_ref) | copy-start | bytes 76804
  31.6 0.6 %copy-start.2 = (f32[5,40,32]{2,1,0:T(8,128)}, f32[5,40,32]{2,1,0:T(8,128)S(1)}, u32[]{:S(2)}) copy-start(f32[5,40,32]{2,1,0:T(8,128)S(1)} %collective-permute-done.3.tw_ref) | copy-start | bytes 76804

commit v14 on v13

--- a/solution.py
+++ b/solution.py
@@ -513,7 +513,9 @@
     fold_row = shift(top, mirror)
     sign = jnp.array([-1.0, -1.0, 1.0, 1.0, 1.0], dtype=jnp.float32)[:, None, None]
     is_top = lax.axis_index("lat") == lax.axis_size("lat") - 1
-    halo_north = jnp.where(is_top, sign * fold_row[:, :, ::-1], halo_north)
+    flip = (jnp.arange(cols)[:, None] + jnp.arange(cols)[None, :] == cols - 1).astype(jnp.float32)
+    mirrored = jnp.dot(fold_row, flip, precision=lax.Precision.HIGHEST)
+    halo_north = jnp.where(is_top, sign * mirrored, halo_north)
     pad = jnp.zeros((fields, 6, levels), jnp.float32)
     west_tall = jnp.concatenate(
         [west_col, halo_south[:, None, :, 0], halo_north[:, None, :, 0], pad], axis=1

time: 50.6 us -> 49.6 us (0.980)
  local copies, waits for them, and re-layouts: 4.4 us -> 3.07 us
  matrix products: 0 us -> 0.52 us
    unnamed x14, local copies, waits for them, and re-layouts: 2.58 us -> 1.8 us
    dot_general x0 -> x1, matrix products: none -> 0.52 us  [per_device(): mirrored = jnp.dot(fold_row, flip, precision=lax.Precision.HIGHEST)]
  transfers between devices with their start and end apart: 5 -> 5, of which waited for: 2 -> 2; matrix products, arithmetic and copies ran while one was open for 4% -> 3% of each run, Pallas kernels for 10% -> 10%
where the time goes in v14:
time: 49.6 us; the launch traced here: 49.3 us
  Pallas kernels  25.5 us (51%)
  starting transfers between devices  14.1 us (28%)
  waiting for transfers between devices  5.32 us (11%)
  local copies, waits for them, and re-layouts  3.07 us (6%)
  between operations  0.74 us (1%)
  matrix products  0.52 us (1%)
    pallas_call x1, Pallas kernels, per_device(): pl.pallas_call(functools.partial(stencil_kernel, total_rows=total_rows),...  18 us
    ppermute x5, starting transfers between devices, shift(): return lax.ppermute(value, ('lon', 'lat'), pairs)  14.1 us
    ppermute x5, waiting for transfers between devices, shift(): return lax.ppermute(value, ('lon', 'lat'), pairs)  5.32 us
    pallas_call x1, Pallas kernels, per_device(): pl.pallas_call(edge_kernel, grid=(levels // chunk,), in_specs=[pl.BlockSp...  4.94 us
    pallas_call x1, Pallas kernels, per_device(): pl.pallas_call(row_kernel, grid=(1,), in_specs=[pl.BlockSpec((levels, til...  2.6 us
    unnamed x14, local copies, waits for them, and re-layouts  1.8 us
  transfers between devices with their start and end apart: 5, of which 2 were waited for; matrix products, arithmetic and copies ran while one was open for 3% of the time, Pallas kernels for 10%

profile of v14, /device:TPU:4, one launch (start us, length us, event | category | flops | bytes accessed | tf_op | source)
XLA Modules:
  0.0 49.3 jit_solution(5598908291001224052)
XLA Ops:
  0.6 2.6 %shard_map.102 = (f32[5,32,256]{2,1,0:T(8,128)}, f32[5,32,256]{2,1,0:T(8,128)}) custom-call(f32[32,32,256]{2,1,0:T(8,128)} %ub_ref.1, f32[32,32,256]{2,1,0:T(8,128)} %vb_ref.1, f32[32,32,256]{2,1,0:T(8,128)} %tb_ref.1, f32[32,32,256]{2,1,0:T(8,128)} %sb_ref.1, s32[32,32,256]{2,1,0:T(8,128)} %wb_ref.1, f32[32,32,256]{2,1,0:T(8,128)} %ub_ref.1, ...), custom_call_target="tpu_custom_call" | custom-call | tf_op jit(solution)/shard_map/pallas_call | solution.py:471
  3.2 3.8 %collective-permute-start.2 = (f32[5,32,256]{2,1,0:T(8,128)}, f32[5,32,256]{2,1,0:T(8,128)S(1)}, u32[]{:S(2)}, u32[]{:S(2)}) collective-permute-start(f32[5,32,256]{2,1,0:T(8,128)} %get-tuple-element.8), channel_id=1, source_target_pairs={{0,1},{16,17},{32,33},{48,49},{64,65},{80,81},{96,97},{112,113},{1... | collective-permute-start | bytes 491528 | tf_op jit(solution)/shard_map/ppermute | solution.py:177
  7.1 0.7 %collective-permute-start = (f32[5,32,256]{2,1,0:T(8,128)}, f32[5,32,256]{2,1,0:T(8,128)S(1)}, u32[]{:S(2)}, u32[]{:S(2)}) collective-permute-start(f32[5,32,256]{2,1,0:T(8,128)} %get-tuple-element.8), channel_id=1, source_target_pairs={{15,255},{31,239},{47,223},{63,207},{79,191},{95,175},{111,159},{1... | collective-permute-start | bytes 491528 | tf_op jit(solution)/shard_map/ppermute | solution.py:177
  7.7 5.8 %collective-permute-start.1 = (f32[5,32,256]{2,1,0:T(8,128)}, f32[5,32,256]{2,1,0:T(8,128)S(1)}, u32[]{:S(2)}, u32[]{:S(2)}) collective-permute-start(f32[5,32,256]{2,1,0:T(8,128)} %get-tuple-element.9), channel_id=1, source_target_pairs={{1,0},{17,16},{33,32},{49,48},{65,64},{81,80},{97,96},{113,112},{1... | collective-permute-start | bytes 491528 | tf_op jit(solution)/shard_map/ppermute | solution.py:177
  13.5 4.9 %shard_map.103 = (f32[5,32,32]{2,1,0:T(8,128)}, f32[5,32,32]{2,1,0:T(8,128)}) custom-call(f32[32,32,256]{2,1,0:T(8,128)} %ub_ref.1, f32[32,32,256]{2,1,0:T(8,128)} %vb_ref.1, f32[32,32,256]{2,1,0:T(8,128)} %tb_ref.1, f32[32,32,256]{2,1,0:T(8,128)} %sb_ref.1, s32[32,32,256]{2,1,0:T(8,128)} %wb_ref.1), custom_call_target="tpu_custom_call" | custom-call | tf_op jit(solution)/shard_map/pallas_call | solution.py:485
  18.5 0.1 pad.7.clone
  18.6 0.0 collective-permute-done.2.rs_ref
  18.6 0.0 copy-start
  18.6 0.1 fusion.5
  18.7 0.6 %copy-done = f32[5,32,256]{2,1,0:T(8,128)} copy-done((f32[5,32,256]{2,1,0:T(8,128)}, f32[5,32,256]{2,1,0:T(8,128)S(1)}, u32[]{:S(2)}) %copy-start) | copy-done | bytes 163864
  19.2 0.1 copy.23
  19.3 0.1 copy.22
  19.4 0.0 copy-start.5
  19.4 0.0 collective-permute-done.1
  19.4 0.2 copy.17
  19.7 0.0 copy-start.3
  19.7 0.0 copy-start.4
  19.7 0.0 collective-permute-done
  19.7 0.4 copy-done.5
  20.1 0.5 %fusion = f32[5,32,256]{1,2,0:T(8,128)S(1)} fusion(f32[5,32,256]{1,2,0:T(8,128)S(1)} %copy.17, f32[5,32,256]{2,1,0:T(8,128)S(1)} %collective-permute-done, f32[5]{0:T(128)S(1)} %copy-done.5, pred[]{:T(512)S(6)} %eq.9), kind=kOutput, calls=%fused_computation.1 | convolution fusion | flops 126042112 | bytes 491541 | tf_op jit(solution)/shard_map/dot_general | solution.py:517
  20.6 0.0 copy-done.3
  20.6 0.0 copy-done.4
  20.7 0.1 maximum_maximum_fusion.1
  20.7 3.8 %collective-permute-start.4 = (f32[5,40,32]{2,1,0:T(8,128)S(1)}, f32[5,40,32]{2,1,0:T(8,128)S(1)}, u32[]{:S(2)}, u32[]{:S(2)}) collective-permute-start(f32[5,40,32]{2,1,0:T(8,128)S(1)} %get-tuple-element.16), channel_id=1, source_target_pairs={{0,240},{16,0},{32,16},{48,32},{64,48},{80,64},{96,80},{112,96},{1... | collective-permute-start | bytes 76808 | tf_op jit(solution)/shard_map/ppermute | solution.py:177
  24.5 0.0 collective-permute-start.3
  24.5 0.9 %copy.20.rn_ref = f32[5,32,256]{2,1,0:T(8,128)} copy(f32[5,32,256]{1,2,0:T(8,128)S(1)} %fusion) | data formatting | bytes 327680 | tf_op jit(solution)/shard_map/jit(_where)/select_n | solution.py:518
  25.4 1.4 %collective-permute-done.4.te_ref = f32[5,40,32]{2,1,0:T(8,128)S(1)} collective-permute-done((f32[5,40,32]{2,1,0:T(8,128)S(1)}, f32[5,40,32]{2,1,0:T(8,128)S(1)}, u32[]{:S(2)}, u32[]{:S(2)}) %collective-permute-start.4) | collective-permute-done | bytes 25632 | tf_op jit(solution)/shard_map/ppermute | solution.py:177
  26.8 0.0 copy-start.1
  26.8 3.9 %collective-permute-done.3.tw_ref = f32[5,40,32]{2,1,0:T(8,128)S(1)} collective-permute-done((f32[5,40,32]{2,1,0:T(8,128)S(1)}, f32[5,40,32]{2,1,0:T(8,128)S(1)}, u32[]{:S(2)}, u32[]{:S(2)}) %collective-permute-start.3) | collective-permute-done | bytes 25632 | tf_op jit(solution)/shard_map/ppermute | solution.py:177
  30.7 0.0 copy-start.2
  30.7 0.0 copy-done.1
  30.7 0.6 %copy-done.2 = f32[5,40,32]{2,1,0:T(8,128)} copy-done((f32[5,40,32]{2,1,0:T(8,128)}, f32[5,40,32]{2,1,0:T(8,128)S(1)}, u32[]{:S(2)}) %copy-start.2) | copy-done | bytes 25624
  31.4 18.0 %shard_map.104 = (f32[32,32,256]{2,1,0:T(8,128)}, f32[32,32,256]{2,1,0:T(8,128)}, f32[32,32,256]{2,1,0:T(8,128)}, f32[32,32,256]{2,1,0:T(8,128)}) custom-call(s32[1]{0:T(128)} %bitcast.meta_ref, f32[32,32,256]{2,1,0:T(8,128)} %ub_ref.1, f32[32,32,256]{2,1,0:T(8,128)} %vb_ref.1, f32[32,32,256]{2,1,0:T(8,128)} %tb_ref.1, f32[32,32,256]{2,1,0:T(8,128)} %sb_ref.1, ...), custom_call_target="tpu_custom_call" | custom-call | tf_op jit(solution)/shard_map/pallas_call | solution.py:547
  (2 shorter events, 0.0 us)
Async XLA Ops:
  3.2 15.3 %collective-permute-start.2 = (f32[5,32,256]{2,1,0:T(8,128)}, f32[5,32,256]{2,1,0:T(8,128)S(1)}, u32[]{:S(2)}, u32[]{:S(2)}) collective-permute-start(f32[5,32,256]{2,1,0:T(8,128)} %get-tuple-element.8), channel_id=1, source_target_pairs={{0,1},{16,17},{32,33},{48,49},{64,65},{80,81},{96,97},{112,113},{1... | collective-permute-start | bytes 491528 | tf_op jit(solution)/shard_map/ppermute | solution.py:177
  7.1 12.6 %collective-permute-start = (f32[5,32,256]{2,1,0:T(8,128)}, f32[5,32,256]{2,1,0:T(8,128)S(1)}, u32[]{:S(2)}, u32[]{:S(2)}) collective-permute-start(f32[5,32,256]{2,1,0:T(8,128)} %get-tuple-element.8), channel_id=1, source_target_pairs={{15,255},{31,239},{47,223},{63,207},{79,191},{95,175},{111,159},{1... | collective-permute-start | bytes 491528 | tf_op jit(solution)/shard_map/ppermute | solution.py:177
  7.7 11.7 %collective-permute-start.1 = (f32[5,32,256]{2,1,0:T(8,128)}, f32[5,32,256]{2,1,0:T(8,128)S(1)}, u32[]{:S(2)}, u32[]{:S(2)}) collective-permute-start(f32[5,32,256]{2,1,0:T(8,128)} %get-tuple-element.9), channel_id=1, source_target_pairs={{1,0},{17,16},{33,32},{49,48},{65,64},{81,80},{97,96},{113,112},{1... | collective-permute-start | bytes 491528 | tf_op jit(solution)/shard_map/ppermute | solution.py:177
  18.6 0.7 %copy-start = (f32[5,32,256]{2,1,0:T(8,128)}, f32[5,32,256]{2,1,0:T(8,128)S(1)}, u32[]{:S(2)}) copy-start(f32[5,32,256]{2,1,0:T(8,128)S(1)} %collective-permute-done.2.rs_ref) | copy-start | bytes 491524
  19.4 0.7 %copy-start.5 = (f32[5]{0:T(128)S(1)}, f32[5]{0:T(128)}, u32[]{:S(2)}) copy-start(f32[5]{0:T(128)} %constant.12.clone) | copy-start | bytes 64
  19.7 1.0 %copy-start.3 = (f32[5,32,32]{2,1,0:T(8,128)S(1)}, f32[5,32,32]{2,1,0:T(8,128)}, u32[]{:S(2)}) copy-start(f32[5,32,32]{2,1,0:T(8,128)} %get-tuple-element.11) | copy-start | bytes 61444
  19.7 1.0 %copy-start.4 = (f32[5,32,32]{2,1,0:T(8,128)S(1)}, f32[5,32,32]{2,1,0:T(8,128)}, u32[]{:S(2)}) copy-start(f32[5,32,32]{2,1,0:T(8,128)} %get-tuple-element.10) | copy-start | bytes 61444
  20.7 6.0 %collective-permute-start.4 = (f32[5,40,32]{2,1,0:T(8,128)S(1)}, f32[5,40,32]{2,1,0:T(8,128)S(1)}, u32[]{:S(2)}, u32[]{:S(2)}) collective-permute-start(f32[5,40,32]{2,1,0:T(8,128)S(1)} %get-tuple-element.16), channel_id=1, source_target_pairs={{0,240},{16,0},{32,16},{48,32},{64,48},{80,64},{96,80},{112,96},{1... | collective-permute-start | bytes 76808 | tf_op jit(solution)/shard_map/ppermute | solution.py:177
  24.5 6.2 %collective-permute-start.3 = (f32[5,40,32]{2,1,0:T(8,128)S(1)}, f32[5,40,32]{2,1,0:T(8,128)S(1)}, u32[]{:S(2)}, u32[]{:S(2)}) collective-permute-start(f32[5,40,32]{2,1,0:T(8,128)S(1)} %get-tuple-element.17), channel_id=1, source_target_pairs={{0,16},{16,32},{32,48},{48,64},{64,80},{80,96},{96,112},{112,128},... | collective-permute-start | bytes 76808 | tf_op jit(solution)/shard_map/ppermute | solution.py:177
  26.8 3.9 %copy-start.1 = (f32[5,40,32]{2,1,0:T(8,128)}, f32[5,40,32]{2,1,0:T(8,128)S(1)}, u32[]{:S(2)}) copy-start(f32[5,40,32]{2,1,0:T(8,128)S(1)} %collective-permute-done.4.te_ref) | copy-start | bytes 76804
  30.7 0.6 %copy-start.2 = (f32[5,40,32]{2,1,0:T(8,128)}, f32[5,40,32]{2,1,0:T(8,128)S(1)}, u32[]{:S(2)}) copy-start(f32[5,40,32]{2,1,0:T(8,128)S(1)} %collective-permute-done.3.tw_ref) | copy-start | bytes 76804

commit v15 on v14

--- a/solution.py
+++ b/solution.py
@@ -218,7 +218,7 @@
 def stencil_kernel(
     meta_ref, u_ref, v_ref, t_ref, s_ref, wet_ref, ua_ref, va_ref, ta_ref, sa_ref, wa_ref,
     ub_ref, vb_ref, tb_ref, sb_ref, wb_ref, clc_ref, rn_ref, rs_ref, tw_ref, te_ref,
-    east_ref, north_ref, temp_ref, salt_ref, p_ref, pe_ref, pn_ref, *, total_rows,
+    east_ref, north_ref, temp_ref, salt_ref, p_ref, pe_ref, pn_ref, pm_ref, *, total_rows,
 ):
     chunk, rows, cols = u_ref.shape
     levels = tw_ref.shape[2]
@@ -242,6 +242,7 @@
         p_ref[...] = jnp.zeros(p_ref.shape, jnp.float32)
         pe_ref[...] = jnp.zeros(pe_ref.shape, jnp.float32)
         pn_ref[...] = jnp.zeros(pn_ref.shape, jnp.float32)
+        pm_ref[...] = jnp.zeros(pm_ref.shape, jnp.float32)
 
     fields = 5
     lane = lax.broadcasted_iota(jnp.int32, (rows, cols), 1)
@@ -278,7 +279,7 @@
         return jnp.where(at_south, row, pltpu.roll(x, 1, 0))
 
     def body(r, carry):
-        pres, pres_e, pres_n = carry
+        pres, pres_e, pres_n, mix_above = carry
         k = step * chunk + r
 
         spread = {}
@@ -311,7 +312,6 @@
             return west_t[0:rows], east_t[0:rows]
 
         w = wet_ref[r].astype(jnp.float32)
-        w_above = level(wet_ref, r, -1).astype(jnp.float32)
         w_below = level(wet_ref, r, 1).astype(jnp.float32)
         w_wc, w_ec = col(4)
         w_e = east(w, w_ec)
@@ -328,7 +328,6 @@
         mix_below = jnp.where(
             k < levels - 1, w * w_below * (k + 1 < count).astype(jnp.float32), 0.0
         )
-        mix_above = jnp.where(k > 0, w_above * w * (k < count).astype(jnp.float32), 0.0)
         bottom = (k == count - 1).astype(jnp.float32)
 
         def column(ref, centre):
@@ -437,10 +436,11 @@
             - drag_coef * bottom * vc
         )
         north_ref[r] = mask_north * (vc + time_step * north_tend)
-        return pres, pres_e, pres_n
-
-    init = (p_ref[...], pe_ref[...], pn_ref[...])
-    pres, pres_e, pres_n = lax.fori_loop(0, chunk, body, init)
+        return pres, pres_e, pres_n, mix_below
+
+    init = (p_ref[...], pe_ref[...], pn_ref[...], pm_ref[...])
+    pres, pres_e, pres_n, mix_last = lax.fori_loop(0, chunk, body, init)
+    pm_ref[...] = mix_last
     p_ref[...] = pres
     pe_ref[...] = pres_e
     pn_ref[...] = pres_n
@@ -558,6 +558,7 @@
             pltpu.VMEM((rows, cols), jnp.float32),
             pltpu.VMEM((rows, cols), jnp.float32),
             pltpu.VMEM((1, cols), jnp.float32),
+            pltpu.VMEM((rows, cols), jnp.float32),
         ],
     )(
         meta.astype(jnp.int32),

time: 49.6 us -> 49.6 us (level)
  no operation moved by 1% of the time
where the time goes in v15:
time: 49.6 us; the launch traced here: 49.3 us
  Pallas kernels  25.5 us (51%)
  starting transfers between devices  14.1 us (28%)
  waiting for transfers between devices  5.32 us (11%)
  local copies, waits for them, and re-layouts  3.07 us (6%)
  between operations  0.74 us (1%)
  matrix products  0.52 us (1%)
    pallas_call x1, Pallas kernels, per_device(): pl.pallas_call(functools.partial(stencil_kernel, total_rows=total_rows),...  17.9 us
    ppermute x5, starting transfers between devices, shift(): return lax.ppermute(value, ('lon', 'lat'), pairs)  14.1 us
    ppermute x5, waiting for transfers between devices, shift(): return lax.ppermute(value, ('lon', 'lat'), pairs)  5.32 us
    pallas_call x1, Pallas kernels, per_device(): pl.pallas_call(edge_kernel, grid=(levels // chunk,), in_specs=[pl.BlockSp...  4.94 us
    pallas_call x1, Pallas kernels, per_device(): pl.pallas_call(row_kernel, grid=(1,), in_specs=[pl.BlockSpec((levels, til...  2.6 us
    unnamed x14, local copies, waits for them, and re-layouts  1.8 us
  transfers between devices with their start and end apart: 5, of which 2 were waited for; matrix products, arithmetic and copies ran while one was open for 3% of the time, Pallas kernels for 10%

profile of v15, /device:TPU:4, one launch (start us, length us, event | category | flops | bytes accessed | tf_op | source)
XLA Modules:
  0.0 49.3 jit_solution(17229326897825423085)
XLA Ops:
  0.6 2.6 %shard_map.102 = (f32[5,32,256]{2,1,0:T(8,128)}, f32[5,32,256]{2,1,0:T(8,128)}) custom-call(f32[32,32,256]{2,1,0:T(8,128)} %ub_ref.1, f32[32,32,256]{2,1,0:T(8,128)} %vb_ref.1, f32[32,32,256]{2,1,0:T(8,128)} %tb_ref.1, f32[32,32,256]{2,1,0:T(8,128)} %sb_ref.1, s32[32,32,256]{2,1,0:T(8,128)} %wb_ref.1, f32[32,32,256]{2,1,0:T(8,128)} %ub_ref.1, ...), custom_call_target="tpu_custom_call" | custom-call | tf_op jit(solution)/shard_map/pallas_call | solution.py:471
  3.2 3.8 %collective-permute-start.2 = (f32[5,32,256]{2,1,0:T(8,128)}, f32[5,32,256]{2,1,0:T(8,128)S(1)}, u32[]{:S(2)}, u32[]{:S(2)}) collective-permute-start(f32[5,32,256]{2,1,0:T(8,128)} %get-tuple-element.8), channel_id=1, source_target_pairs={{0,1},{16,17},{32,33},{48,49},{64,65},{80,81},{96,97},{112,113},{1... | collective-permute-start | bytes 491528 | tf_op jit(solution)/shard_map/ppermute | solution.py:177
  7.1 0.7 %collective-permute-start = (f32[5,32,256]{2,1,0:T(8,128)}, f32[5,32,256]{2,1,0:T(8,128)S(1)}, u32[]{:S(2)}, u32[]{:S(2)}) collective-permute-start(f32[5,32,256]{2,1,0:T(8,128)} %get-tuple-element.8), channel_id=1, source_target_pairs={{15,255},{31,239},{47,223},{63,207},{79,191},{95,175},{111,159},{1... | collective-permute-start | bytes 491528 | tf_op jit(solution)/shard_map/ppermute | solution.py:177
  7.7 5.8 %collective-permute-start.1 = (f32[5,32,256]{2,1,0:T(8,128)}, f32[5,32,256]{2,1,0:T(8,128)S(1)}, u32[]{:S(2)}, u32[]{:S(2)}) collective-permute-start(f32[5,32,256]{2,1,0:T(8,128)} %get-tuple-element.9), channel_id=1, source_target_pairs={{1,0},{17,16},{33,32},{49,48},{65,64},{81,80},{97,96},{113,112},{1... | collective-permute-start | bytes 491528 | tf_op jit(solution)/shard_map/ppermute | solution.py:177
  13.5 4.9 %shard_map.103 = (f32[5,32,32]{2,1,0:T(8,128)}, f32[5,32,32]{2,1,0:T(8,128)}) custom-call(f32[32,32,256]{2,1,0:T(8,128)} %ub_ref.1, f32[32,32,256]{2,1,0:T(8,128)} %vb_ref.1, f32[32,32,256]{2,1,0:T(8,128)} %tb_ref.1, f32[32,32,256]{2,1,0:T(8,128)} %sb_ref.1, s32[32,32,256]{2,1,0:T(8,128)} %wb_ref.1), custom_call_target="tpu_custom_call" | custom-call | tf_op jit(solution)/shard_map/pallas_call | solution.py:485
  18.5 0.1 pad.7.clone
  18.6 0.0 collective-permute-done.2.rs_ref
  18.6 0.0 copy-start
  18.6 0.1 fusion.5
  18.7 0.6 %copy-done = f32[5,32,256]{2,1,0:T(8,128)} copy-done((f32[5,32,256]{2,1,0:T(8,128)}, f32[5,32,256]{2,1,0:T(8,128)S(1)}, u32[]{:S(2)}) %copy-start) | copy-done | bytes 163864
  19.2 0.1 copy.23
  19.3 0.1 copy.22
  19.4 0.0 copy-start.5
  19.4 0.0 collective-permute-done.1
  19.4 0.2 copy.17
  19.7 0.0 copy-start.3
  19.7 0.0 copy-start.4
  19.7 0.0 collective-permute-done
  19.7 0.4 copy-done.5
  20.1 0.5 %fusion = f32[5,32,256]{1,2,0:T(8,128)S(1)} fusion(f32[5,32,256]{1,2,0:T(8,128)S(1)} %copy.17, f32[5,32,256]{2,1,0:T(8,128)S(1)} %collective-permute-done, f32[5]{0:T(128)S(1)} %copy-done.5, pred[]{:T(512)S(6)} %eq.9), kind=kOutput, calls=%fused_computation.1 | convolution fusion | flops 126042112 | bytes 491541 | tf_op jit(solution)/shard_map/dot_general | solution.py:517
  20.6 0.0 copy-done.3
  20.6 0.0 copy-done.4
  20.7 0.1 maximum_maximum_fusion.1
  20.7 3.8 %collective-permute-start.4 = (f32[5,40,32]{2,1,0:T(8,128)S(1)}, f32[5,40,32]{2,1,0:T(8,128)S(1)}, u32[]{:S(2)}, u32[]{:S(2)}) collective-permute-start(f32[5,40,32]{2,1,0:T(8,128)S(1)} %get-tuple-element.16), channel_id=1, source_target_pairs={{0,240},{16,0},{32,16},{48,32},{64,48},{80,64},{96,80},{112,96},{1... | collective-permute-start | bytes 76808 | tf_op jit(solution)/shard_map/ppermute | solution.py:177
  24.5 0.0 collective-permute-start.3
  24.5 0.9 %copy.20.rn_ref = f32[5,32,256]{2,1,0:T(8,128)} copy(f32[5,32,256]{1,2,0:T(8,128)S(1)} %fusion) | data formatting | bytes 327680 | tf_op jit(solution)/shard_map/jit(_where)/select_n | solution.py:518
  25.4 1.4 %collective-permute-done.4.te_ref = f32[5,40,32]{2,1,0:T(8,128)S(1)} collective-permute-done((f32[5,40,32]{2,1,0:T(8,128)S(1)}, f32[5,40,32]{2,1,0:T(8,128)S(1)}, u32[]{:S(2)}, u32[]{:S(2)}) %collective-permute-start.4) | collective-permute-done | bytes 25632 | tf_op jit(solution)/shard_map/ppermute | solution.py:177
  26.8 0.0 copy-start.1
  26.8 3.9 %collective-permute-done.3.tw_ref = f32[5,40,32]{2,1,0:T(8,128)S(1)} collective-permute-done((f32[5,40,32]{2,1,0:T(8,128)S(1)}, f32[5,40,32]{2,1,0:T(8,128)S(1)}, u32[]{:S(2)}, u32[]{:S(2)}) %collective-permute-start.3) | collective-permute-done | bytes 25632 | tf_op jit(solution)/shard_map/ppermute | solution.py:177
  30.7 0.0 copy-start.2
  30.7 0.0 copy-done.1
  30.7 0.6 %copy-done.2 = f32[5,40,32]{2,1,0:T(8,128)} copy-done((f32[5,40,32]{2,1,0:T(8,128)}, f32[5,40,32]{2,1,0:T(8,128)S(1)}, u32[]{:S(2)}) %copy-start.2) | copy-done | bytes 25624
  31.4 17.9 %shard_map.104 = (f32[32,32,256]{2,1,0:T(8,128)}, f32[32,32,256]{2,1,0:T(8,128)}, f32[32,32,256]{2,1,0:T(8,128)}, f32[32,32,256]{2,1,0:T(8,128)}) custom-call(s32[1]{0:T(128)} %bitcast.meta_ref, f32[32,32,256]{2,1,0:T(8,128)} %ub_ref.1, f32[32,32,256]{2,1,0:T(8,128)} %vb_ref.1, f32[32,32,256]{2,1,0:T(8,128)} %tb_ref.1, f32[32,32,256]{2,1,0:T(8,128)} %sb_ref.1, ...), custom_call_target="tpu_custom_call" | custom-call | tf_op jit(solution)/shard_map/pallas_call | solution.py:547
  (2 shorter events, 0.0 us)
Async XLA Ops:
  3.2 15.3 %collective-permute-start.2 = (f32[5,32,256]{2,1,0:T(8,128)}, f32[5,32,256]{2,1,0:T(8,128)S(1)}, u32[]{:S(2)}, u32[]{:S(2)}) collective-permute-start(f32[5,32,256]{2,1,0:T(8,128)} %get-tuple-element.8), channel_id=1, source_target_pairs={{0,1},{16,17},{32,33},{48,49},{64,65},{80,81},{96,97},{112,113},{1... | collective-permute-start | bytes 491528 | tf_op jit(solution)/shard_map/ppermute | solution.py:177
  7.1 12.6 %collective-permute-start = (f32[5,32,256]{2,1,0:T(8,128)}, f32[5,32,256]{2,1,0:T(8,128)S(1)}, u32[]{:S(2)}, u32[]{:S(2)}) collective-permute-start(f32[5,32,256]{2,1,0:T(8,128)} %get-tuple-element.8), channel_id=1, source_target_pairs={{15,255},{31,239},{47,223},{63,207},{79,191},{95,175},{111,159},{1... | collective-permute-start | bytes 491528 | tf_op jit(solution)/shard_map/ppermute | solution.py:177
  7.7 11.7 %collective-permute-start.1 = (f32[5,32,256]{2,1,0:T(8,128)}, f32[5,32,256]{2,1,0:T(8,128)S(1)}, u32[]{:S(2)}, u32[]{:S(2)}) collective-permute-start(f32[5,32,256]{2,1,0:T(8,128)} %get-tuple-element.9), channel_id=1, source_target_pairs={{1,0},{17,16},{33,32},{49,48},{65,64},{81,80},{97,96},{113,112},{1... | collective-permute-start | bytes 491528 | tf_op jit(solution)/shard_map/ppermute | solution.py:177
  18.6 0.7 %copy-start = (f32[5,32,256]{2,1,0:T(8,128)}, f32[5,32,256]{2,1,0:T(8,128)S(1)}, u32[]{:S(2)}) copy-start(f32[5,32,256]{2,1,0:T(8,128)S(1)} %collective-permute-done.2.rs_ref) | copy-start | bytes 491524
  19.4 0.7 %copy-start.5 = (f32[5]{0:T(128)S(1)}, f32[5]{0:T(128)}, u32[]{:S(2)}) copy-start(f32[5]{0:T(128)} %constant.12.clone) | copy-start | bytes 64
  19.7 1.0 %copy-start.3 = (f32[5,32,32]{2,1,0:T(8,128)S(1)}, f32[5,32,32]{2,1,0:T(8,128)}, u32[]{:S(2)}) copy-start(f32[5,32,32]{2,1,0:T(8,128)} %get-tuple-element.11) | copy-start | bytes 61444
  19.7 1.0 %copy-start.4 = (f32[5,32,32]{2,1,0:T(8,128)S(1)}, f32[5,32,32]{2,1,0:T(8,128)}, u32[]{:S(2)}) copy-start(f32[5,32,32]{2,1,0:T(8,128)} %get-tuple-element.10) | copy-start | bytes 61444
  20.7 6.0 %collective-permute-start.4 = (f32[5,40,32]{2,1,0:T(8,128)S(1)}, f32[5,40,32]{2,1,0:T(8,128)S(1)}, u32[]{:S(2)}, u32[]{:S(2)}) collective-permute-start(f32[5,40,32]{2,1,0:T(8,128)S(1)} %get-tuple-element.16), channel_id=1, source_target_pairs={{0,240},{16,0},{32,16},{48,32},{64,48},{80,64},{96,80},{112,96},{1... | collective-permute-start | bytes 76808 | tf_op jit(solution)/shard_map/ppermute | solution.py:177
  24.5 6.2 %collective-permute-start.3 = (f32[5,40,32]{2,1,0:T(8,128)S(1)}, f32[5,40,32]{2,1,0:T(8,128)S(1)}, u32[]{:S(2)}, u32[]{:S(2)}) collective-permute-start(f32[5,40,32]{2,1,0:T(8,128)S(1)} %get-tuple-element.17), channel_id=1, source_target_pairs={{0,16},{16,32},{32,48},{48,64},{64,80},{80,96},{96,112},{112,128},... | collective-permute-start | bytes 76808 | tf_op jit(solution)/shard_map/ppermute | solution.py:177
  26.8 3.9 %copy-start.1 = (f32[5,40,32]{2,1,0:T(8,128)}, f32[5,40,32]{2,1,0:T(8,128)S(1)}, u32[]{:S(2)}) copy-start(f32[5,40,32]{2,1,0:T(8,128)S(1)} %collective-permute-done.4.te_ref) | copy-start | bytes 76804
  30.7 0.6 %copy-start.2 = (f32[5,40,32]{2,1,0:T(8,128)}, f32[5,40,32]{2,1,0:T(8,128)S(1)}, u32[]{:S(2)}) copy-start(f32[5,40,32]{2,1,0:T(8,128)S(1)} %collective-permute-done.3.tw_ref) | copy-start | bytes 76804

commit v16 on v14

--- a/solution.py
+++ b/solution.py
@@ -184,9 +184,8 @@
     top_ref, bottom_ref = refs[2 * fields :]
     chunk, tile, cols = lows[0].shape
     for field in range(fields):
-        for r in range(chunk):
-            top_ref[field, r : r + 1, :] = highs[field][r][tile - 1 : tile, :].astype(jnp.float32)
-            bottom_ref[field, r : r + 1, :] = lows[field][r][0:1, :].astype(jnp.float32)
+        top_ref[field] = highs[field][:, tile - 1, :].astype(jnp.float32)
+        bottom_ref[field] = lows[field][:, 0, :].astype(jnp.float32)
 
 
 def edge_kernel(*refs):

time: 49.6 us -> 49.5 us (level)
  no operation moved by 1% of the time
where the time goes in v16:
time: 49.5 us; the launch traced here: 49.3 us
  Pallas kernels  25.4 us (51%)
  starting transfers between devices  14.1 us (28%)
  waiting for transfers between devices  5.32 us (11%)
  local copies, waits for them, and re-layouts  3.07 us (6%)
  between operations  0.74 us (1%)
  matrix products  0.52 us (1%)
    pallas_call x1, Pallas kernels, per_device(): pl.pallas_call(functools.partial(stencil_kernel, total_rows=total_rows),...  18 us
    ppermute x5, starting transfers between devices, shift(): return lax.ppermute(value, ('lon', 'lat'), pairs)  14.1 us
    ppermute x5, waiting for transfers between devices, shift(): return lax.ppermute(value, ('lon', 'lat'), pairs)  5.32 us
    pallas_call x1, Pallas kernels, per_device(): pl.pallas_call(edge_kernel, grid=(levels // chunk,), in_specs=[pl.BlockSp...  4.94 us
    pallas_call x1, Pallas kernels, per_device(): pl.pallas_call(row_kernel, grid=(1,), in_specs=[pl.BlockSpec((levels, til...  2.52 us
    unnamed x14, local copies, waits for them, and re-layouts  1.8 us
  transfers between devices with their start and end apart: 5, of which 2 were waited for; matrix products, arithmetic and copies ran while one was open for 3% of the time, Pallas kernels for 10%

profile of v16, /device:TPU:4, one launch (start us, length us, event | category | flops | bytes accessed | tf_op | source)
XLA Modules:
  0.0 49.3 jit_solution(6717860680372611010)
XLA Ops:
  0.6 2.5 %shard_map.102 = (f32[5,32,256]{2,1,0:T(8,128)}, f32[5,32,256]{2,1,0:T(8,128)}) custom-call(f32[32,32,256]{2,1,0:T(8,128)} %ub_ref.1, f32[32,32,256]{2,1,0:T(8,128)} %vb_ref.1, f32[32,32,256]{2,1,0:T(8,128)} %tb_ref.1, f32[32,32,256]{2,1,0:T(8,128)} %sb_ref.1, s32[32,32,256]{2,1,0:T(8,128)} %wb_ref.1, f32[32,32,256]{2,1,0:T(8,128)} %ub_ref.1, ...), custom_call_target="tpu_custom_call" | custom-call | tf_op jit(solution)/shard_map/pallas_call | solution.py:470
  3.1 3.8 %collective-permute-start.2 = (f32[5,32,256]{2,1,0:T(8,128)}, f32[5,32,256]{2,1,0:T(8,128)S(1)}, u32[]{:S(2)}, u32[]{:S(2)}) collective-permute-start(f32[5,32,256]{2,1,0:T(8,128)} %get-tuple-element.8), channel_id=1, source_target_pairs={{0,1},{16,17},{32,33},{48,49},{64,65},{80,81},{96,97},{112,113},{1... | collective-permute-start | bytes 491528 | tf_op jit(solution)/shard_map/ppermute | solution.py:177
  7.0 0.7 %collective-permute-start = (f32[5,32,256]{2,1,0:T(8,128)}, f32[5,32,256]{2,1,0:T(8,128)S(1)}, u32[]{:S(2)}, u32[]{:S(2)}) collective-permute-start(f32[5,32,256]{2,1,0:T(8,128)} %get-tuple-element.8), channel_id=1, source_target_pairs={{15,255},{31,239},{47,223},{63,207},{79,191},{95,175},{111,159},{1... | collective-permute-start | bytes 491528 | tf_op jit(solution)/shard_map/ppermute | solution.py:177
  7.6 5.8 %collective-permute-start.1 = (f32[5,32,256]{2,1,0:T(8,128)}, f32[5,32,256]{2,1,0:T(8,128)S(1)}, u32[]{:S(2)}, u32[]{:S(2)}) collective-permute-start(f32[5,32,256]{2,1,0:T(8,128)} %get-tuple-element.9), channel_id=1, source_target_pairs={{1,0},{17,16},{33,32},{49,48},{65,64},{81,80},{97,96},{113,112},{1... | collective-permute-start | bytes 491528 | tf_op jit(solution)/shard_map/ppermute | solution.py:177
  13.5 4.9 %shard_map.103 = (f32[5,32,32]{2,1,0:T(8,128)}, f32[5,32,32]{2,1,0:T(8,128)}) custom-call(f32[32,32,256]{2,1,0:T(8,128)} %ub_ref.1, f32[32,32,256]{2,1,0:T(8,128)} %vb_ref.1, f32[32,32,256]{2,1,0:T(8,128)} %tb_ref.1, f32[32,32,256]{2,1,0:T(8,128)} %sb_ref.1, s32[32,32,256]{2,1,0:T(8,128)} %wb_ref.1), custom_call_target="tpu_custom_call" | custom-call | tf_op jit(solution)/shard_map/pallas_call | solution.py:484
  18.4 0.1 pad.7.clone
  18.5 0.0 collective-permute-done.2.rs_ref
  18.5 0.0 copy-start
  18.5 0.1 fusion.5
  18.6 0.6 %copy-done = f32[5,32,256]{2,1,0:T(8,128)} copy-done((f32[5,32,256]{2,1,0:T(8,128)}, f32[5,32,256]{2,1,0:T(8,128)S(1)}, u32[]{:S(2)}) %copy-start) | copy-done | bytes 163864
  19.1 0.1 copy.23
  19.2 0.1 copy.22
  19.3 0.0 copy-start.5
  19.3 0.0 collective-permute-done.1
  19.3 0.2 copy.17
  19.6 0.0 copy-start.3
  19.6 0.0 copy-start.4
  19.6 0.0 collective-permute-done
  19.6 0.4 copy-done.5
  20.0 0.5 %fusion = f32[5,32,256]{1,2,0:T(8,128)S(1)} fusion(f32[5,32,256]{1,2,0:T(8,128)S(1)} %copy.17, f32[5,32,256]{2,1,0:T(8,128)S(1)} %collective-permute-done, f32[5]{0:T(128)S(1)} %copy-done.5, pred[]{:T(512)S(6)} %eq.9), kind=kOutput, calls=%fused_computation.1 | convolution fusion | flops 126042112 | bytes 491541 | tf_op jit(solution)/shard_map/dot_general | solution.py:516
  20.5 0.0 copy-done.3
  20.6 0.0 copy-done.4
  20.6 0.1 maximum_maximum_fusion.1
  20.7 3.8 %collective-permute-start.4 = (f32[5,40,32]{2,1,0:T(8,128)S(1)}, f32[5,40,32]{2,1,0:T(8,128)S(1)}, u32[]{:S(2)}, u32[]{:S(2)}) collective-permute-start(f32[5,40,32]{2,1,0:T(8,128)S(1)} %get-tuple-element.16), channel_id=1, source_target_pairs={{0,240},{16,0},{32,16},{48,32},{64,48},{80,64},{96,80},{112,96},{1... | collective-permute-start | bytes 76808 | tf_op jit(solution)/shard_map/ppermute | solution.py:177
  24.4 0.0 collective-permute-start.3
  24.4 0.9 %copy.20.rn_ref = f32[5,32,256]{2,1,0:T(8,128)} copy(f32[5,32,256]{1,2,0:T(8,128)S(1)} %fusion) | data formatting | bytes 327680 | tf_op jit(solution)/shard_map/jit(_where)/select_n | solution.py:517
  25.3 1.4 %collective-permute-done.4.te_ref = f32[5,40,32]{2,1,0:T(8,128)S(1)} collective-permute-done((f32[5,40,32]{2,1,0:T(8,128)S(1)}, f32[5,40,32]{2,1,0:T(8,128)S(1)}, u32[]{:S(2)}, u32[]{:S(2)}) %collective-permute-start.4) | collective-permute-done | bytes 25632 | tf_op jit(solution)/shard_map/ppermute | solution.py:177
  26.7 0.0 copy-start.1
  26.7 3.9 %collective-permute-done.3.tw_ref = f32[5,40,32]{2,1,0:T(8,128)S(1)} collective-permute-done((f32[5,40,32]{2,1,0:T(8,128)S(1)}, f32[5,40,32]{2,1,0:T(8,128)S(1)}, u32[]{:S(2)}, u32[]{:S(2)}) %collective-permute-start.3) | collective-permute-done | bytes 25632 | tf_op jit(solution)/shard_map/ppermute | solution.py:177
  30.6 0.0 copy-start.2
  30.6 0.0 copy-done.1
  30.6 0.6 %copy-done.2 = f32[5,40,32]{2,1,0:T(8,128)} copy-done((f32[5,40,32]{2,1,0:T(8,128)}, f32[5,40,32]{2,1,0:T(8,128)S(1)}, u32[]{:S(2)}) %copy-start.2) | copy-done | bytes 25624
  31.3 18.0 %shard_map.104 = (f32[32,32,256]{2,1,0:T(8,128)}, f32[32,32,256]{2,1,0:T(8,128)}, f32[32,32,256]{2,1,0:T(8,128)}, f32[32,32,256]{2,1,0:T(8,128)}) custom-call(s32[1]{0:T(128)} %bitcast.meta_ref, f32[32,32,256]{2,1,0:T(8,128)} %ub_ref.1, f32[32,32,256]{2,1,0:T(8,128)} %vb_ref.1, f32[32,32,256]{2,1,0:T(8,128)} %tb_ref.1, f32[32,32,256]{2,1,0:T(8,128)} %sb_ref.1, ...), custom_call_target="tpu_custom_call" | custom-call | tf_op jit(solution)/shard_map/pallas_call | solution.py:546
  (2 shorter events, 0.0 us)
Async XLA Ops:
  3.1 15.3 %collective-permute-start.2 = (f32[5,32,256]{2,1,0:T(8,128)}, f32[5,32,256]{2,1,0:T(8,128)S(1)}, u32[]{:S(2)}, u32[]{:S(2)}) collective-permute-start(f32[5,32,256]{2,1,0:T(8,128)} %get-tuple-element.8), channel_id=1, source_target_pairs={{0,1},{16,17},{32,33},{48,49},{64,65},{80,81},{96,97},{112,113},{1... | collective-permute-start | bytes 491528 | tf_op jit(solution)/shard_map/ppermute | solution.py:177
  7.0 12.6 %collective-permute-start = (f32[5,32,256]{2,1,0:T(8,128)}, f32[5,32,256]{2,1,0:T(8,128)S(1)}, u32[]{:S(2)}, u32[]{:S(2)}) collective-permute-start(f32[5,32,256]{2,1,0:T(8,128)} %get-tuple-element.8), channel_id=1, source_target_pairs={{15,255},{31,239},{47,223},{63,207},{79,191},{95,175},{111,159},{1... | collective-permute-start | bytes 491528 | tf_op jit(solution)/shard_map/ppermute | solution.py:177
  7.6 11.7 %collective-permute-start.1 = (f32[5,32,256]{2,1,0:T(8,128)}, f32[5,32,256]{2,1,0:T(8,128)S(1)}, u32[]{:S(2)}, u32[]{:S(2)}) collective-permute-start(f32[5,32,256]{2,1,0:T(8,128)} %get-tuple-element.9), channel_id=1, source_target_pairs={{1,0},{17,16},{33,32},{49,48},{65,64},{81,80},{97,96},{113,112},{1... | collective-permute-start | bytes 491528 | tf_op jit(solution)/shard_map/ppermute | solution.py:177
  18.5 0.7 %copy-start = (f32[5,32,256]{2,1,0:T(8,128)}, f32[5,32,256]{2,1,0:T(8,128)S(1)}, u32[]{:S(2)}) copy-start(f32[5,32,256]{2,1,0:T(8,128)S(1)} %collective-permute-done.2.rs_ref) | copy-start | bytes 491524
  19.3 0.7 %copy-start.5 = (f32[5]{0:T(128)S(1)}, f32[5]{0:T(128)}, u32[]{:S(2)}) copy-start(f32[5]{0:T(128)} %constant.12.clone) | copy-start | bytes 64
  19.6 1.0 %copy-start.3 = (f32[5,32,32]{2,1,0:T(8,128)S(1)}, f32[5,32,32]{2,1,0:T(8,128)}, u32[]{:S(2)}) copy-start(f32[5,32,32]{2,1,0:T(8,128)} %get-tuple-element.11) | copy-start | bytes 61444
  19.6 1.0 %copy-start.4 = (f32[5,32,32]{2,1,0:T(8,128)S(1)}, f32[5,32,32]{2,1,0:T(8,128)}, u32[]{:S(2)}) copy-start(f32[5,32,32]{2,1,0:T(8,128)} %get-tuple-element.10) | copy-start | bytes 61444
  20.7 6.0 %collective-permute-start.4 = (f32[5,40,32]{2,1,0:T(8,128)S(1)}, f32[5,40,32]{2,1,0:T(8,128)S(1)}, u32[]{:S(2)}, u32[]{:S(2)}) collective-permute-start(f32[5,40,32]{2,1,0:T(8,128)S(1)} %get-tuple-element.16), channel_id=1, source_target_pairs={{0,240},{16,0},{32,16},{48,32},{64,48},{80,64},{96,80},{112,96},{1... | collective-permute-start | bytes 76808 | tf_op jit(solution)/shard_map/ppermute | solution.py:177
  24.4 6.2 %collective-permute-start.3 = (f32[5,40,32]{2,1,0:T(8,128)S(1)}, f32[5,40,32]{2,1,0:T(8,128)S(1)}, u32[]{:S(2)}, u32[]{:S(2)}) collective-permute-start(f32[5,40,32]{2,1,0:T(8,128)S(1)} %get-tuple-element.17), channel_id=1, source_target_pairs={{0,16},{16,32},{32,48},{48,64},{64,80},{80,96},{96,112},{112,128},... | collective-permute-start | bytes 76808 | tf_op jit(solution)/shard_map/ppermute | solution.py:177
  26.7 3.9 %copy-start.1 = (f32[5,40,32]{2,1,0:T(8,128)}, f32[5,40,32]{2,1,0:T(8,128)S(1)}, u32[]{:S(2)}) copy-start(f32[5,40,32]{2,1,0:T(8,128)S(1)} %collective-permute-done.4.te_ref) | copy-start | bytes 76804
  30.6 0.6 %copy-start.2 = (f32[5,40,32]{2,1,0:T(8,128)}, f32[5,40,32]{2,1,0:T(8,128)S(1)}, u32[]{:S(2)}) copy-start(f32[5,40,32]{2,1,0:T(8,128)S(1)} %collective-permute-done.3.tw_ref) | copy-start | bytes 76804

commit v17 on v14

--- a/solution.py
+++ b/solution.py
@@ -440,7 +440,7 @@
         return pres, pres_e, pres_n
 
     init = (p_ref[...], pe_ref[...], pn_ref[...])
-    pres, pres_e, pres_n = lax.fori_loop(0, chunk, body, init)
+    pres, pres_e, pres_n = lax.fori_loop(0, chunk, body, init, unroll=2)
     p_ref[...] = pres
     pe_ref[...] = pres_e
     pn_ref[...] = pres_n

time: 49.6 us -> 48.9 us (0.986)
  Pallas kernels: 25.5 us -> 24.8 us
    pallas_call x1, Pallas kernels: 18 us -> 17.2 us  [per_device(): pl.pallas_call(functools.partial(stencil_kernel, total_rows=total_rows),...]
where the time goes in v17:
time: 48.9 us; the launch traced here: 48.6 us
  Pallas kernels  24.8 us (51%)
  starting transfers between devices  14.1 us (29%)
  waiting for transfers between devices  5.32 us (11%)
  local copies, waits for them, and re-layouts  3.07 us (6%)
  between operations  0.74 us (2%)
  matrix products  0.52 us (1%)
    pallas_call x1, Pallas kernels, per_device(): pl.pallas_call(functools.partial(stencil_kernel, total_rows=total_rows),...  17.2 us
    ppermute x5, starting transfers between devices, shift(): return lax.ppermute(value, ('lon', 'lat'), pairs)  14.1 us
    ppermute x5, waiting for transfers between devices, shift(): return lax.ppermute(value, ('lon', 'lat'), pairs)  5.32 us
    pallas_call x1, Pallas kernels, per_device(): pl.pallas_call(edge_kernel, grid=(levels // chunk,), in_specs=[pl.BlockSp...  4.94 us
    pallas_call x1, Pallas kernels, per_device(): pl.pallas_call(row_kernel, grid=(1,), in_specs=[pl.BlockSpec((levels, til...  2.6 us
    unnamed x14, local copies, waits for them, and re-layouts  1.8 us
  transfers between devices with their start and end apart: 5, of which 2 were waited for; matrix products, arithmetic and copies ran while one was open for 3% of the time, Pallas kernels for 10%

profile of v17, /device:TPU:4, one launch (start us, length us, event | category | flops | bytes accessed | tf_op | source)
XLA Modules:
  0.0 48.6 jit_solution(3956679804383617748)
XLA Ops:
  0.6 2.6 %shard_map.102 = (f32[5,32,256]{2,1,0:T(8,128)}, f32[5,32,256]{2,1,0:T(8,128)}) custom-call(f32[32,32,256]{2,1,0:T(8,128)} %ub_ref.1, f32[32,32,256]{2,1,0:T(8,128)} %vb_ref.1, f32[32,32,256]{2,1,0:T(8,128)} %tb_ref.1, f32[32,32,256]{2,1,0:T(8,128)} %sb_ref.1, s32[32,32,256]{2,1,0:T(8,128)} %wb_ref.1, f32[32,32,256]{2,1,0:T(8,128)} %ub_ref.1, ...), custom_call_target="tpu_custom_call" | custom-call | tf_op jit(solution)/shard_map/pallas_call | solution.py:471
  3.2 3.8 %collective-permute-start.2 = (f32[5,32,256]{2,1,0:T(8,128)}, f32[5,32,256]{2,1,0:T(8,128)S(1)}, u32[]{:S(2)}, u32[]{:S(2)}) collective-permute-start(f32[5,32,256]{2,1,0:T(8,128)} %get-tuple-element.8), channel_id=1, source_target_pairs={{0,1},{16,17},{32,33},{48,49},{64,65},{80,81},{96,97},{112,113},{1... | collective-permute-start | bytes 491528 | tf_op jit(solution)/shard_map/ppermute | solution.py:177
  7.1 0.7 %collective-permute-start = (f32[5,32,256]{2,1,0:T(8,128)}, f32[5,32,256]{2,1,0:T(8,128)S(1)}, u32[]{:S(2)}, u32[]{:S(2)}) collective-permute-start(f32[5,32,256]{2,1,0:T(8,128)} %get-tuple-element.8), channel_id=1, source_target_pairs={{15,255},{31,239},{47,223},{63,207},{79,191},{95,175},{111,159},{1... | collective-permute-start | bytes 491528 | tf_op jit(solution)/shard_map/ppermute | solution.py:177
  7.7 5.8 %collective-permute-start.1 = (f32[5,32,256]{2,1,0:T(8,128)}, f32[5,32,256]{2,1,0:T(8,128)S(1)}, u32[]{:S(2)}, u32[]{:S(2)}) collective-permute-start(f32[5,32,256]{2,1,0:T(8,128)} %get-tuple-element.9), channel_id=1, source_target_pairs={{1,0},{17,16},{33,32},{49,48},{65,64},{81,80},{97,96},{113,112},{1... | collective-permute-start | bytes 491528 | tf_op jit(solution)/shard_map/ppermute | solution.py:177
  13.5 4.9 %shard_map.103 = (f32[5,32,32]{2,1,0:T(8,128)}, f32[5,32,32]{2,1,0:T(8,128)}) custom-call(f32[32,32,256]{2,1,0:T(8,128)} %ub_ref.1, f32[32,32,256]{2,1,0:T(8,128)} %vb_ref.1, f32[32,32,256]{2,1,0:T(8,128)} %tb_ref.1, f32[32,32,256]{2,1,0:T(8,128)} %sb_ref.1, s32[32,32,256]{2,1,0:T(8,128)} %wb_ref.1), custom_call_target="tpu_custom_call" | custom-call | tf_op jit(solution)/shard_map/pallas_call | solution.py:485
  18.5 0.1 pad.7.clone
  18.6 0.0 collective-permute-done.2.rs_ref
  18.6 0.0 copy-start
  18.6 0.1 fusion.5
  18.7 0.6 %copy-done = f32[5,32,256]{2,1,0:T(8,128)} copy-done((f32[5,32,256]{2,1,0:T(8,128)}, f32[5,32,256]{2,1,0:T(8,128)S(1)}, u32[]{:S(2)}) %copy-start) | copy-done | bytes 163864
  19.2 0.1 copy.23
  19.3 0.1 copy.22
  19.4 0.0 copy-start.5
  19.4 0.0 collective-permute-done.1
  19.4 0.2 copy.17
  19.7 0.0 copy-start.3
  19.7 0.0 copy-start.4
  19.7 0.0 collective-permute-done
  19.7 0.4 copy-done.5
  20.1 0.5 %fusion = f32[5,32,256]{1,2,0:T(8,128)S(1)} fusion(f32[5,32,256]{1,2,0:T(8,128)S(1)} %copy.17, f32[5,32,256]{2,1,0:T(8,128)S(1)} %collective-permute-done, f32[5]{0:T(128)S(1)} %copy-done.5, pred[]{:T(512)S(6)} %eq.9), kind=kOutput, calls=%fused_computation.1 | convolution fusion | flops 126042112 | bytes 491541 | tf_op jit(solution)/shard_map/dot_general | solution.py:517
  20.6 0.0 copy-done.3
  20.6 0.0 copy-done.4
  20.7 0.1 maximum_maximum_fusion.1
  20.7 3.8 %collective-permute-start.4 = (f32[5,40,32]{2,1,0:T(8,128)S(1)}, f32[5,40,32]{2,1,0:T(8,128)S(1)}, u32[]{:S(2)}, u32[]{:S(2)}) collective-permute-start(f32[5,40,32]{2,1,0:T(8,128)S(1)} %get-tuple-element.16), channel_id=1, source_target_pairs={{0,240},{16,0},{32,16},{48,32},{64,48},{80,64},{96,80},{112,96},{1... | collective-permute-start | bytes 76808 | tf_op jit(solution)/shard_map/ppermute | solution.py:177
  24.5 0.0 collective-permute-start.3
  24.5 0.9 %copy.20.rn_ref = f32[5,32,256]{2,1,0:T(8,128)} copy(f32[5,32,256]{1,2,0:T(8,128)S(1)} %fusion) | data formatting | bytes 327680 | tf_op jit(solution)/shard_map/jit(_where)/select_n | solution.py:518
  25.4 1.4 %collective-permute-done.4.te_ref = f32[5,40,32]{2,1,0:T(8,128)S(1)} collective-permute-done((f32[5,40,32]{2,1,0:T(8,128)S(1)}, f32[5,40,32]{2,1,0:T(8,128)S(1)}, u32[]{:S(2)}, u32[]{:S(2)}) %collective-permute-start.4) | collective-permute-done | bytes 25632 | tf_op jit(solution)/shard_map/ppermute | solution.py:177
  26.8 0.0 copy-start.1
  26.8 3.9 %collective-permute-done.3.tw_ref = f32[5,40,32]{2,1,0:T(8,128)S(1)} collective-permute-done((f32[5,40,32]{2,1,0:T(8,128)S(1)}, f32[5,40,32]{2,1,0:T(8,128)S(1)}, u32[]{:S(2)}, u32[]{:S(2)}) %collective-permute-start.3) | collective-permute-done | bytes 25632 | tf_op jit(solution)/shard_map/ppermute | solution.py:177
  30.7 0.0 copy-start.2
  30.7 0.0 copy-done.1
  30.7 0.6 %copy-done.2 = f32[5,40,32]{2,1,0:T(8,128)} copy-done((f32[5,40,32]{2,1,0:T(8,128)}, f32[5,40,32]{2,1,0:T(8,128)S(1)}, u32[]{:S(2)}) %copy-start.2) | copy-done | bytes 25624
  31.4 17.2 %shard_map.104 = (f32[32,32,256]{2,1,0:T(8,128)}, f32[32,32,256]{2,1,0:T(8,128)}, f32[32,32,256]{2,1,0:T(8,128)}, f32[32,32,256]{2,1,0:T(8,128)}) custom-call(s32[1]{0:T(128)} %bitcast.meta_ref, f32[32,32,256]{2,1,0:T(8,128)} %ub_ref.1, f32[32,32,256]{2,1,0:T(8,128)} %vb_ref.1, f32[32,32,256]{2,1,0:T(8,128)} %tb_ref.1, f32[32,32,256]{2,1,0:T(8,128)} %sb_ref.1, ...), custom_call_target="tpu_custom_call" | custom-call | tf_op jit(solution)/shard_map/pallas_call | solution.py:547
  (2 shorter events, 0.0 us)
Async XLA Ops:
  3.2 15.3 %collective-permute-start.2 = (f32[5,32,256]{2,1,0:T(8,128)}, f32[5,32,256]{2,1,0:T(8,128)S(1)}, u32[]{:S(2)}, u32[]{:S(2)}) collective-permute-start(f32[5,32,256]{2,1,0:T(8,128)} %get-tuple-element.8), channel_id=1, source_target_pairs={{0,1},{16,17},{32,33},{48,49},{64,65},{80,81},{96,97},{112,113},{1... | collective-permute-start | bytes 491528 | tf_op jit(solution)/shard_map/ppermute | solution.py:177
  7.1 12.6 %collective-permute-start = (f32[5,32,256]{2,1,0:T(8,128)}, f32[5,32,256]{2,1,0:T(8,128)S(1)}, u32[]{:S(2)}, u32[]{:S(2)}) collective-permute-start(f32[5,32,256]{2,1,0:T(8,128)} %get-tuple-element.8), channel_id=1, source_target_pairs={{15,255},{31,239},{47,223},{63,207},{79,191},{95,175},{111,159},{1... | collective-permute-start | bytes 491528 | tf_op jit(solution)/shard_map/ppermute | solution.py:177
  7.7 11.7 %collective-permute-start.1 = (f32[5,32,256]{2,1,0:T(8,128)}, f32[5,32,256]{2,1,0:T(8,128)S(1)}, u32[]{:S(2)}, u32[]{:S(2)}) collective-permute-start(f32[5,32,256]{2,1,0:T(8,128)} %get-tuple-element.9), channel_id=1, source_target_pairs={{1,0},{17,16},{33,32},{49,48},{65,64},{81,80},{97,96},{113,112},{1... | collective-permute-start | bytes 491528 | tf_op jit(solution)/shard_map/ppermute | solution.py:177
  18.6 0.7 %copy-start = (f32[5,32,256]{2,1,0:T(8,128)}, f32[5,32,256]{2,1,0:T(8,128)S(1)}, u32[]{:S(2)}) copy-start(f32[5,32,256]{2,1,0:T(8,128)S(1)} %collective-permute-done.2.rs_ref) | copy-start | bytes 491524
  19.4 0.7 %copy-start.5 = (f32[5]{0:T(128)S(1)}, f32[5]{0:T(128)}, u32[]{:S(2)}) copy-start(f32[5]{0:T(128)} %constant.12.clone) | copy-start | bytes 64
  19.7 1.0 %copy-start.3 = (f32[5,32,32]{2,1,0:T(8,128)S(1)}, f32[5,32,32]{2,1,0:T(8,128)}, u32[]{:S(2)}) copy-start(f32[5,32,32]{2,1,0:T(8,128)} %get-tuple-element.11) | copy-start | bytes 61444
  19.7 1.0 %copy-start.4 = (f32[5,32,32]{2,1,0:T(8,128)S(1)}, f32[5,32,32]{2,1,0:T(8,128)}, u32[]{:S(2)}) copy-start(f32[5,32,32]{2,1,0:T(8,128)} %get-tuple-element.10) | copy-start | bytes 61444
  20.7 6.0 %collective-permute-start.4 = (f32[5,40,32]{2,1,0:T(8,128)S(1)}, f32[5,40,32]{2,1,0:T(8,128)S(1)}, u32[]{:S(2)}, u32[]{:S(2)}) collective-permute-start(f32[5,40,32]{2,1,0:T(8,128)S(1)} %get-tuple-element.16), channel_id=1, source_target_pairs={{0,240},{16,0},{32,16},{48,32},{64,48},{80,64},{96,80},{112,96},{1... | collective-permute-start | bytes 76808 | tf_op jit(solution)/shard_map/ppermute | solution.py:177
  24.5 6.2 %collective-permute-start.3 = (f32[5,40,32]{2,1,0:T(8,128)S(1)}, f32[5,40,32]{2,1,0:T(8,128)S(1)}, u32[]{:S(2)}, u32[]{:S(2)}) collective-permute-start(f32[5,40,32]{2,1,0:T(8,128)S(1)} %get-tuple-element.17), channel_id=1, source_target_pairs={{0,16},{16,32},{32,48},{48,64},{64,80},{80,96},{96,112},{112,128},... | collective-permute-start | bytes 76808 | tf_op jit(solution)/shard_map/ppermute | solution.py:177
  26.8 3.9 %copy-start.1 = (f32[5,40,32]{2,1,0:T(8,128)}, f32[5,40,32]{2,1,0:T(8,128)S(1)}, u32[]{:S(2)}) copy-start(f32[5,40,32]{2,1,0:T(8,128)S(1)} %collective-permute-done.4.te_ref) | copy-start | bytes 76804
  30.7 0.6 %copy-start.2 = (f32[5,40,32]{2,1,0:T(8,128)}, f32[5,40,32]{2,1,0:T(8,128)S(1)}, u32[]{:S(2)}) copy-start(f32[5,40,32]{2,1,0:T(8,128)S(1)} %collective-permute-done.3.tw_ref) | copy-start | bytes 76804
